TPU v7x, 32 devices: a whole 2x2x4 slice. The times are simulated.
32 devices in a mesh: dp: 8 (over z, y), hid: 4 (over x, core).
Axes of the slice: x: 2, y: 2, z: 4, core: 2. Of those that a mesh axis runs over, the one named last changes fastest.
Arguments:
- tokens: bfloat16 [16384, 1024], P('dp', 'hid'), may hold values from -6 to 6
- query_weight: bfloat16 [1024, 1024], P(None, 'hid'), may hold values from -0.1875 to 0.1875
- query_bias: float32 [1024], P('hid'), may hold values from -4 to 4
- key_weight: bfloat16 [1024, 1024], P(None, 'hid'), may hold values from -0.1875 to 0.1875
- value_weight: bfloat16 [1024, 1024], P(None, 'hid'), may hold values from -0.1875 to 0.1875
- value_bias: float32 [1024], P('hid'), may hold values from -4 to 4
- output_weight: bfloat16 [1024, 1024], P('hid'), may hold values from -0.75 to 0.75
- output_bias: float32 [1024], P('hid'), may hold values from -4 to 4
- attention_gain: float32 [1024], P('hid'), may hold values from 0.5 to 1.5
- attention_shift: float32 [1024], P('hid'), may hold values from -4 to 4
- inner_weight: bfloat16 [1024, 4096], P(None, 'hid'), may hold values from -0.1875 to 0.1875
- inner_bias: float32 [4096], P('hid'), may hold values from -4 to 4
- down_weight: bfloat16 [4096, 1024], P('hid'), may hold values from -0.1875 to 0.1875
- down_bias: float32 [1024], P('hid'), may hold values from -4 to 4
- final_gain: float32 [1024], P('hid'), may hold values from 0.5 to 1.5
- final_shift: float32 [1024], P('hid'), may hold values from -4 to 4
- head_alpha: float32 [16], replicated, may hold values from -1 to 3
- unit_alpha: float32 [4096], replicated, may hold values from -1 to 3
- width_alpha: float32 [1024], replicated, may hold values from -1 to 3
- multipliers: float32 [2], replicated, may hold values from -1 to 1
- head_noise: float32 [16], P('hid'), may hold values from 0.02 to 0.98
- unit_noise: float32 [4096], P('hid'), may hold values from 0.02 to 0.98
- width_noise: float32 [1024], P('hid'), may hold values from 0.02 to 0.98
- lengths: int32 [32], replicated, may hold values from 64 to 512, as said below
- teacher: bfloat16 [16384, 1024], P('dp', 'hid'), may hold values from -6 to 6
- upstream: bfloat16 [16384, 1024], P('dp', 'hid'), may hold values from -6 to 6
Outputs:
- output: bfloat16 [16384, 1024], P('dp', 'hid')
- tokens_grad: float32 [16384, 1024], P('dp', 'hid')
- query_weight_grad: float32 [1024, 1024], P(None, 'hid')
- query_bias_grad: float32 [1024], P('hid')
- key_weight_grad: float32 [1024, 1024], P(None, 'hid')
- value_weight_grad: float32 [1024, 1024], P(None, 'hid')
- value_bias_grad: float32 [1024], P('hid')
- output_weight_grad: float32 [1024, 1024], P('hid')
- output_bias_grad: float32 [1024], P('hid')
- attention_gain_grad: float32 [1024], P('hid')
- attention_shift_grad: float32 [1024], P('hid')
- inner_weight_grad: float32 [1024, 4096], P(None, 'hid')
- inner_bias_grad: float32 [4096], P('hid')
- down_weight_grad: float32 [4096, 1024], P('hid')
- down_bias_grad: float32 [1024], P('hid')
- final_gain_grad: float32 [1024], P('hid')
- final_shift_grad: float32 [1024], P('hid')
- head_alpha_grad: float32 [16], P('hid')
- unit_alpha_grad: float32 [4096], P('hid')
- width_alpha_grad: float32 [1024], P('hid')
- distill_mse: float32 [], replicated
- multipliers_new: float32 [2], replicated
Inputs may be any that keep to these rules, and one draw needn't show every extreme that they name: `lengths`: each sequence has 64 to 512 live tokens at its start; in every draw some sequence has 512 and some has 64.
All inputs are finite; a program needn't handle non-finite values.
Results may differ from a plain program's by a relative error of at most 0.02.
Values may be sent and summed in bfloat16 or wider, within the bound.
A program may use at most 192 MiB of HBM per device.

v0:
```python
import jax
import jax.numpy as jnp
from jax import lax
from jax.sharding import PartitionSpec as P

D = 1024
HD = 64
FF = 4096
SLOT = 512


BETA = 2.0 / 3.0
GAMMA = -0.1
ZETA = 1.1
TARGET = 0.7
ASCENT = 1.0
EPS = 1e-12
MASKED = -1000000000.0
ROOT_HALF = 0.7071067811865476
ROOT_TWO_PI = 2.5066282746310002


def erf_gelu(values):
    return 0.5 * values * (1.0 + lax.erf(values * ROOT_HALF))


def gelu_slope(values):
    return (
        0.5 * (1.0 + lax.erf(values * ROOT_HALF))
        + values * jnp.exp(-0.5 * values * values) / ROOT_TWO_PI
    )


def gate_value(noise, alpha):
    logits = (jnp.log(noise) - jnp.log(1.0 - noise) + alpha) / BETA
    stretched = jax.nn.sigmoid(logits) * (ZETA - GAMMA) + GAMMA
    return jnp.clip(stretched, 0.0, 1.0)


def keep_prob(alpha):
    return jax.nn.sigmoid(alpha - BETA * jnp.log(-GAMMA / ZETA))


def lagrangian(head_alpha, unit_alpha, width_alpha, multipliers):
    heads_kept = jnp.sum(keep_prob(head_alpha))
    units_kept = jnp.sum(keep_prob(unit_alpha))
    dims_kept = jnp.sum(keep_prob(width_alpha))
    full_size = 4.0 * D * D + 2.0 * D * FF
    expected = (4.0 * HD * heads_kept * dims_kept + 2.0 * units_kept * dims_kept) / full_size
    gap_value = 1.0 - expected - TARGET
    return multipliers[0] * gap_value + multipliers[1] * gap_value * gap_value


def inner_rows(left_side, right_side):
    return lax.dot_general(
        left_side, right_side, (((0,), (0,)), ((), ())), preferred_element_type=jnp.float32
    )


def times_transpose(left_side, right_side):
    return lax.dot_general(
        left_side, right_side, (((1,), (1,)), ((), ())), preferred_element_type=jnp.float32
    )


def gather_features(sharded):
    return lax.all_gather(sharded, "hid", axis=1, tiled=True)


def branch_total(partial_sum):
    return lax.psum_scatter(
        partial_sum.astype(jnp.bfloat16), "hid", scatter_dimension=1, tiled=True
    ).astype(jnp.float32)


def gather_grads(sharded):
    return lax.all_gather(sharded, "hid", axis=1, tiled=True)


def input_total(partial_sum):
    return lax.psum_scatter(
        partial_sum.astype(jnp.bfloat16), "hid", scatter_dimension=1, tiled=True
    ).astype(jnp.float32)


def norm_forward(residual, scale_gain, shift_bias):
    row_total = lax.psum(jnp.sum(residual, axis=1), "hid")
    row_mean = (row_total / D)[:, None]
    centered = residual - row_mean
    variance = (lax.psum(jnp.sum(centered * centered, axis=1), "hid") / D)[:, None]
    row_rstd = lax.rsqrt(variance + EPS)
    normed = (residual - row_mean) * row_rstd
    return (normed, row_rstd, normed * scale_gain + shift_bias)


def norm_backward(d_output, normed, row_rstd, scale_gain):
    d_normed = d_output * scale_gain
    sum_plain, sum_cross = lax.psum(
        (jnp.sum(d_normed, axis=1), jnp.sum(d_normed * normed, axis=1)), "hid"
    )
    return row_rstd * (d_normed - (sum_plain / D)[:, None] - normed * (sum_cross / D)[:, None])


def on_device(
    tokens,
    query_weight,
    query_bias,
    key_weight,
    value_weight,
    value_bias,
    output_weight,
    output_bias,
    attention_gain,
    attention_shift,
    inner_weight,
    inner_bias,
    down_weight,
    down_bias,
    final_gain,
    final_shift,
    head_alpha,
    unit_alpha,
    width_alpha,
    multipliers,
    head_noise,
    unit_noise,
    width_noise,
    lengths,
    teacher,
    upstream,
):
    row_count, local_width = tokens.shape
    heads_here = local_width // HD
    units_here = inner_weight.shape[1]
    seq_local = row_count // SLOT
    hid_rank = lax.axis_index("hid")
    data_rank = lax.axis_index("dp")
    scale_factor = HD ** (-0.5)
    local_lengths = lax.dynamic_slice_in_dim(lengths, data_rank * seq_local, seq_local)
    key_valid = jnp.arange(SLOT)[None, :] < local_lengths[:, None]
    live_rows = key_valid.reshape(row_count, 1).astype(jnp.float32)
    head_local = lax.dynamic_slice_in_dim(head_alpha, hid_rank * heads_here, heads_here)
    unit_local = lax.dynamic_slice_in_dim(unit_alpha, hid_rank * units_here, units_here)
    width_local = lax.dynamic_slice_in_dim(width_alpha, hid_rank * local_width, local_width)
    head_gate, head_pull = jax.vjp(
        lambda alpha_part: gate_value(head_noise, alpha_part), head_local
    )
    unit_gate, unit_pull = jax.vjp(
        lambda alpha_part: gate_value(unit_noise, alpha_part), unit_local
    )
    width_gate, width_pull = jax.vjp(
        lambda alpha_part: gate_value(width_noise, alpha_part), width_local
    )
    full_tokens = gather_features(tokens)
    shaped = (seq_local, SLOT, heads_here, HD)
    queries = (
        (jnp.dot(full_tokens, query_weight, preferred_element_type=jnp.float32) + query_bias)
        .astype(jnp.bfloat16)
        .reshape(shaped)
    )
    keys_all = (
        jnp.dot(full_tokens, key_weight, preferred_element_type=jnp.float32)
        .astype(jnp.bfloat16)
        .reshape(shaped)
    )
    values = (
        (jnp.dot(full_tokens, value_weight, preferred_element_type=jnp.float32) + value_bias)
        .astype(jnp.bfloat16)
        .reshape(shaped)
    )
    valid_keys = key_valid[:, None, None, :]

    def masked_scores():
        raw_scores = jnp.einsum(
            "sqhd,skhd->shqk", queries, keys_all, preferred_element_type=jnp.float32
        )
        return jnp.where(valid_keys, raw_scores * scale_factor, MASKED)

    scores = masked_scores()
    highest = jnp.max(scores, axis=-1, keepdims=True)
    exponent = jnp.exp(scores - highest)
    totals = jnp.sum(exponent, axis=-1, keepdims=True)
    log_total = highest + jnp.log(totals)
    context = jnp.einsum(
        "shqk,skhd->sqhd",
        (exponent / totals).astype(jnp.bfloat16),
        values,
        preferred_element_type=jnp.float32,
    ).reshape(row_count, heads_here, HD)
    gated_low = (
        (context * head_gate[None, :, None]).reshape(row_count, local_width).astype(jnp.bfloat16)
    )
    attention_pre = (
        branch_total(jnp.dot(gated_low, output_weight, preferred_element_type=jnp.float32))
        + output_bias
    )
    tokens_float = tokens.astype(jnp.float32)
    normed_one, rstd_one, middle = norm_forward(
        tokens_float + attention_pre * width_gate, attention_gain, attention_shift
    )
    middle_low = middle.astype(jnp.bfloat16)
    middle_full = gather_features(middle_low)
    pre_act = jnp.dot(middle_full, inner_weight, preferred_element_type=jnp.float32) + inner_bias
    activated = erf_gelu(pre_act)
    inner_act = (activated * unit_gate).astype(jnp.bfloat16)
    ffn_pre = (
        branch_total(jnp.dot(inner_act, down_weight, preferred_element_type=jnp.float32))
        + down_bias
    )
    normed_two, rstd_two, final_out = norm_forward(
        middle + ffn_pre * width_gate, final_gain, final_shift
    )
    differ = final_out - teacher.astype(jnp.float32)
    squared = lax.psum(jnp.sum(live_rows * differ * differ), ("dp", "hid"))
    distill_mse = squared / (jnp.sum(lengths).astype(jnp.float32) * D)
    d_final = live_rows * (upstream.astype(jnp.float32) + differ)
    final_gain_grad = jnp.sum(d_final * normed_two, axis=0)
    final_shift_grad = jnp.sum(d_final, axis=0)
    d_resid_two = norm_backward(d_final, normed_two, rstd_two, final_gain)
    width_grad = jnp.sum(d_resid_two * ffn_pre, axis=0)
    d_ffn_pre = d_resid_two * width_gate
    down_bias_grad = jnp.sum(d_ffn_pre, axis=0)
    d_ffn_full = gather_grads(d_ffn_pre.astype(jnp.bfloat16))
    down_weight_grad = inner_rows(inner_act, d_ffn_full)
    d_inner = times_transpose(d_ffn_full, down_weight)
    unit_grad = jnp.sum(d_inner * activated, axis=0)
    d_pre = (d_inner * unit_gate * gelu_slope(pre_act)).astype(jnp.bfloat16)
    inner_bias_grad = jnp.sum(d_pre.astype(jnp.float32), axis=0)
    inner_weight_grad = inner_rows(middle_full, d_pre)
    unit_alpha_task = unit_pull(unit_grad)[0]
    d_middle = d_resid_two + input_total(times_transpose(d_pre, inner_weight))
    attention_gain_grad = jnp.sum(d_middle * normed_one, axis=0)
    attention_shift_grad = jnp.sum(d_middle, axis=0)
    d_resid_one = norm_backward(d_middle, normed_one, rstd_one, attention_gain)
    width_grad = width_grad + jnp.sum(d_resid_one * attention_pre, axis=0)
    d_attn_pre = d_resid_one * width_gate
    output_bias_grad = jnp.sum(d_attn_pre, axis=0)
    d_attn_full = gather_grads(d_attn_pre.astype(jnp.bfloat16))
    output_weight_grad = inner_rows(gated_low, d_attn_full)
    d_gated = times_transpose(d_attn_full, output_weight).reshape(row_count, heads_here, HD)
    head_grad = jnp.sum(d_gated * context, axis=(0, 2))
    d_context = (d_gated * head_gate[None, :, None]).astype(jnp.bfloat16).reshape(shaped)
    d_probs = jnp.einsum("sqhd,skhd->shqk", d_context, values, preferred_element_type=jnp.float32)
    probabilities = jnp.exp(masked_scores() - log_total)
    d_scores = (
        probabilities * (d_probs - jnp.sum(probabilities * d_probs, axis=-1, keepdims=True))
    ).astype(jnp.bfloat16)
    d_queries = (
        (
            jnp.einsum("shqk,skhd->sqhd", d_scores, keys_all, preferred_element_type=jnp.float32)
            * scale_factor
        )
        .astype(jnp.bfloat16)
        .reshape(row_count, local_width)
    )
    d_keys = (
        (
            jnp.einsum("shqk,sqhd->skhd", d_scores, queries, preferred_element_type=jnp.float32)
            * scale_factor
        )
        .astype(jnp.bfloat16)
        .reshape(row_count, local_width)
    )
    d_values = (
        jnp.einsum(
            "shqk,sqhd->skhd",
            probabilities.astype(jnp.bfloat16),
            d_context,
            preferred_element_type=jnp.float32,
        )
        .astype(jnp.bfloat16)
        .reshape(row_count, local_width)
    )
    query_bias_grad = jnp.sum(d_queries.astype(jnp.float32), axis=0)
    value_bias_grad = jnp.sum(d_values.astype(jnp.float32), axis=0)
    query_weight_grad = inner_rows(full_tokens, d_queries)
    key_weight_grad = inner_rows(full_tokens, d_keys)
    value_weight_grad = inner_rows(full_tokens, d_values)
    d_tokens_part = (
        times_transpose(d_queries, query_weight)
        + times_transpose(d_keys, key_weight)
        + times_transpose(d_values, value_weight)
    )
    tokens_grad = d_resid_one + input_total(d_tokens_part)
    head_alpha_task = head_pull(head_grad)[0]
    width_alpha_task = width_pull(width_grad)[0]
    (
        query_weight_grad,
        query_bias_grad,
        key_weight_grad,
        value_weight_grad,
        value_bias_grad,
        output_weight_grad,
        output_bias_grad,
        attention_gain_grad,
        attention_shift_grad,
        inner_weight_grad,
        inner_bias_grad,
        down_weight_grad,
        down_bias_grad,
        final_gain_grad,
        final_shift_grad,
        head_alpha_task,
        unit_alpha_task,
        width_alpha_task,
    ) = (
        lax.psum(query_weight_grad.astype(jnp.bfloat16), "dp").astype(jnp.float32),
        lax.psum(query_bias_grad.astype(jnp.bfloat16), "dp").astype(jnp.float32),
        lax.psum(key_weight_grad.astype(jnp.bfloat16), "dp").astype(jnp.float32),
        lax.psum(value_weight_grad.astype(jnp.bfloat16), "dp").astype(jnp.float32),
        lax.psum(value_bias_grad.astype(jnp.bfloat16), "dp").astype(jnp.float32),
        lax.psum(output_weight_grad.astype(jnp.bfloat16), "dp").astype(jnp.float32),
        lax.psum(output_bias_grad.astype(jnp.bfloat16), "dp").astype(jnp.float32),
        lax.psum(attention_gain_grad.astype(jnp.bfloat16), "dp").astype(jnp.float32),
        lax.psum(attention_shift_grad.astype(jnp.bfloat16), "dp").astype(jnp.float32),
        lax.psum(inner_weight_grad.astype(jnp.bfloat16), "dp").astype(jnp.float32),
        lax.psum(inner_bias_grad.astype(jnp.bfloat16), "dp").astype(jnp.float32),
        lax.psum(down_weight_grad.astype(jnp.bfloat16), "dp").astype(jnp.float32),
        lax.psum(down_bias_grad.astype(jnp.bfloat16), "dp").astype(jnp.float32),
        lax.psum(final_gain_grad.astype(jnp.bfloat16), "dp").astype(jnp.float32),
        lax.psum(final_shift_grad.astype(jnp.bfloat16), "dp").astype(jnp.float32),
        lax.psum(head_alpha_task.astype(jnp.bfloat16), "dp").astype(jnp.float32),
        lax.psum(unit_alpha_task.astype(jnp.bfloat16), "dp").astype(jnp.float32),
        lax.psum(width_alpha_task.astype(jnp.bfloat16), "dp").astype(jnp.float32),
    )
    lag_grads = jax.grad(lagrangian, argnums=(0, 1, 2, 3))(
        head_alpha, unit_alpha, width_alpha, multipliers
    )
    head_alpha_grad = head_alpha_task + lax.dynamic_slice_in_dim(
        lag_grads[0], hid_rank * heads_here, heads_here
    )
    unit_alpha_grad = unit_alpha_task + lax.dynamic_slice_in_dim(
        lag_grads[1], hid_rank * units_here, units_here
    )
    width_alpha_grad = width_alpha_task + lax.dynamic_slice_in_dim(
        lag_grads[2], hid_rank * local_width, local_width
    )
    multipliers_new = multipliers + ASCENT * lag_grads[3]
    return (
        final_out.astype(jnp.bfloat16),
        tokens_grad,
        query_weight_grad,
        query_bias_grad,
        key_weight_grad,
        value_weight_grad,
        value_bias_grad,
        output_weight_grad,
        output_bias_grad,
        attention_gain_grad,
        attention_shift_grad,
        inner_weight_grad,
        inner_bias_grad,
        down_weight_grad,
        down_bias_grad,
        final_gain_grad,
        final_shift_grad,
        head_alpha_grad,
        unit_alpha_grad,
        width_alpha_grad,
        distill_mse,
        multipliers_new,
    )


def solution(mesh):
    return jax.shard_map(
        on_device,
        mesh=mesh,
        in_specs=(
            P("dp", "hid"),
            P(None, "hid"),
            P("hid"),
            P(None, "hid"),
            P(None, "hid"),
            P("hid"),
            P("hid", None),
            P("hid"),
            P("hid"),
            P("hid"),
            P(None, "hid"),
            P("hid"),
            P("hid", None),
            P("hid"),
            P("hid"),
            P("hid"),
            P(),
            P(),
            P(),
            P(),
            P("hid"),
            P("hid"),
            P("hid"),
            P(),
            P("dp", "hid"),
            P("dp", "hid"),
        ),
        out_specs=(
            P("dp", "hid"),
            P("dp", "hid"),
            P(None, "hid"),
            P("hid"),
            P(None, "hid"),
            P(None, "hid"),
            P("hid"),
            P("hid", None),
            P("hid"),
            P("hid"),
            P("hid"),
            P(None, "hid"),
            P("hid"),
            P("hid", None),
            P("hid"),
            P("hid"),
            P("hid"),
            P("hid"),
            P("hid"),
            P("hid"),
            P(),
            P(),
        ),
        check_vma=False,
    )
```

profile of v0, /device:TPU:0, one launch (start us, length us, event | category | flops | bytes accessed | tf_op | source)
XLA Modules:
  0.0 802.9 jit_solution(3298500553793230705)
XLA Ops:
  10.2 37.1 %all-gather.5.cloned.1.call-done = bf16[2048,1024]{1,0:T(8,128)(2,1)} async-done(((bf16[2048,256]{1,0:T(8,128)(2,1)}), bf16[2048,1024]{1,0:T(8,128)(2,1)}) %all-gather.5.cloned.1.call-update) | async-done | bytes 4194320 | tf_op jit(solution)/shard_map/all_gather | solution.py:67
  78.4 8.6 %fusion.60 = (f32[4,4,512]{2,1,0:T(4,128)S(1)}, f32[4,4,512,512]{2,3,1,0:T(8,128)}) fusion(bf16[4,512,4,64]{1,3,2,0:T(8,128)(2,1)S(1)} %copy.113, bf16[4,512,4,64]{1,3,2,0:T(8,128)(2,1)} %copy.114, pred[4,512]{1,0:T(4,128)(4,1)S(1)} %get-tuple-element.162), kind=kOutput, calls=%fused_computation.150 | convolution fusion | flops 549445632 | bytes 18909184 | tf_op jit(solution)/shard_map/sqhd,skhd->shqk/dot_general | solution.py:174
  87.0 8.3 %fusion = f32[4,4,512]{2,1,0:T(4,128)S(1)} fusion(f32[4,4,512,512]{2,3,1,0:T(8,128)} %get-tuple-element.165, f32[4,4,512]{2,1,0:T(4,128)S(1)} %get-tuple-element.164), kind=kLoop, calls=%fused_computation.6 | loop fusion | flops 8380416 | bytes 16842752 | tf_op jit(solution)/shard_map/reduce_sum | solution.py:182
  95.3 7.6 fusion.17
  111.9 42.6 %reduce-scatter.5.cloned.1.call-done = bf16[2048,256]{1,0:T(8,128)(2,1)} async-done(((bf16[2048,1024]{1,0:T(8,128)(2,1)}), bf16[2048,256]{1,0:T(8,128)(2,1)}) %reduce-scatter.5.cloned.1.call-update) | async-done | bytes 1048592 | tf_op jit(solution)/shard_map/reduce_scatter | solution.py:71
  172.7 35.8 %all-gather.7.cloned.1.call-done = bf16[2048,1024]{1,0:T(8,128)(2,1)} async-done(((bf16[2048,256]{1,0:T(8,128)(2,1)}), bf16[2048,1024]{1,0:T(8,128)(2,1)}) %all-gather.7.cloned.1.call-update) | async-done | bytes 4194320 | tf_op jit(solution)/shard_map/all_gather | solution.py:67
  208.5 9.6 %multiply_convert_fusion.1 = (bf16[2048,1024]{1,0:T(8,128)(2,1)S(1)}, f32[2048,1024]{1,0:T(8,128)}) fusion(f32[1024]{0:T(1024)S(1)} %fusion.37, f32[1024]{0:T(1024)S(1)} %copy-done.38, bf16[2048,1024]{1,0:T(8,128)(2,1)} %all-gather.7.cloned.1.call-done, bf16[1024,1024]{1,0:T(8,128)(2,1)} %param.36), kind=kOutput, calls=%fused_computation.19 | convolution fusion | flops 4309647360 | bytes 18882560 | tf_op jit(solution)/shard_map/dot_general | solution.py:203
  226.2 44.5 %reduce-scatter.7.cloned.1.call-done = bf16[2048,256]{1,0:T(8,128)(2,1)} async-done(((bf16[2048,1024]{1,0:T(8,128)(2,1)}), bf16[2048,256]{1,0:T(8,128)(2,1)}) %reduce-scatter.7.cloned.1.call-update) | async-done | bytes 1048592 | tf_op jit(solution)/shard_map/reduce_scatter | solution.py:71
  287.6 6.7 fusion.54
  294.3 10.6 %all-reduce.3 = (f32[2048]{0:T(1024)S(1)}, f32[2048]{0:T(1024)S(1)}) all-reduce(f32[2048]{0:T(1024)S(1)} %get-tuple-element.114, f32[2048]{0:T(1024)S(1)} %get-tuple-element.115), channel_id=1, replica_groups=mesh['dp'=8,'hid'=4] {'hid'}, use_global_device_ids=true, to_apply=%region_15.16 | all-reduce | flops 4096 | bytes 32768 | tf_op jit(solution)/shard_map/psum | solution.py:98
  310.9 35.9 %all-gather.9.cloned.1.call-done = bf16[2048,1024]{1,0:T(8,128)(2,1)} async-done(((bf16[2048,256]{1,0:T(8,128)(2,1)}), bf16[2048,1024]{1,0:T(8,128)(2,1)}) %all-gather.9.cloned.1.call-update) | async-done | bytes 4194320 | tf_op jit(solution)/shard_map/all_gather | solution.py:77
  346.8 12.4 %fusion.57 = (bf16[1024]{0:T(1024)(128)(2,1)S(1)}, bf16[2048,1024]{1,0:T(8,128)(2,1)S(1)}, f32[2048,1024]{1,0:T(8,128)}) fusion(f32[2048,1024]{1,0:T(8,128)} %get-tuple-element.167, f32[1024]{0:T(1024)S(1)} %copy-done.38, f32[1024]{0:T(1024)S(1)} %fusion.37, bf16[2048,1024]{1,0:T(8,128)(2,1)} %all-gather.9.cloned.1.call-done, ...), kind=kOutput, calls=%fused_computation.148 | convolution fusion | flops 4322229248 | bytes 27273216 | tf_op jit(solution)/shard_map/dot_general | solution.py:61
  367.6 44.5 %reduce-scatter.9.cloned.1.call-done = bf16[2048,256]{1,0:T(8,128)(2,1)} async-done(((bf16[2048,1024]{1,0:T(8,128)(2,1)}), bf16[2048,256]{1,0:T(8,128)(2,1)}) %reduce-scatter.9.cloned.1.call-update) | async-done | bytes 1048592 | tf_op jit(solution)/shard_map/reduce_scatter | solution.py:81
  415.4 10.1 %all-reduce.2 = (f32[2048]{0:T(1024)S(1)}, f32[2048]{0:T(1024)S(1)}) all-reduce(f32[2048]{0:T(1024)S(1)} %get-tuple-element.111, f32[2048]{0:T(1024)S(1)} %get-tuple-element.117), channel_id=1, replica_groups=mesh['dp'=8,'hid'=4] {'hid'}, use_global_device_ids=true, to_apply=%region_20.21 | all-reduce | flops 4096 | bytes 32768 | tf_op jit(solution)/shard_map/psum | solution.py:98
  434.4 9.5 %convolution_convert_fusion.4 = bf16[1024,1024]{1,0:T(8,128)(2,1)} fusion(bf16[2048,1024]{1,0:T(8,128)(2,1)} %copy-done.50, bf16[2048,1024]{1,0:T(8,128)(2,1)} %all-gather.9.cloned.1.call-done), kind=kOutput, calls=%fused_computation.64 | convolution fusion | flops 4296015872 | bytes 10485760 | tf_op jit(solution)/shard_map/dot_general | solution.py:55
  449.8 17.6 %all-gather.11.cloned.1.call-done = bf16[2048,1024]{1,0:T(8,128)(2,1)} async-done(((bf16[2048,256]{1,0:T(8,128)(2,1)}), bf16[2048,1024]{1,0:T(8,128)(2,1)}) %all-gather.11.cloned.1.call-update) | async-done | bytes 4194320 | tf_op jit(solution)/shard_map/all_gather | solution.py:77
  482.7 9.3 %fusion.62 = (bf16[4,64]{1,0:T(4,128)(2,1)S(1)}, bf16[4,512,4,64]{1,3,2,0:T(8,128)(2,1)S(1)}) fusion(f32[4,4,512,512]{2,3,1,0:T(8,128)} %get-tuple-element.165, f32[4,4,512]{2,1,0:T(4,128)S(1)} %bitcast.99, f32[4,512,4,64]{1,3,2,0:T(8,128)} %copy.119, f32[4]{0:T(128)S(1)} %get-tuple-element.155), kind=kOutput, calls=%fused_computation.152 | convolution fusion | flops 547356416 | bytes 19956240 | tf_op jit(solution)/shard_map/shqk,sqhd->skhd/dot_general | solution.py:265
  492.0 11.4 %multiply_reduce_fusion = (f32[4,4,512]{2,1,0:T(4,128)S(1)}, f32[4,4,512,512]{2,3,1,0:T(8,128)}) fusion(f32[4,4,512,512]{2,3,1,0:T(8,128)} %get-tuple-element.165, f32[4,4,512]{2,1,0:T(4,128)S(1)} %bitcast.100, bf16[4,512,4,64]{1,3,2,0:T(8,128)(2,1)S(1)} %copy-done.18, f32[4,512,4,64]{1,3,2,0:T(8,128)S(1)} %copy-done.7, f32[4]{0:T(128)S(1)} %get-tuple-element.155), kind=kOutput, calls=%fused_computation.1 | convolution fusion | flops 550494208 | bytes 36765712 | tf_op jit(solution)/shard_map/sqhd,skhd->shqk/dot_general | solution.py:243
  503.5 12.1 %multiply_convert_fusion = bf16[4,4,512,512]{2,3,1,0:T(8,128)(2,1)S(1)} fusion(f32[4,4,512,512]{2,3,1,0:T(8,128)} %get-tuple-element.170, f32[4,4,512,512]{2,3,1,0:T(8,128)} %get-tuple-element.165, f32[4,4,512]{2,1,0:T(4,128)S(1)} %get-tuple-element.169, f32[4,4,512]{2,1,0:T(4,128)S(1)} %bitcast.101), kind=kLoop, calls=%fused_computation | loop fusion | flops 16777216 | bytes 42008576 | tf_op jit(solution)/shard_map/convert_element_type | solution.py:247
  551.4 42.3 %psum.215 = f32[]{:T(128)} all-reduce(f32[]{:T(128)} %get-tuple-element.116), channel_id=1, replica_groups=mesh['dp'=8,'hid'=4] {'dp','hid'}, use_global_device_ids=true, to_apply=%region_59.60 | all-reduce | flops 1 | bytes 8 | tf_op jit(solution)/shard_map/psum | solution.py:214
  594.3 7.0 multiply_reduce_fusion.1
  601.8 23.1 %all-reduce.4 = (bf16[256]{0:T(256)(128)(2,1)S(1)}, bf16[256]{0:T(256)(128)(2,1)S(1)}, bf16[256]{0:T(256)(128)(2,1)S(1)}, bf16[256]{0:T(256)(128)(2,1)S(1)}, bf1...) all-reduce(bf16[256]{0:T(256)(128)(2,1)S(1)} %reduce_sum.283, ...), channel_id=1, replica_groups=mesh['dp'=8,'hid'=4] {'dp'}, use_global_device_ids=true, to_apply=%region_25.26 | all-reduce | flops 4356 | bytes 17424 | tf_op jit(solution)/shard_map/psum | solution.py:308
  631.9 113.6 %all-reduce.8.cloned.1.call-done = (bf16[1024,256]{0,1:T(8,128)(2,1)}, bf16[1024,256]{0,1:T(8,128)(2,1)}, bf16[1024,256]{0,1:T(8,128)(2,1)}, bf16[256,1024]{1,0:...) async-done(((bf16[1024,256]{0,1:T(8,128)(2,1)}, bf16[1024,256]{0,1:T(8,128)(2,1)}, bf16[1024,256]{0,1:T(8,128)(2,1)}, bf16[256,1024]{1,0:T(8,128)(2,1)}, ...) | async-done | bytes 6291472 | tf_op jit(solution)/shard_map/psum | solution.py:307
  757.7 33.6 %reduce-scatter.11.cloned.1.call-done = bf16[2048,256]{1,0:T(8,128)(2,1)} async-done(((bf16[2048,1024]{1,0:T(8,128)(2,1)}), bf16[2048,256]{1,0:T(8,128)(2,1)}) %reduce-scatter.11.cloned.1.call-update) | async-done | bytes 1048592 | tf_op jit(solution)/shard_map/reduce_scatter | solution.py:81
  (221 shorter events, 185.6 us)
Async XLA Ops:
  7.2 212.9 %copy-start = (bf16[1024,1024]{1,0:T(8,128)(2,1)S(1)}, bf16[1024,1024]{1,0:T(8,128)(2,1)}, u32[]{:S(2)}) copy-start(bf16[1024,1024]{1,0:T(8,128)(2,1)} %param.38) | copy-start | bytes 6291460
  7.2 40.1 %all-gather.5.cloned.1.call-start = ((), (), s32[]{:S(2)}) async-start(), calls=%async_computation.4 | async-start | bytes 5242880 | tf_op jit(solution)/shard_map/all_gather | solution.py:67
  7.9 146.6 %reduce-scatter.5.cloned.1.call-start = ((), (), s32[]{:S(2)}) async-start(), calls=%async_computation.5 | async-start | bytes 5242880 | tf_op jit(solution)/shard_map/reduce_scatter | solution.py:71
  65.1 13.4 %copy-start.9 = (bf16[4,512,4,64]{1,3,2,0:T(8,128)(2,1)}, bf16[4,512,4,64]{1,3,2,0:T(8,128)(2,1)S(1)}, u32[]{:S(2)}) copy-start(bf16[4,512,4,64]{1,3,2,0:T(8,128)(2,1)S(1)} %copy.113) | copy-start | bytes 3145732
  109.9 44.6 %copy-start.2 = (bf16[2048,256]{1,0:T(8,128)(2,1)S(1)}, bf16[2048,256]{1,0:T(8,128)(2,1)}, u32[]{:S(2)}) copy-start(bf16[2048,256]{1,0:T(8,128)(2,1)} %param.26) | copy-start | bytes 3145732
  109.9 44.6 %copy-start.28 = (f32[256]{0:T(256)S(1)}, f32[256]{0:T(256)}, u32[]{:S(2)}) copy-start(f32[256]{0:T(256)} %param.33) | copy-start | bytes 3076
  109.9 98.6 %all-gather.7.cloned.1.call-start = ((), (), s32[]{:S(2)}) async-start(), calls=%async_computation.6 | async-start | bytes 5242880 | tf_op jit(solution)/shard_map/all_gather | solution.py:67
  154.5 15.4 %copy-start.30 = (f32[256]{0:T(256)S(1)}, f32[256]{0:T(256)}, u32[]{:S(2)}) copy-start(f32[256]{0:T(256)} %param.34) | copy-start | bytes 3076
  154.5 15.4 %copy-start.34 = (f32[256]{0:T(256)S(1)}, f32[256]{0:T(256)}, u32[]{:S(2)}) copy-start(f32[256]{0:T(256)} %param.35) | copy-start | bytes 3076
  170.0 38.5 %copy-start.38 = (f32[1024]{0:T(1024)S(1)}, f32[1024]{0:T(1024)}, u32[]{:S(2)}) copy-start(f32[1024]{0:T(1024)} %param.37) | copy-start | bytes 12292
  172.6 98.1 %reduce-scatter.7.cloned.1.call-start = ((), (), s32[]{:S(2)}) async-start(), calls=%async_computation.7 | async-start | bytes 5242880 | tf_op jit(solution)/shard_map/reduce_scatter | solution.py:71
  226.2 44.6 %copy-start.35 = (f32[256]{0:T(256)S(1)}, f32[256]{0:T(256)}, u32[]{:S(2)}) copy-start(f32[256]{0:T(256)} %param.39) | copy-start | bytes 3076
  226.2 120.6 %all-gather.9.cloned.1.call-start = ((), (), s32[]{:S(2)}) async-start(), calls=%async_computation.8 | async-start | bytes 5242880 | tf_op jit(solution)/shard_map/all_gather | solution.py:77
  273.2 14.4 %copy-start.39 = (f32[256]{0:T(256)S(1)}, f32[256]{0:T(256)}, u32[]{:S(2)}) copy-start(f32[256]{0:T(256)} %param.41) | copy-start | bytes 3076
  273.2 14.4 %copy-start.40 = (f32[256]{0:T(256)S(1)}, f32[256]{0:T(256)}, u32[]{:S(2)}) copy-start(f32[256]{0:T(256)} %param.40) | copy-start | bytes 3076
  310.8 101.2 %reduce-scatter.9.cloned.1.call-start = ((), (), s32[]{:S(2)}) async-start(), calls=%async_computation.9 | async-start | bytes 5242880 | tf_op jit(solution)/shard_map/reduce_scatter | solution.py:81
  346.8 14.4 %copy-start.46 = (bf16[1024,1024]{1,0:T(8,128)(2,1)S(1)}, bf16[1024,1024]{1,0:T(8,128)(2,1)}, u32[]{:S(2)}) copy-start(bf16[1024,1024]{1,0:T(8,128)(2,1)} %param.36) | copy-start | bytes 6291460
  367.5 44.6 %copy-start.3 = (bf16[2048,256]{1,0:T(8,128)(2,1)S(1)}, bf16[2048,256]{1,0:T(8,128)(2,1)}, u32[]{:S(2)}) copy-start(bf16[2048,256]{1,0:T(8,128)(2,1)} %reduce-scatter.5.cloned.1.call-done) | copy-start | bytes 3145732
  367.5 44.6 %copy-start.8 = (bf16[2048,256]{1,0:T(8,128)(2,1)S(1)}, bf16[2048,256]{1,0:T(8,128)(2,1)}, u32[]{:S(2)}) copy-start(bf16[2048,256]{1,0:T(8,128)(2,1)} %reduce-scatter.7.cloned.1.call-done) | copy-start | bytes 3145732
  367.5 99.9 %all-gather.11.cloned.1.call-start = ((), (), s32[]{:S(2)}) async-start(), calls=%async_computation.10 | async-start | bytes 5242880 | tf_op jit(solution)/shard_map/all_gather | solution.py:77
  431.7 313.8 %all-reduce.8.cloned.1.call-start = ((), (), s32[]{:S(2)}) async-start(), calls=%async_computation.12 | async-start | bytes 12582912 | tf_op jit(solution)/shard_map/psum | solution.py:307
  444.0 23.4 %copy-start.22 = (bf16[256,1024]{1,0:T(8,128)(2,1)S(1)}, bf16[256,1024]{1,0:T(8,128)(2,1)}, u32[]{:S(2)}) copy-start(bf16[256,1024]{1,0:T(8,128)(2,1)} %param.32) | copy-start | bytes 1572868
  533.1 258.3 %reduce-scatter.11.cloned.1.call-start = ((), (), s32[]{:S(2)}) async-start(), calls=%async_computation.11 | async-start | bytes 5242880 | tf_op jit(solution)/shard_map/reduce_scatter | solution.py:81
  755.2 39.5 %copy-start.1 = (bf16[1024,1024]{1,0:T(8,128)(2,1)S(1)}, bf16[1024,1024]{1,0:T(8,128)(2,1)}, u32[]{:S(2)}) copy-start(bf16[1024,1024]{1,0:T(8,128)(2,1)} %param.38) | copy-start | bytes 6291460
  (38 other events, 160.4 us)
Sparse Core Ops, SparseCore 0:
  9.6 37.7 all-gather.4
  110.0 44.4 reduce-scatter.4
  172.7 35.7 all-gather.6
  226.3 44.3 reduce-scatter.6
  311.0 35.7 all-gather.8
  367.6 44.3 reduce-scatter.8
  431.8 35.5 all-gather.10
  533.2 212.1 all-reduce.7
  748.0 43.3 reduce-scatter.10
where the time goes:
time: 813 us; the launch traced here: 803 us
  waiting for transfers between devices  406 us (50%)
  matrix products  126 us (15%)
  blocking collectives  109 us (13%)
  other arithmetic  82.2 us (10%)
  local copies, waits for them, and re-layouts  55.4 us (7%)
  between operations  23.3 us (3%)
    psum x1, waiting for transfers between devices, on_device(): lax.psum(query_weight_grad.astype(jnp.bfloat16), 'dp').astype(jnp.float32)  114 us
    reduce_scatter x2, waiting for transfers between devices, branch_total(): lax.psum_scatter(partial_sum.astype(jnp.bfloat16), 'hid', scatter_dimensi...  87.1 us
    reduce_scatter x2, waiting for transfers between devices, input_total(): lax.psum_scatter(partial_sum.astype(jnp.bfloat16), 'hid', scatter_dimensi...  78.2 us
    all_gather x2, waiting for transfers between devices, gather_features(): return lax.all_gather(sharded, 'hid', axis=1, tiled=True)  72.9 us
    all_gather x2, waiting for transfers between devices, gather_grads(): return lax.all_gather(sharded, 'hid', axis=1, tiled=True)  53.5 us
    psum x1, blocking collectives, on_device(): squared = lax.psum(jnp.sum(live_rows * differ * differ), ('dp', 'hid'))  42.3 us
    dot_general x6, matrix products, times_transpose(): lax.dot_general(left_side, right_side, (((1,), (1,)), ((), ())), preferre...  30.1 us
    dot_general x6, matrix products, inner_rows(): lax.dot_general(left_side, right_side, (((0,), (0,)), ((), ())), preferre...  23.6 us
  transfers between devices with their start and end apart: 9, of which 9 were waited for; matrix products, arithmetic and copies ran while one was open for 7% of the time, Pallas kernels for 0%

commit v1 on v0

v1 whole, which is shorter than its diff:
```python
import functools

import jax
import jax.numpy as jnp
from jax import lax
from jax.experimental import pallas as pl
from jax.experimental.pallas import tpu as pltpu
from jax.sharding import PartitionSpec as P

D = 1024
HD = 64
FF = 4096
SLOT = 512

BETA = 2.0 / 3.0
GAMMA = -0.1
ZETA = 1.1
TARGET = 0.7
ASCENT = 1.0
EPS = 1e-12
MASKED = -1000000000.0
ROOT_HALF = 0.7071067811865476
ROOT_TWO_PI = 2.5066282746310002

MESH = pl.DeviceIdType.MESH
VMEM_LIMIT = 66_000_000
BF = jnp.bfloat16
F32 = jnp.float32
NB = 256
RB = 16


def gate_value(noise, alpha):
    logits = (jnp.log(noise) - jnp.log(1.0 - noise) + alpha) / BETA
    stretched = jax.nn.sigmoid(logits) * (ZETA - GAMMA) + GAMMA
    return jnp.clip(stretched, 0.0, 1.0)


def keep_prob(alpha):
    return jax.nn.sigmoid(alpha - BETA * jnp.log(-GAMMA / ZETA))


def lagrangian(head_alpha, unit_alpha, width_alpha, multipliers):
    heads_kept = jnp.sum(keep_prob(head_alpha))
    units_kept = jnp.sum(keep_prob(unit_alpha))
    dims_kept = jnp.sum(keep_prob(width_alpha))
    full_size = 4.0 * D * D + 2.0 * D * FF
    expected = (4.0 * HD * heads_kept * dims_kept + 2.0 * units_kept * dims_kept) / full_size
    gap_value = 1.0 - expected - TARGET
    return multipliers[0] * gap_value + multipliers[1] * gap_value * gap_value


def nn(a, b):
    return jnp.dot(a, b, preferred_element_type=F32)


def nt(a, b):
    return lax.dot_general(a, b, (((1,), (1,)), ((), ())), preferred_element_type=F32)


def tn(a, b):
    return lax.dot_general(a, b, (((0,), (0,)), ((), ())), preferred_element_type=F32)


def fold(values):
    return jnp.sum(values.reshape(values.shape[0] // 8, 8, values.shape[1]), axis=0)


class Group:
    def __init__(self, n):
        self.n = n
        self.nx = n // 2
        self.me = lax.axis_index("hid")
        self.x = lax.div(self.me, 2)
        self.c = lax.rem(self.me, 2)
        self.partner = 2 * self.x + 1 - self.c

    def chip_ahead(self, j):
        return lax.rem(self.x + 1 + j, self.nx)

    def chip_behind(self, j):
        return lax.rem(self.x - 1 - j + self.nx, self.nx)

    def slot(self, h):
        return lax.rem(h, 2) * self.nx + lax.div(h, 2)

    def all_peers(self):
        return [{"hid": lax.rem(self.me + 1 + i, self.n)} for i in range(self.n - 1)]

    def near_peers(self):
        near = [self.partner] + [2 * self.chip_ahead(j) + self.c for j in range(self.nx - 1)]
        return [{"hid": peer} for peer in near]


def remote(src, dst, send_sem, recv_sem, to):
    return pltpu.make_async_remote_copy(
        src_ref=src,
        dst_ref=dst,
        send_sem=send_sem,
        recv_sem=recv_sem,
        device_id=to if isinstance(to, dict) else {"hid": to},
        device_id_type=MESH,
    )


def gather_sems(seqs, nx):
    wide = pltpu.SemaphoreType.DMA((seqs, nx - 1))
    return [wide] * 4 + [pltpu.SemaphoreType.DMA((seqs,))] * 3


def reduce_sems(seqs, nx):
    wide = pltpu.SemaphoreType.DMA((seqs, nx - 1))
    return [wide] * 2 + [pltpu.SemaphoreType.DMA((seqs,))] * 2


class Gather:
    def __init__(self, group, sems, source, region):
        self.g, self.source, self.region = group, source, region
        self.xs, self.xr, self.rs, self.rr, self.ps, self.pr, self.os = sems

    def _own(self, s):
        return pltpu.make_async_copy(self.source(s), self.region(s, self.g.me), self.os.at[s])

    def _cross(self, s, j):
        to = 2 * self.g.chip_ahead(j) + self.g.c
        return remote(
            self.source(s), self.region(s, self.g.me), self.xs.at[s, j], self.xr.at[s, j], to
        )

    def _crossed(self, s, j):
        to = 2 * self.g.chip_ahead(j) + self.g.c
        block = self.region(s, 2 * self.g.chip_behind(j) + self.g.c)
        return remote(self.source(s), block, self.xs.at[s, j], self.xr.at[s, j], to)

    def _pair(self, s):
        return remote(
            self.source(s),
            self.region(s, self.g.me),
            self.ps.at[s],
            self.pr.at[s],
            self.g.partner,
        )

    def _paired(self, s):
        block = self.region(s, self.g.partner)
        return remote(self.source(s), block, self.ps.at[s], self.pr.at[s], self.g.partner)

    def _relay(self, s, j):
        block = self.region(s, 2 * self.g.chip_behind(j) + self.g.c)
        return remote(block, block, self.rs.at[s, j], self.rr.at[s, j], self.g.partner)

    def _relayed(self, s, j):
        block = self.region(s, 2 * self.g.chip_behind(j) + 1 - self.g.c)
        return remote(block, block, self.rs.at[s, j], self.rr.at[s, j], self.g.partner)

    def start(self, s):
        for j in range(self.g.nx - 1):
            self._cross(s, j).start()
        self._pair(s).start()
        self._own(s).start()

    def relay(self, s):
        for j in range(self.g.nx - 1):
            self._crossed(s, j).wait_recv()
            self._relay(s, j).start()

    def wait(self, s):
        self._own(s).wait()
        self._paired(s).wait_recv()
        for j in range(self.g.nx - 1):
            self._relayed(s, j).wait_recv()

    def drain(self, s):
        self._pair(s).wait_send()
        for j in range(self.g.nx - 1):
            self._cross(s, j).wait_send()
            self._relay(s, j).wait_send()


class Reduce:
    def __init__(self, group, sems, psend, precv, own, xsend, xrecv):
        self.g = group
        self.psend, self.precv, self.own, self.xsend, self.xrecv = psend, precv, own, xsend, xrecv
        self.xs, self.xr, self.ps, self.pr = sems

    def _pair(self, s):
        return remote(
            self.psend.at[s], self.precv.at[s], self.ps.at[s], self.pr.at[s], self.g.partner
        )

    def _cross(self, s, j):
        to = 2 * self.g.chip_ahead(j) + self.g.c
        return remote(
            self.xsend.at[s, j], self.xrecv.at[s, j], self.xs.at[s, j], self.xr.at[s, j], to
        )

    def start(self, s):
        self._pair(s).start()

    def cross(self, s):
        self._pair(s).wait()
        rows = self.own.shape[2]
        for j in range(self.g.nx - 1):
            chip = self.g.chip_ahead(j)

            def add(i, carry, chip=chip, j=j):
                at = pl.ds(pl.multiple_of(i * RB, RB), RB)
                total = self.own[s, chip, at, :] + self.precv[s, chip, at, :].astype(F32)
                self.xsend[s, j, at, :] = total.astype(BF)
                return carry

            lax.fori_loop(0, rows // RB, add, 0)
            self._cross(s, j).start()

    def arrive(self, s):
        for j in range(self.g.nx - 1):
            self._cross(s, j).wait()

    def total(self, s, at):
        total = self.own[s, self.g.x, at, :] + self.precv[s, self.g.x, at, :].astype(F32)
        for j in range(self.g.nx - 1):
            total = total + self.xrecv[s, j, at, :].astype(F32)
        return total


class Cycle:
    def __init__(self, size):
        self.size = size
        self.me = lax.axis_index("dp")
        self.length = size // 2
        line, column = lax.div(self.me, 2), lax.rem(self.me, 2)
        self.place = line + column * (size - 1 - 2 * line)

    def device(self, place):
        column = lax.div(place, self.length)
        line = place + column * (self.size - 1 - 2 * place)
        return 2 * line + column

    def beside(self, way):
        return self.device(lax.rem(self.place + way + self.size, self.size))


def split(shape, size):
    tall = max(16, shape[0] // (2 * size))
    across = 2 * size * tall // shape[0]
    return tall, shape[1] // across, across


def ring_scratch(shape, size):
    tall, broad, _ = split(shape, size)
    step = pltpu.SemaphoreType.DMA((size - 1,))
    return [
        pltpu.VMEM((size - 1, tall, broad), BF),
        pltpu.VMEM((2, tall, broad), F32),
        pltpu.SemaphoreType.DMA((2, 3)),
    ] + [step] * 4 + [pltpu.SemaphoreType.REGULAR]


class Ring:
    def __init__(self, cycle, data, outs, way, scratch):
        self.cycle, self.data, self.outs, self.way = cycle, data, outs, way
        self.size = cycle.size
        self.recv, self.stage, self.stage_sem, self.ss, self.sr, self.gs, self.gr, self.free = scratch
        self.tall, self.broad, self.across = split(data.shape, self.size)
        self.to, self.frm = {"dp": cycle.beside(way)}, {"dp": cycle.beside(-way)}
        self.ticks = 2 * self.size - 1

    def block(self, number):
        place = lax.rem(self.cycle.place + self.way * number + 2 * self.size, self.size)
        index = 2 * place + (0 if self.way > 0 else 1)
        if self.across == 1:
            return pl.multiple_of(index * self.tall, self.tall), 0
        row = lax.div(index, self.across)
        column = lax.rem(index, self.across)
        return (
            pl.multiple_of(row * self.tall, self.tall),
            pl.multiple_of(column * self.broad, self.broad),
        )

    def view(self, number):
        row, column = self.block(number)
        return self.data.at[pl.ds(row, self.tall), pl.ds(column, self.broad)]

    def _add(self, t):
        return remote(self.view(-t), self.recv.at[t], self.ss.at[t], self.sr.at[t], self.to)

    def _pass(self, t):
        block = self.view(1 - t)
        return remote(block, block, self.gs.at[t], self.gr.at[t], self.to)

    def _passed(self, t):
        block = self.view(-t)
        return remote(block, block, self.gs.at[t], self.gr.at[t], self.to)

    def _sum(self, t):
        row, column = self.block(-t)

        def part(i, carry):
            at = pl.ds(pl.multiple_of(row + i * RB, RB), RB)
            cols = pl.ds(column, self.broad)
            arrived = self.recv[t - 1, pl.ds(pl.multiple_of(i * RB, RB), RB), :].astype(F32)
            self.data[at, cols] = (self.data[at, cols].astype(F32) + arrived).astype(BF)
            return carry

        lax.fori_loop(0, self.tall // RB, part, 0)

    def _puts(self, number, slot):
        row, column = self.block(number)
        puts = []
        for k, (target, first, count) in enumerate(self.outs):
            if self.across == 1:
                source = self.stage.at[slot, :, pl.ds(first, count)]
                place = target.at[pl.ds(row, self.tall), :]
            else:
                source = self.stage.at[slot]
                place = target.at[pl.ds(row, self.tall), pl.ds(column, self.broad)]
            puts.append(pltpu.make_async_copy(source, place, self.stage_sem.at[slot, k]))
        return puts

    def _put(self, number, count):
        slot = lax.rem(count, 2)

        @pl.when(count >= 2)
        def _():
            for put in self._puts(number, slot):
                put.wait()

        row, column = self.block(number)

        def part(i, carry):
            at = pl.ds(pl.multiple_of(row + i * RB, RB), RB)
            value = self.data[at, pl.ds(column, self.broad)].astype(F32)
            self.stage[slot, pl.ds(pl.multiple_of(i * RB, RB), RB), :] = value
            return carry

        lax.fori_loop(0, self.tall // RB, part, 0)
        for put in self._puts(number, slot):
            put.start()

    def tick(self, t):
        size = self.size

        @pl.when(t == 0)
        def _():
            self._add(0).start()

        @pl.when((t >= 1) & (t <= size - 1))
        def _():
            self._add(t - 1).wait_recv()
            self._sum(t)

        @pl.when((t >= 1) & (t < size - 1))
        def _():
            self._add(t).start()

        @pl.when((t >= 1) & (t <= size - 1))
        def _():
            self._add(t - 1).wait_send()
            pl.semaphore_signal(self.free, inc=1, device_id=self.frm, device_id_type=MESH)

        @pl.when(t == size - 1)
        def _():
            pl.semaphore_wait(self.free, 1)
            self._pass(0).start()
            self._put(1, 0)

        @pl.when((t > size - 1) & (t < 2 * size - 1))
        def _():
            u = t - size
            self._passed(u).wait_recv()

            @pl.when(t < 2 * size - 2)
            def _():
                pl.semaphore_wait(self.free, 1)
                self._pass(u + 1).start()

            self._put(-u, u + 1)

    def drain(self):
        for slot in range(2):
            for put in self._puts(0, slot):
                put.wait()

        def step(t, carry):
            self._pass(t).wait_send()
            return carry

        lax.fori_loop(0, self.size - 1, step, 0)


def meet(peers):
    barrier = pltpu.get_barrier_semaphore()
    for peer in peers:
        pl.semaphore_signal(barrier, inc=1, device_id=peer, device_id_type=MESH)
    pl.semaphore_wait(barrier, len(peers))


def mean_of(values):
    return jnp.sum(values, axis=1, keepdims=True) * (1.0 / D)


def attend_kernel(n, seqs, heads, *refs):
    (
        len_ref, tok_ref, change_ref, par_ref, wq_ref, wk_ref, wv_ref, qb_ref, vb_ref, wo_ref, gate_ref,
        full_o, qkv_o, prob_o, ctx_o, gat_o, nrm_o, pre_o, rstd_o, mid_o, par_o, change_o,
        full, wqkv, wo, qkv, prob, ctx, gat, own, psend, precv, xsend, xrecv,
        nrm, pre, rstd, mid, par, score, in_sem, out_sem, vec_send, vec_recv, ch_send, ch_recv, *sems,
    ) = refs
    g = Group(n)
    width = heads * HD
    rows = SLOT // n
    gsems, rsems = sems[:7], sems[7:]
    cols = lambda h: pl.ds(pl.multiple_of(h * width, width), width)
    seq = lambda s: pl.ds(pl.multiple_of(s * SLOT, SLOT), SLOT)
    own_rows = lambda s: pl.ds(pl.multiple_of(s * rows, rows), rows)
    ga = Gather(g, gsems, lambda s: tok_ref.at[seq(s), :], lambda s, h: full.at[seq(s), cols(h)])
    re = Reduce(g, rsems, psend, precv, own, xsend, xrecv)

    def vec_to(i):
        to = lax.rem(g.me + 1 + i, n)
        return remote(par_ref, par.at[:, cols(g.me)], vec_send.at[i], vec_recv.at[i], to)

    def vec_from(i):
        to = lax.rem(g.me + 1 + i, n)
        frm = lax.rem(g.me - 1 - i + n, n)
        return remote(par_ref, par.at[:, cols(frm)], vec_send.at[i], vec_recv.at[i], to)

    def change_to(i):
        to = lax.rem(g.me + 1 + i, n)
        return remote(
            change_ref.at[:, g.slot(to)], change_o.at[:, :, cols(g.me)], ch_send.at[i], ch_recv.at[i], to
        )

    def change_from(i):
        to = lax.rem(g.me + 1 + i, n)
        frm = lax.rem(g.me - 1 - i + n, n)
        return remote(
            change_ref.at[:, g.slot(to)], change_o.at[:, :, cols(frm)], ch_send.at[i], ch_recv.at[i], to
        )

    loads = [
        pltpu.make_async_copy(wq_ref, wqkv.at[:, pl.ds(0, width)], in_sem.at[0]),
        pltpu.make_async_copy(wk_ref, wqkv.at[:, pl.ds(width, width)], in_sem.at[1]),
        pltpu.make_async_copy(wv_ref, wqkv.at[:, pl.ds(2 * width, width)], in_sem.at[2]),
        pltpu.make_async_copy(wo_ref, wo, in_sem.at[3]),
        pltpu.make_async_copy(par_ref, par.at[:, cols(g.me)], in_sem.at[4]),
        pltpu.make_async_copy(
            change_ref.at[:, g.slot(g.me)], change_o.at[:, :, cols(g.me)], in_sem.at[5]
        ),
    ]

    def sequence_outs(s):
        return [
            pltpu.make_async_copy(full.at[seq(s), :], full_o.at[seq(s), :], out_sem.at[s, 0]),
            pltpu.make_async_copy(qkv.at[seq(s), :], qkv_o.at[seq(s), :], out_sem.at[s, 1]),
            pltpu.make_async_copy(prob.at[s], prob_o.at[s], out_sem.at[s, 2]),
            pltpu.make_async_copy(ctx.at[seq(s), :], ctx_o.at[seq(s), :], out_sem.at[s, 3]),
            pltpu.make_async_copy(gat.at[seq(s), :], gat_o.at[seq(s), :], out_sem.at[s, 4]),
        ]

    def row_outs(s):
        return [
            pltpu.make_async_copy(nrm.at[own_rows(s), :], nrm_o.at[own_rows(s), :], out_sem.at[s, 5]),
            pltpu.make_async_copy(pre.at[own_rows(s), :], pre_o.at[own_rows(s), :], out_sem.at[s, 6]),
            pltpu.make_async_copy(rstd.at[own_rows(s), :], rstd_o.at[own_rows(s), :], out_sem.at[s, 7]),
            pltpu.make_async_copy(mid.at[own_rows(s), :], mid_o.at[own_rows(s), :], out_sem.at[s, 8]),
        ]

    meet(g.all_peers())

    def begin(s, carry):
        ga.start(s)
        return carry

    lax.fori_loop(0, seqs, begin, 0)
    for i in range(n - 1):
        vec_to(i).start()
    for load in loads:
        load.start()
    for i in range(n - 1):
        change_to(i).start()
    ga.relay(0)
    for load in loads[:5]:
        load.wait()
    for i in range(n - 1):
        vec_from(i).wait()
    par_o[...] = par[...]

    lanes = lax.broadcasted_iota(jnp.int32, (1, width), 1)
    head_lanes = [
        jnp.where((lanes >= h * HD) & (lanes < (h + 1) * HD), 1.0, 0.0).astype(BF) for h in range(heads)
    ]

    def finish(s):
        re.arrive(s)

        def block(i, carry):
            at = pl.ds(pl.multiple_of(i * RB, RB), RB)
            here = pl.ds(pl.multiple_of(s * rows + i * RB, RB), RB)
            token_row = pl.multiple_of(s * SLOT + g.slot(g.me) * rows + i * RB, RB)
            attention_pre = re.total(s, at) + par[0:1, :]
            residual = full[pl.ds(token_row, RB), :].astype(F32) + attention_pre * par[1:2, :]
            centered = residual - mean_of(residual)
            row_rstd = lax.rsqrt(mean_of(centered * centered) + EPS)
            normed = centered * row_rstd
            middle = normed * par[2:3, :] + par[3:4, :]
            nrm[here, :] = normed
            pre[here, :] = attention_pre
            rstd[here, :] = jnp.broadcast_to(row_rstd, (RB, 128))
            mid[here, :] = middle.astype(BF)
            return carry

        lax.fori_loop(0, rows // RB, block, 0)
        for copy in row_outs(s):
            copy.start()

    def sequence(s, carry):
        ga.wait(s)
        here = seq(s)
        projected = nn(full[here, :], wqkv[...])
        qkv[here, 0:width] = (projected[:, 0:width] + qb_ref[...]).astype(BF)
        qkv[here, width : 2 * width] = projected[:, width : 2 * width].astype(BF)
        qkv[here, 2 * width : 3 * width] = (projected[:, 2 * width : 3 * width] + vb_ref[...]).astype(BF)

        @pl.when(s + 1 < seqs)
        def _():
            ga.relay(s + 1)

        @pl.when(s > 0)
        def _():
            re.cross(s - 1)

        length = len_ref[s]
        for h in range(heads):
            score[...] = nt(qkv[here, 0:width] * head_lanes[h], qkv[here, width : 2 * width])

            def softmax(i, carry, h=h):
                at = pl.ds(pl.multiple_of(i * 64, 64), 64)
                places = lax.broadcasted_iota(jnp.int32, (64, SLOT), 1)
                scores = jnp.where(places < length, score[at, :] * (HD**-0.5), MASKED)
                exponent = jnp.exp(scores - jnp.max(scores, axis=1, keepdims=True))
                total = jnp.sum(exponent, axis=1, keepdims=True)
                prob[s, h, at, :] = (exponent * (1.0 / total)).astype(BF)
                return carry

            lax.fori_loop(0, SLOT // 64, softmax, 0)
            term = nn(prob[s, h], qkv[here, 2 * width : 3 * width] * head_lanes[h])
            ctx[here, :] = term if h == 0 else ctx[here, :] + term
        gat[here, :] = (ctx[here, :] * gate_ref[...]).astype(BF)
        for copy in sequence_outs(s):
            copy.start()
        half = SLOT // 2
        there = pl.ds(pl.multiple_of(s * SLOT + (1 - g.c) * half, half), half)
        psend[s] = nn(gat[there, :], wo[...]).astype(BF).reshape(n // 2, rows, D)
        re.start(s)
        mine = pl.ds(pl.multiple_of(s * SLOT + g.c * half, half), half)
        own[s] = nn(gat[mine, :], wo[...]).reshape(n // 2, rows, D)

        @pl.when(s > 0)
        def _():
            finish(s - 1)

        return carry

    lax.fori_loop(0, seqs, sequence, 0)
    re.cross(seqs - 1)
    finish(seqs - 1)
    loads[5].wait()
    for i in range(n - 1):
        change_from(i).wait()

    def end(s, carry):
        ga.drain(s)
        for copy in sequence_outs(s) + row_outs(s):
            copy.wait()
        return carry

    lax.fori_loop(0, seqs, end, 0)


def feed_kernel(n, seqs, units, *refs):
    (
        len_ref, mid_ref, nrm_ref, pre_ref, rstd_ref, par, change_ref, w1_ref, b1_ref, w2_ref, ugate_ref,
        out_o, dlow_o, dres_o, dw1_o, dw2_o, rowsum_o, unitsum_o,
        midf, dffn, w1, w2, act, inner, slope, own, psend, precv, xsend, xrecv,
        nrm, pre, rstd, change, dtwo, dsend, fout, dlow, dres, wide, grad, sums, unit_sums,
        in_sem, out_sem, grad_sem, *sems,
    ) = refs
    g = Group(n)
    rows = SLOT // n
    half = SLOT // 2
    g1, r1, g2, r2 = sems[:7], sems[7:11], sems[11:18], sems[18:]
    seq = lambda s: pl.ds(pl.multiple_of(s * SLOT, SLOT), SLOT)
    own_rows = lambda s: pl.ds(pl.multiple_of(s * rows, rows), rows)
    spot = lambda s, h: pl.ds(pl.multiple_of(s * SLOT + g.slot(h) * rows, rows), rows)
    gm = Gather(g, g1, lambda s: mid_ref.at[own_rows(s), :], lambda s, h: midf.at[spot(s, h), :])
    gd = Gather(g, g2, lambda s: dsend.at[own_rows(s), :], lambda s, h: dffn.at[spot(s, h), :])
    rf = Reduce(g, r1, psend, precv, own, xsend, xrecv)
    rb = Reduce(g, r2, psend, precv, own, xsend, xrecv)
    loads = [
        pltpu.make_async_copy(w1_ref, w1, in_sem.at[0]),
        pltpu.make_async_copy(w2_ref, w2, in_sem.at[1]),
        pltpu.make_async_copy(nrm_ref, nrm, in_sem.at[2]),
        pltpu.make_async_copy(change_ref, change, in_sem.at[3]),
        pltpu.make_async_copy(pre_ref, pre, in_sem.at[4]),
        pltpu.make_async_copy(rstd_ref, rstd, in_sem.at[5]),
    ]

    meet(g.near_peers())

    def begin(s, carry):
        gm.start(s)
        return carry

    lax.fori_loop(0, seqs, begin, 0)
    for load in loads:
        load.start()
    sums[...] = jnp.zeros_like(sums)
    unit_sums[...] = jnp.zeros_like(unit_sums)
    gm.relay(0)
    for load in loads:
        load.wait()

    def finish_forward(s):
        rf.arrive(s)
        length = len_ref[s]

        def block(i, carry):
            at = pl.ds(pl.multiple_of(i * RB, RB), RB)
            here = pl.ds(pl.multiple_of(s * rows + i * RB, RB), RB)
            ffn_pre = rf.total(s, at) + par[4:5, :]
            middle = nrm[here, :] * par[2:3, :] + par[3:4, :]
            residual = middle + ffn_pre * par[1:2, :]
            centered = residual - mean_of(residual)
            row_rstd = lax.rsqrt(mean_of(centered * centered) + EPS)
            normed = centered * row_rstd
            final = normed * par[5:6, :] + par[6:7, :]
            fout[here, :] = final.astype(BF)
            place = g.slot(g.me) * rows + i * RB + lax.broadcasted_iota(jnp.int32, (RB, 1), 0)
            live = jnp.where(place < length, 1.0, 0.0)
            d_final = live * (change[here, :].astype(F32) + final)
            sums[0] += fold(d_final * normed)
            sums[1] += fold(d_final)
            d_normed = d_final * par[5:6, :]
            d_two = row_rstd * (d_normed - mean_of(d_normed) - normed * mean_of(d_normed * normed))
            sums[2] += fold(d_two * ffn_pre)
            d_ffn = d_two * par[1:2, :]
            sums[3] += fold(d_ffn)
            dtwo[here, :] = d_two
            dsend[here, :] = d_ffn.astype(BF)
            return carry

        lax.fori_loop(0, rows // RB, block, 0)
        gd.start(s)

    def forward(s, carry):
        gm.wait(s)
        here = seq(s)

        def part(b, carry):
            cols = pl.ds(pl.multiple_of(b * NB, NB), NB)
            wide[...] = nn(midf[here, :], w1[:, cols])
            bias = b1_ref[:, cols]
            gate = ugate_ref[:, cols]

            def block(i, carry):
                at = pl.ds(pl.multiple_of(i * 32, 32), 32)
                row = pl.ds(pl.multiple_of(s * SLOT + i * 32, 32), 32)
                v = wide[at, :] + bias
                phi = 0.5 * (1.0 + lax.erf(v * ROOT_HALF))
                activated = v * phi
                act[row, cols] = activated.astype(BF)
                inner[row, cols] = (activated * gate).astype(BF)
                steep = phi + v * jnp.exp(-0.5 * v * v) * (1.0 / ROOT_TWO_PI)
                slope[row, cols] = (gate * steep).astype(BF)
                return carry

            lax.fori_loop(0, SLOT // 32, block, 0)
            return carry

        lax.fori_loop(0, units // NB, part, 0)

        @pl.when(s + 1 < seqs)
        def _():
            gm.relay(s + 1)

        @pl.when(s > 0)
        def _():
            rf.cross(s - 1)

        there = pl.ds(pl.multiple_of(s * SLOT + (1 - g.c) * half, half), half)
        psend[s] = nn(inner[there, :], w2[...]).astype(BF).reshape(n // 2, rows, D)
        rf.start(s)
        mine = pl.ds(pl.multiple_of(s * SLOT + g.c * half, half), half)
        own[s] = nn(inner[mine, :], w2[...]).reshape(n // 2, rows, D)

        @pl.when(s > 0)
        def _():
            finish_forward(s - 1)

        return carry

    lax.fori_loop(0, seqs, forward, 0)
    rf.cross(seqs - 1)
    gd.relay(0)
    finish_forward(seqs - 1)

    def row_outs(s):
        return [
            pltpu.make_async_copy(fout.at[own_rows(s), :], out_o.at[own_rows(s), :], out_sem.at[s, 0]),
            pltpu.make_async_copy(dlow.at[own_rows(s), :], dlow_o.at[own_rows(s), :], out_sem.at[s, 1]),
            pltpu.make_async_copy(dres.at[own_rows(s), :], dres_o.at[own_rows(s), :], out_sem.at[s, 2]),
        ]

    def finish_backward(s):
        rb.arrive(s)

        def block(i, carry):
            at = pl.ds(pl.multiple_of(i * RB, RB), RB)
            here = pl.ds(pl.multiple_of(s * rows + i * RB, RB), RB)
            normed = nrm[here, :]
            d_middle = dtwo[here, :] + rb.total(s, at)
            sums[4] += fold(d_middle * normed)
            sums[5] += fold(d_middle)
            d_normed = d_middle * par[2:3, :]
            d_one = rstd[here, 0:1] * (
                d_normed - mean_of(d_normed) - normed * mean_of(d_normed * normed)
            )
            sums[2] += fold(d_one * pre[here, :])
            d_attn = d_one * par[1:2, :]
            sums[6] += fold(d_attn)
            dres[here, :] = d_one
            dlow[here, :] = d_attn.astype(BF)
            return carry

        lax.fori_loop(0, rows // RB, block, 0)
        for copy in row_outs(s):
            copy.start()

    def backward(s, carry):
        gd.wait(s)
        here = seq(s)

        def part(b, carry):
            cols = pl.ds(pl.multiple_of(b * NB, NB), NB)
            wide[...] = nt(dffn[here, :], w2[cols, :])

            def block(i, sums_here):
                unit_part, bias_part = sums_here
                at = pl.ds(pl.multiple_of(i * 32, 32), 32)
                row = pl.ds(pl.multiple_of(s * SLOT + i * 32, 32), 32)
                d_inner = wide[at, :]
                d_pre = (d_inner * slope[row, cols].astype(F32)).astype(BF)
                unit_part = unit_part + fold(d_inner * act[row, cols].astype(F32))
                bias_part = bias_part + fold(d_pre.astype(F32))
                slope[row, cols] = d_pre
                return (unit_part, bias_part)

            zero = jnp.zeros((8, NB), F32)
            unit_part, bias_part = lax.fori_loop(0, SLOT // 32, block, (zero, zero))
            unit_sums[0, :, cols] += unit_part
            unit_sums[1, :, cols] += bias_part
            return carry

        lax.fori_loop(0, units // NB, part, 0)

        @pl.when(s + 1 < seqs)
        def _():
            gd.relay(s + 1)

        @pl.when(s > 0)
        def _():
            rb.cross(s - 1)

        there = pl.ds(pl.multiple_of(s * SLOT + (1 - g.c) * half, half), half)
        psend[s] = nt(slope[there, :], w1[...]).astype(BF).reshape(n // 2, rows, D)
        rb.start(s)
        mine = pl.ds(pl.multiple_of(s * SLOT + g.c * half, half), half)
        own[s] = nt(slope[mine, :], w1[...]).reshape(n // 2, rows, D)

        @pl.when(s > 0)
        def _():
            finish_backward(s - 1)

        return carry

    lax.fori_loop(0, seqs, backward, 0)
    rb.cross(seqs - 1)

    def grad_out(k, b):
        target = (dw2_o, dw1_o)[k]
        at = pl.ds(pl.multiple_of(b * NB, NB), NB)
        return pltpu.make_async_copy(grad.at[b], target.at[at, :], grad_sem.at[k, b])

    def down_grad(b, carry):
        cols = pl.ds(pl.multiple_of(b * NB, NB), NB)
        grad[b] = tn(inner[:, cols], dffn[...]).astype(BF)
        grad_out(0, b).start()
        return carry

    lax.fori_loop(0, units // NB, down_grad, 0)
    finish_backward(seqs - 1)
    for b in range(units // NB):
        grad_out(0, b).wait()

    def inner_grad(b, carry):
        cols = pl.ds(pl.multiple_of(b * NB, NB), NB)
        grad[b, :, 0:units] = tn(midf[:, cols], slope[...]).astype(BF)
        pltpu.make_async_copy(
            grad.at[b, :, pl.ds(0, units)], dw1_o.at[cols, :], grad_sem.at[1, b]
        ).start()
        return carry

    lax.fori_loop(0, D // NB, inner_grad, 0)
    for k in range(7):
        rowsum_o[k : k + 1, :] = jnp.sum(sums[k], axis=0, keepdims=True)
    rowsum_o[7:8, :] = jnp.zeros((1, D), F32)
    for k in range(2):
        unitsum_o[k : k + 1, :] = jnp.sum(unit_sums[k], axis=0, keepdims=True)
    for b in range(D // NB):
        at = pl.ds(b * NB, NB)
        pltpu.make_async_copy(
            grad.at[b, :, pl.ds(0, units)], dw1_o.at[at, :], grad_sem.at[1, b]
        ).wait()

    def end(s, carry):
        gm.drain(s)
        gd.drain(s)
        for copy in row_outs(s):
            copy.wait()
        return carry

    lax.fori_loop(0, seqs, end, 0)


def attend_back_kernel(n, seqs, heads, size, *refs):
    (
        dlow_ref, dres_ref, full_ref, qkv_ref, prob_ref, ctx_ref, gat_ref,
        wq_ref, wk_ref, wv_ref, wo_ref, dw1_ref, dw2_ref, out_ref, gate_ref,
        tgrad_o, dwqkv_o, dwo_o, dw1_o, dw2_o, output_o, sums_o,
        dattn, dres, full, qkv, prob, ctx, gat, wqkv, wo, dctx, dqkv, dprob, dscore, acc,
        block_f, own, psend, precv, xsend, xrecv, tgrad, grad, gwo, sums, dw1, dw2,
        in_sem, out_sem, grad_sem, move_send, move_recv, *sems,
    ) = refs
    g = Group(n)
    cycle = Cycle(size)
    rings = []
    for k, (data, target) in enumerate(((dw1, dw1_o), (dw2, dw2_o))):
        for way in (1, -1):
            i = 11 + 8 * len(rings)
            outs = [(target, 0, data.shape[1])]
            rings.append(Ring(cycle, data, outs, way, sems[i : i + 8]))
    ticks = rings[0].ticks

    def tick(t):
        for ring in rings:
            ring.tick(t)

    def move_to(i):
        to = lax.rem(g.me + 1 + i, n)
        return remote(
            out_ref.at[:, :, cols_of(to)], output_o.at[:, g.slot(g.me)], move_send.at[i], move_recv.at[i], to
        )

    def move_from(i):
        to = lax.rem(g.me + 1 + i, n)
        frm = lax.rem(g.me - 1 - i + n, n)
        return remote(
            out_ref.at[:, :, cols_of(to)], output_o.at[:, g.slot(frm)], move_send.at[i], move_recv.at[i], to
        )

    width = heads * HD
    rows = SLOT // n
    gsems, rsems = sems[:7], sems[7:11]
    cols_of = lambda h: pl.ds(pl.multiple_of(h * width, width), width)
    seq = lambda s: pl.ds(pl.multiple_of(s * SLOT, SLOT), SLOT)
    own_rows = lambda s: pl.ds(pl.multiple_of(s * rows, rows), rows)
    spot = lambda s, h: pl.ds(pl.multiple_of(s * SLOT + g.slot(h) * rows, rows), rows)
    ga = Gather(g, gsems, lambda s: dlow_ref.at[own_rows(s), :], lambda s, h: dattn.at[spot(s, h), :])
    re = Reduce(g, rsems, psend, precv, own, xsend, xrecv)
    loads = [
        pltpu.make_async_copy(wo_ref, wo, in_sem.at[0]),
        pltpu.make_async_copy(ctx_ref, ctx, in_sem.at[1]),
        pltpu.make_async_copy(qkv_ref, qkv, in_sem.at[2]),
        pltpu.make_async_copy(prob_ref, prob, in_sem.at[3]),
        pltpu.make_async_copy(wq_ref, wqkv.at[:, pl.ds(0, width)], in_sem.at[4]),
        pltpu.make_async_copy(wk_ref, wqkv.at[:, pl.ds(width, width)], in_sem.at[5]),
        pltpu.make_async_copy(wv_ref, wqkv.at[:, pl.ds(2 * width, width)], in_sem.at[6]),
        pltpu.make_async_copy(dres_ref, dres, in_sem.at[7]),
        pltpu.make_async_copy(full_ref, full, in_sem.at[8]),
        pltpu.make_async_copy(gat_ref, gat, in_sem.at[9]),
        pltpu.make_async_copy(
            out_ref.at[:, :, cols_of(g.me)], output_o.at[:, g.slot(g.me)], in_sem.at[11]
        ),
    ]
    grads_in = [
        pltpu.make_async_copy(dw1_ref, dw1, in_sem.at[12]),
        pltpu.make_async_copy(dw2_ref, dw2, in_sem.at[13]),
    ]
    meet(g.all_peers() + [{"dp": cycle.beside(1)}, {"dp": cycle.beside(-1)}])
    for load in grads_in:
        load.start()

    def begin(s, carry):
        ga.start(s)
        return carry

    lax.fori_loop(0, seqs, begin, 0)
    for load in loads:
        load.start()
    sums[...] = jnp.zeros_like(sums)
    for load in grads_in:
        load.wait()
    tick(0)
    ga.relay(0)
    for load in loads[:8]:
        load.wait()

    lanes = lax.broadcasted_iota(jnp.int32, (1, width), 1)
    head_lanes = [
        jnp.where((lanes >= h * HD) & (lanes < (h + 1) * HD), 1.0, 0.0).astype(BF) for h in range(heads)
    ]

    def out(s):
        return pltpu.make_async_copy(tgrad.at[seq(s), :], tgrad_o.at[seq(s), :], out_sem.at[s])

    def finish(s):
        re.arrive(s)

        def block(i, carry):
            at = pl.ds(pl.multiple_of(i * 32, 32), 32)
            tgrad[pl.ds(pl.multiple_of(s * SLOT + i * 32, 32), 32), :] = re.total(s, at)
            return carry

        lax.fori_loop(0, SLOT // 32, block, 0)
        out(s).start()

    def token_block(s, h):
        cols = pl.ds(pl.multiple_of(h * width, width), width)
        block_f[...] = nt(dqkv[seq(s), :], wqkv[cols, :])
        mine = pl.ds(pl.multiple_of(g.slot(g.me) * rows, rows), rows)
        block_f[mine, :] += dres[own_rows(s), cols]

    def sequence(s, carry):
        ga.wait(s)
        here = seq(s)
        d_gated = nt(dattn[here, :], wo[...])
        sums[0] += fold(d_gated * ctx[here, :])
        dctx[...] = (d_gated * gate_ref[...]).astype(BF)

        @pl.when(s + 1 < seqs)
        def _():
            ga.relay(s + 1)

        @pl.when(s > 0)
        def _():
            re.cross(s - 1)

        for h in range(heads):
            d_context = dctx[...] * head_lanes[h]
            dprob[...] = nt(d_context, qkv[here, 2 * width : 3 * width])

            def softmax(i, carry, h=h):
                at = pl.ds(pl.multiple_of(i * 64, 64), 64)
                p = prob[s, h, at, :].astype(F32)
                weighted = p * dprob[at, :]
                total = jnp.sum(weighted, axis=1, keepdims=True)
                dscore[at, :] = (weighted - p * total).astype(BF)
                return carry

            lax.fori_loop(0, SLOT // 64, softmax, 0)
            terms = (
                nn(dscore[...], qkv[here, width : 2 * width] * head_lanes[h]),
                tn(dscore[...], qkv[here, 0:width] * head_lanes[h]),
                tn(prob[s, h], d_context),
            )
            for k in range(3):
                acc[k] = terms[k] if h == 0 else acc[k] + terms[k]
            tick(s * heads + h + 1)
        scales = (HD**-0.5, HD**-0.5, 1.0)
        for k in range(3):
            rounded = (acc[k] * scales[k]).astype(BF)
            dqkv[here, k * width : (k + 1) * width] = rounded
            sums[1 + k] += fold(rounded.astype(F32))
        for chip in range(n // 2):
            token_block(s, 2 * chip + 1 - g.c)
            psend[s, chip] = block_f[...].astype(BF)
        re.start(s)
        for chip in range(n // 2):
            token_block(s, 2 * chip + g.c)
            own[s, chip] = block_f[...]

        @pl.when(s > 0)
        def _():
            finish(s - 1)

        return carry

    lax.fori_loop(0, seqs, sequence, 0)
    re.cross(seqs - 1)
    for i in range(n - 1):
        move_to(i).start()
    for load in loads[8:]:
        load.wait()

    def grad_out(b):
        at = pl.ds(pl.multiple_of(b * NB, NB), NB)
        return pltpu.make_async_copy(grad.at[b], dwqkv_o.at[at, :], grad_sem.at[b])

    def token_grad(b, carry):
        cols = pl.ds(pl.multiple_of(b * NB, NB), NB)
        grad[b] = tn(full[:, cols], dqkv[...]).astype(BF)
        grad_out(b).start()
        return carry

    lax.fori_loop(0, D // NB, token_grad, 0)
    gwo[...] = tn(gat[...], dattn[...]).astype(BF)
    gwo_out = pltpu.make_async_copy(gwo, dwo_o, in_sem.at[10])
    gwo_out.start()
    finish(seqs - 1)
    for k in range(4):
        sums_o[k : k + 1, :] = jnp.sum(sums[k], axis=0, keepdims=True)
    sums_o[4:8, :] = jnp.zeros((4, width), F32)
    gwo_out.wait()

    def rest(t, carry):
        tick(t)
        return carry

    lax.fori_loop(seqs * heads + 1, ticks, rest, 0)
    for ring in rings:
        ring.drain()
    for i in range(n - 1):
        move_from(i).wait()

    def end_grad(b, carry):
        grad_out(b).wait()
        return carry

    lax.fori_loop(0, D // NB, end_grad, 0)

    def end(s, carry):
        ga.drain(s)
        out(s).wait()
        return carry

    lax.fori_loop(0, seqs, end, 0)


def settle_kernel(n, size, seqs, *refs):
    (
        len_ref, dwqkv_ref, dwo_ref, output_ref, teacher_ref, row_ref, unit_ref, head_ref,
        dwq_o, dwk_o, dwv_o, dwo_o, small_o, units_o,
        dwqkv, dwo, output, teacher, parts, small, rbuf, sbuf, ubuf,
        in_sem, r_send, r_recv, s_send, s_recv, u_send, u_recv, *sems,
    ) = refs
    g = Group(n)
    cycle = Cycle(size)
    width = head_ref.shape[1]
    cols = lambda h: pl.ds(pl.multiple_of(h * width, width), width)
    outs = [(dwq_o, 0, width), (dwk_o, width, width), (dwv_o, 2 * width, width)]
    rings = []
    for data, targets in ((dwqkv, outs), (dwo, [(dwo_o, 0, D)])):
        for way in (1, -1):
            i = 8 * len(rings)
            rings.append(Ring(cycle, data, targets, way, sems[i : i + 8]))

    def tick(t):
        for ring in rings:
            ring.tick(t)

    def row_to(i):
        to = lax.rem(g.me + 1 + i, n)
        return remote(parts.at[:, cols(to)], rbuf.at[i], r_send.at[i], r_recv.at[i], to)

    def small_to(i):
        to = {"dp": lax.rem(cycle.me + 1 + i, size)}
        return remote(small, sbuf.at[i], s_send.at[i], s_recv.at[i], to)

    def units_to(i):
        to = {"dp": lax.rem(cycle.me + 1 + i, size)}
        return remote(unit_ref, ubuf.at[i], u_send.at[i], u_recv.at[i], to)

    loads = [
        pltpu.make_async_copy(dwqkv_ref, dwqkv, in_sem.at[0]),
        pltpu.make_async_copy(dwo_ref, dwo, in_sem.at[1]),
        pltpu.make_async_copy(output_ref, output, in_sem.at[2]),
        pltpu.make_async_copy(teacher_ref, teacher, in_sem.at[3]),
    ]
    for load in loads:
        load.start()
    meet(g.all_peers() + [{"dp": lax.rem(cycle.me + 1 + i, size)} for i in range(size - 1)])
    for load in loads[:2]:
        load.wait()
    tick(0)
    for load in loads[2:]:
        load.wait()
    for i in range(size - 1):
        units_to(i).start()

    def sequence(s, total):
        length = len_ref[s]

        def block(i, total):
            at = pl.ds(pl.multiple_of(s * SLOT + i * 32, 32), 32)
            place = i * 32 + lax.broadcasted_iota(jnp.int32, (32, 1), 0)
            differ = output[at, :].astype(F32) - teacher[at, :].astype(F32)
            return total + fold(jnp.where(place < length, differ * differ, 0.0))

        return lax.fori_loop(0, SLOT // 32, block, total)

    squares = lax.fori_loop(0, seqs, sequence, jnp.zeros((8, width), F32))
    parts[...] = row_ref[...]
    for h in range(n):
        parts[7:8, h * width : (h + 1) * width] = jnp.sum(squares, axis=0, keepdims=True)
    for i in range(n - 1):
        row_to(i).start()
    tick(1)
    total = parts[:, cols(g.me)]
    for i in range(n - 1):
        row_to(i).wait()
        total = total + rbuf[i]
    small[:, 0:width] = total
    small[:, width : 2 * width] = head_ref[...]
    for i in range(size - 1):
        small_to(i).start()

    def rest(t, carry):
        tick(t)
        return carry

    lax.fori_loop(2, rings[0].ticks, rest, 0)
    small_sum = small[...]
    unit_sum = unit_ref[...]
    for i in range(size - 1):
        small_to(i).wait()
        units_to(i).wait()
        small_sum = small_sum + sbuf[i]
        unit_sum = unit_sum + ubuf[i]
    small_o[...] = small_sum
    units_o[...] = unit_sum
    for ring in rings:
        ring.drain()


def hbm():
    return pl.BlockSpec(memory_space=pl.ANY)


def vmem():
    return pl.BlockSpec(memory_space=pltpu.VMEM)


def smem():
    return pl.BlockSpec(memory_space=pltpu.SMEM)


def call(kernel, name, ident, ins, outs, scratch, flops):
    return pl.pallas_call(
        kernel,
        name=name,
        out_shape=[jax.ShapeDtypeStruct(shape, dtype) for shape, dtype, _ in outs],
        in_specs=ins,
        out_specs=[spec for _, _, spec in outs],
        scratch_shapes=scratch,
        compiler_params=pltpu.CompilerParams(
            collective_id=ident, has_side_effects=True, vmem_limit_bytes=VMEM_LIMIT
        ),
        cost_estimate=pl.CostEstimate(flops=flops, bytes_accessed=30_000_000, transcendentals=0),
    )


def attend(n, seqs, heads, args):
    width, rows, nx, half = heads * HD, SLOT // n, n // 2, SLOT // 2
    tokens, owned = seqs * SLOT, seqs * rows
    v, dma = pltpu.VMEM, pltpu.SemaphoreType.DMA
    return call(
        functools.partial(attend_kernel, n, seqs, heads),
        "attend",
        0,
        [smem(), hbm(), hbm(), vmem(), hbm(), hbm(), hbm(), vmem(), vmem(), hbm(), vmem()],
        [
            ((tokens, D), BF, hbm()),
            ((tokens, 3 * width), BF, hbm()),
            ((seqs, heads, SLOT, SLOT), BF, hbm()),
            ((tokens, width), F32, hbm()),
            ((tokens, width), BF, hbm()),
            ((owned, D), F32, hbm()),
            ((owned, D), F32, hbm()),
            ((owned, 128), F32, hbm()),
            ((owned, D), BF, hbm()),
            ((8, D), F32, vmem()),
            ((seqs, rows, D), BF, hbm()),
        ],
        [
            v((tokens, D), BF),
            v((D, 3 * width), BF),
            v((width, D), BF),
            v((tokens, 3 * width), BF),
            v((seqs, heads, SLOT, SLOT), BF),
            v((tokens, width), F32),
            v((tokens, width), BF),
            v((seqs, nx, rows, D), F32),
            v((seqs, nx, rows, D), BF),
            v((seqs, nx, rows, D), BF),
            v((seqs, nx - 1, rows, D), BF),
            v((seqs, nx - 1, rows, D), BF),
            v((owned, D), F32),
            v((owned, D), F32),
            v((owned, 128), F32),
            v((owned, D), BF),
            v((8, D), F32),
            v((SLOT, SLOT), F32),
            dma((6,)),
            dma((seqs, 9)),
            dma((n - 1,)),
            dma((n - 1,)),
            dma((n - 1,)),
            dma((n - 1,)),
        ]
        + gather_sems(seqs, nx)
        + reduce_sems(seqs, nx),
        10_000_000_000,
    )(*args)


def feed(n, seqs, units, args):
    rows, nx = SLOT // n, n // 2
    tokens, owned = seqs * SLOT, seqs * rows
    v, dma = pltpu.VMEM, pltpu.SemaphoreType.DMA
    return call(
        functools.partial(feed_kernel, n, seqs, units),
        "feed",
        1,
        [smem(), hbm(), hbm(), hbm(), hbm(), vmem(), hbm(), hbm(), vmem(), hbm(), vmem()],
        [
            ((owned, D), BF, hbm()),
            ((owned, D), BF, hbm()),
            ((owned, D), F32, hbm()),
            ((D, units), BF, hbm()),
            ((units, D), BF, hbm()),
            ((8, D), F32, vmem()),
            ((2, units), F32, vmem()),
        ],
        [
            v((tokens, D), BF),
            v((tokens, D), BF),
            v((D, units), BF),
            v((units, D), BF),
            v((tokens, units), BF),
            v((tokens, units), BF),
            v((tokens, units), BF),
            v((seqs, nx, rows, D), F32),
            v((seqs, nx, rows, D), BF),
            v((seqs, nx, rows, D), BF),
            v((seqs, nx - 1, rows, D), BF),
            v((seqs, nx - 1, rows, D), BF),
            v((owned, D), F32),
            v((owned, D), F32),
            v((owned, 128), F32),
            v((owned, D), BF),
            v((owned, D), F32),
            v((owned, D), BF),
            v((owned, D), BF),
            v((owned, D), BF),
            v((owned, D), F32),
            v((SLOT, NB), F32),
            v((D // NB, NB, D), BF),
            v((7, 8, D), F32),
            v((2, 8, units), F32),
            dma((6,)),
            dma((seqs, 3)),
            dma((2, D // NB)),
        ]
        + (gather_sems(seqs, nx) + reduce_sems(seqs, nx)) * 2,
        30_000_000_000,
    )(*args)


def attend_back(n, seqs, heads, units, size, args):
    width, rows, nx = heads * HD, SLOT // n, n // 2
    tokens, owned = seqs * SLOT, seqs * rows
    v, dma = pltpu.VMEM, pltpu.SemaphoreType.DMA
    return call(
        functools.partial(attend_back_kernel, n, seqs, heads, size),
        "attend_back",
        2,
        [hbm()] * 14 + [vmem()],
        [
            ((tokens, width), F32, hbm()),
            ((D, 3 * width), BF, hbm()),
            ((width, D), BF, hbm()),
            ((D, units), F32, hbm()),
            ((units, D), F32, hbm()),
            ((seqs, n, rows, width), BF, hbm()),
            ((8, width), F32, vmem()),
        ],
        [
            v((tokens, D), BF),
            v((owned, D), F32),
            v((tokens, D), BF),
            v((tokens, 3 * width), BF),
            v((seqs, heads, SLOT, SLOT), BF),
            v((tokens, width), F32),
            v((tokens, width), BF),
            v((D, 3 * width), BF),
            v((width, D), BF),
            v((SLOT, width), BF),
            v((tokens, 3 * width), BF),
            v((SLOT, SLOT), F32),
            v((SLOT, SLOT), BF),
            v((3, SLOT, width), F32),
            v((SLOT, width), F32),
            v((seqs, nx, SLOT, width), F32),
            v((seqs, nx, SLOT, width), BF),
            v((seqs, nx, SLOT, width), BF),
            v((seqs, nx - 1, SLOT, width), BF),
            v((seqs, nx - 1, SLOT, width), BF),
            v((tokens, width), F32),
            v((D // NB, NB, 3 * width), BF),
            v((width, D), BF),
            v((4, 8, width), F32),
            v((D, units), BF),
            v((units, D), BF),
            dma((14,)),
            dma((seqs,)),
            dma((D // NB,)),
            dma((n - 1,)),
            dma((n - 1,)),
        ]
        + gather_sems(seqs, nx)
        + reduce_sems(seqs, nx)
        + ring_scratch((D, units), size) * 2
        + ring_scratch((units, D), size) * 2,
        20_000_000_000,
    )(*args)


def settle(n, size, seqs, width, units, args):
    v, dma = pltpu.VMEM, pltpu.SemaphoreType.DMA
    tokens = seqs * SLOT
    return call(
        functools.partial(settle_kernel, n, size, seqs),
        "settle",
        3,
        [smem()] + [hbm()] * 4 + [vmem()] * 3,
        [((D, width), F32, hbm())] * 3
        + [((width, D), F32, hbm()), ((8, 2 * width), F32, vmem()), ((2, units), F32, vmem())],
        [
            v((D, 3 * width), BF),
            v((width, D), BF),
            v((tokens, width), BF),
            v((tokens, width), BF),
            v((8, D), F32),
            v((8, 2 * width), F32),
            v((n - 1, 8, width), F32),
            v((size - 1, 8, 2 * width), F32),
            v((size - 1, 2, units), F32),
            dma((4,)),
            dma((n - 1,)),
            dma((n - 1,)),
        ]
        + [dma((size - 1,))] * 4
        + ring_scratch((D, 3 * width), size) * 2
        + ring_scratch((width, D), size) * 2,
        1_000_000_000,
    )(*args)


def on_device(
    n,
    size,
    tokens,
    query_weight,
    query_bias,
    key_weight,
    value_weight,
    value_bias,
    output_weight,
    output_bias,
    attention_gain,
    attention_shift,
    inner_weight,
    inner_bias,
    down_weight,
    down_bias,
    final_gain,
    final_shift,
    head_alpha,
    unit_alpha,
    width_alpha,
    multipliers,
    head_noise,
    unit_noise,
    width_noise,
    lengths,
    teacher,
    upstream,
):
    row_count, width = tokens.shape
    heads = width // HD
    units = inner_weight.shape[1]
    seqs = row_count // SLOT
    rows = SLOT // n
    rank = lax.axis_index("hid")
    local_lengths = lax.dynamic_slice_in_dim(lengths, lax.axis_index("dp") * seqs, seqs)
    head_local = lax.dynamic_slice_in_dim(head_alpha, rank * heads, heads)
    unit_local = lax.dynamic_slice_in_dim(unit_alpha, rank * units, units)
    width_local = lax.dynamic_slice_in_dim(width_alpha, rank * width, width)
    head_gate, head_pull = jax.vjp(lambda part: gate_value(head_noise, part), head_local)
    unit_gate, unit_pull = jax.vjp(lambda part: gate_value(unit_noise, part), unit_local)
    width_gate, width_pull = jax.vjp(lambda part: gate_value(width_noise, part), width_local)
    gate_row = jnp.repeat(head_gate, HD)[None, :]
    vectors = jnp.stack(
        [
            output_bias,
            width_gate,
            attention_gain,
            attention_shift,
            down_bias,
            final_gain,
            final_shift,
            jnp.zeros_like(down_bias),
        ]
    )
    change = (upstream.astype(F32) - teacher.astype(F32)).astype(BF).reshape(seqs, n, rows, width)
    full, qkv, prob, ctx, gat, nrm, pre, rstd, mid, par, change_rows = attend(
        n,
        seqs,
        heads,
        (
            local_lengths,
            tokens,
            change,
            vectors,
            query_weight,
            key_weight,
            value_weight,
            query_bias[None, :],
            value_bias[None, :],
            output_weight,
            gate_row,
        ),
    )
    out_rows, d_low, d_res, dw_inner, dw_down, row_sums, unit_sums = feed(
        n,
        seqs,
        units,
        (
            local_lengths,
            mid,
            nrm,
            pre,
            rstd,
            par,
            change_rows.reshape(seqs * rows, D),
            inner_weight,
            inner_bias[None, :],
            down_weight,
            unit_gate[None, :],
        ),
    )
    tokens_grad, dw_qkv, dw_o, dw_inner, dw_down, output, head_sums = attend_back(
        n,
        seqs,
        heads,
        units,
        size,
        (
            d_low,
            d_res,
            full,
            qkv,
            prob,
            ctx,
            gat,
            query_weight,
            key_weight,
            value_weight,
            output_weight,
            dw_inner,
            dw_down,
            out_rows.reshape(seqs, rows, D),
            gate_row,
        ),
    )
    output = output.reshape(row_count, width)
    dw_q, dw_k, dw_v, dw_o, small, unit_all = settle(
        n,
        size,
        seqs,
        width,
        units,
        (local_lengths, dw_qkv, dw_o, output, teacher, row_sums, unit_sums, head_sums),
    )
    rows_all, head_all = small[:, :width], small[:, width:]
    distill_mse = jnp.sum(rows_all[7]) / (jnp.sum(lengths).astype(F32) * D)
    lag = jax.grad(lagrangian, argnums=(0, 1, 2, 3))(head_alpha, unit_alpha, width_alpha, multipliers)
    head_alpha_grad = head_pull(jnp.sum(head_all[0].reshape(heads, HD), axis=1))[0]
    head_alpha_grad += lax.dynamic_slice_in_dim(lag[0], rank * heads, heads)
    unit_alpha_grad = unit_pull(unit_all[0])[0]
    unit_alpha_grad += lax.dynamic_slice_in_dim(lag[1], rank * units, units)
    width_alpha_grad = width_pull(rows_all[2])[0]
    width_alpha_grad += lax.dynamic_slice_in_dim(lag[2], rank * width, width)
    return (
        output,
        tokens_grad,
        dw_q,
        head_all[1],
        dw_k,
        dw_v,
        head_all[3],
        dw_o,
        rows_all[6],
        rows_all[4],
        rows_all[5],
        dw_inner,
        unit_all[1],
        dw_down,
        rows_all[3],
        rows_all[0],
        rows_all[1],
        head_alpha_grad,
        unit_alpha_grad,
        width_alpha_grad,
        distill_mse,
        multipliers + ASCENT * lag[3],
    )


def solution(mesh):
    tall, wide, vec, rep = P("dp", "hid"), P(None, "hid"), P("hid"), P()
    deep = P("hid", None)
    return jax.shard_map(
        functools.partial(on_device, mesh.shape["hid"], mesh.shape["dp"]),
        mesh=mesh,
        in_specs=(tall, wide, vec, wide, wide, vec, deep, vec, vec, vec, wide, vec, deep)
        + (vec,) * 3
        + (rep,) * 4
        + (vec,) * 3
        + (rep, tall, tall),
        out_specs=(tall, tall, wide, vec, wide, wide, vec, deep, vec, vec, vec, wide, vec, deep)
        + (vec,) * 6
        + (rep, rep),
        check_vma=False,
    )
```

time: 813 us -> 453 us (0.56); the launches traced: 803 us -> 452 us
  Pallas kernels: 0 us -> 412 us
  waiting for transfers between devices: 406 us -> 0 us
  matrix products: 126 us -> 0 us
  blocking collectives: 109 us -> 0 us
  other arithmetic: 82.2 us -> 12.2 us
  local copies, waits for them, and re-layouts: 55.4 us -> 19.5 us
  between operations: 23.3 us -> 9.11 us
    pallas_call x0 -> x4, Pallas kernels: none -> 412 us  [the longest x1 131 us: feed(): call(functools.partial(feed_kernel, n, seqs, units), 'feed', 1, [smem(),...]
    reduce_scatter x4 -> x0, waiting for transfers between devices: 165 us -> none  [the longest x2 87.1 us: branch_total(): lax.psum_scatter(partial_sum.astype(jnp.bfloat16), 'hid', scatter_dimensi...]
    all_gather x4 -> x0, waiting for transfers between devices: 126 us -> none  [the longest x2 72.9 us: gather_features(): return lax.all_gather(sharded, 'hid', axis=1, tiled=True)]
    dot_general x24 -> x0, matrix products: 126 us -> none  [the longest x6 30.1 us: times_transpose(): lax.dot_general(left_side, right_side, (((1,), (1,)), ((), ())), preferre...]
    psum x1 -> x0, waiting for transfers between devices: 114 us -> none  [on_device(): lax.psum(query_weight_grad.astype(jnp.bfloat16), 'dp').astype(jnp.float32)]
    psum x8 -> x0, blocking collectives: 109 us -> none  [the longest x1 42.3 us: on_device(): squared = lax.psum(jnp.sum(live_rows * differ * differ), ('dp', 'hid'))]
    reduce_sum x11 -> x3, other arithmetic: 38.5 us -> 2.94 us  [the longest x2 2.82 us: on_device(): distill_mse = jnp.sum(rows_all[7]) / (jnp.sum(lengths).astype(F32) * D)]
    reshape x9 -> x0, local copies, waits for them, and re-layouts: 30.8 us -> none  [the longest x2 9.82 us: on_device(): times_transpose(d_attn_full, output_weight)]
  transfers between devices with their start and end apart: 9 -> 0, of which waited for: 9 -> 0; matrix products, arithmetic and copies ran while one was open for 7% -> 0% of each run, Pallas kernels for 0% -> 0%
where the time goes in v1:
time: 453 us; the launch traced here: 452 us
  Pallas kernels  412 us (91%)
  local copies, waits for them, and re-layouts  19.5 us (4%)
  other arithmetic  12.2 us (3%)
  between operations  9.11 us (2%)
    pallas_call x1, Pallas kernels, feed(): call(functools.partial(feed_kernel, n, seqs, units), 'feed', 1, [smem(),...  131 us
    pallas_call x1, Pallas kernels, attend_back(): call(functools.partial(attend_back_kernel, n, seqs, heads, size), 'attend...  125 us
    pallas_call x1, Pallas kernels, attend(): call(functools.partial(attend_kernel, n, seqs, heads), 'attend', 0, [smem...  88.1 us
    pallas_call x1, Pallas kernels, settle(): call(functools.partial(settle_kernel, n, size, seqs), 'settle', 3, [smem(...  66.8 us
    unnamed x34, local copies, waits for them, and re-layouts  14.1 us

profile of v1, /device:TPU:0, one launch (start us, length us, event | category | flops | bytes accessed | tf_op | source)
XLA Modules:
  0.0 452.4 jit_solution(3432104709149990476)
XLA Ops:
  0.7 0.8 fusion.19
  1.5 0.7 broadcast_in_dim_reshape.3.refs_10_.refs_14_
  2.1 0.8 fusion.13
  2.9 1.4 stack.31.refs_3_
  4.3 1.2 dynamic_slice.21.refs_0_
  5.5 2.8 subtract_convert_fusion
  8.3 88.1 %attend.1 = (bf16[2048,1024]{1,0:T(8,128)(2,1)}, bf16[2048,768]{1,0:T(8,128)(2,1)}, bf16[4,4,512,512]{3,2,1,0:T(8,128)(2,1)}, f32[2048,256]{1,0:T(8,128)}, bf16[...) custom-call(s32[4]{0:T(128)} %dynamic_slice.21.refs_0_, ...), custom_call_target="tpu_custom_call" | custom-call | flops 10000000000 | bytes 30000000 | tf_op jit(solution)/shard_map/attend/pallas_call | solution.py:1177
  97.1 131.4 %feed.1 = (bf16[512,1024]{1,0:T(8,128)(2,1)}, bf16[512,1024]{1,0:T(8,128)(2,1)}, f32[512,1024]{1,0:T(8,128)}, bf16[1024,1024]{1,0:T(8,128)(2,1)}, bf16[1024,1024...) custom-call(s32[4]{0:T(128)} %dynamic_slice.21.refs_0_, bf16[512,1024]{1,0:T(8,128)(2,1)} %get-tuple-element.53.refs_1_, ...), custom_call_target="tpu_custom_call" | custom-call | flops 30000001024 | bytes 30000000 | tf_op jit(solution)/shard_map/feed/pallas_call | solution.py:1231
  228.4 125.3 %attend_back.1 = (f32[2048,256]{1,0:T(8,128)}, bf16[1024,768]{1,0:T(8,128)(2,1)}, bf16[256,1024]{1,0:T(8,128)(2,1)}, f32[1024,1024]{1,0:T(8,128)}, f32[1024,1024...) custom-call(bf16[512,1024]{1,0:T(8,128)(2,1)} %get-tuple-element.59.refs_0_, ...), custom_call_target="tpu_custom_call" | custom-call | flops 20000000000 | bytes 30000000 | tf_op jit(solution)/shard_map/attend_back/pallas_call | solution.py:1284
  353.8 66.8 %settle.1 = (f32[1024,256]{1,0:T(8,128)}, f32[1024,256]{1,0:T(8,128)}, f32[1024,256]{1,0:T(8,128)}, f32[256,1024]{1,0:T(8,128)}, f32[8,512]{1,0:T(8,128)}, /*index=5*/f32[2,1024]{1,0:T(2,128)}) custom-call(s32[4]{0:T(128)} %dynamic_slice.21.refs_0_, bf16[1024,768]{1,0:T(8,128)(2,1)} %get-tuple-element.71.refs_1_, ...), custom_call_target="tpu_custom_call" | custom-call | flops 1000000000 | bytes 30000000 | tf_op jit(solution)/shard_map/settle/pallas_call | solution.py:1342
  420.6 2.2 slice_reduce_fusion
  430.5 0.6 fusion.9
  431.1 1.4 fusion.22
  433.1 0.6 fusion.2
  437.1 2.3 copy.56
  439.4 1.3 copy.57
  440.7 0.6 copy-done.6
  441.3 1.0 copy.58
  442.3 1.0 copy.59
  443.3 1.0 copy.60
  444.3 1.0 copy.61
  445.5 2.1 copy.62
  447.6 1.6 copy-done
  449.2 2.0 copy.63
  (38 shorter events, 5.5 us)
Async XLA Ops:
  8.3 88.1 %copy-start.7 = (f32[4096]{0:T(1024)S(1)}, f32[4096]{0:T(1024)}, u32[]{:S(2)}) copy-start(f32[4096]{0:T(1024)} %param.43) | copy-start | bytes 49156
  8.3 88.1 %copy-start.9 = (f32[1024]{0:T(1024)S(1)}, f32[1024]{0:T(1024)}, u32[]{:S(2)}) copy-start(f32[1024]{0:T(1024)} %param.47) | copy-start | bytes 12292
  353.7 70.3 %copy-start.11 = (f32[16]{0:T(128)S(1)}, f32[16]{0:T(128)}, u32[]{:S(2)}) copy-start(f32[16]{0:T(128)} %param.42) | copy-start | bytes 196
  353.8 71.6 %copy-start.8 = (f32[1024]{0:T(1024)S(1)}, f32[1024]{0:T(1024)}, u32[]{:S(2)}) copy-start(f32[1024]{0:T(1024)} %param.44) | copy-start | bytes 12292
  353.8 72.8 %copy-start.10 = (f32[2]{0:T(128)S(1)}, f32[2]{0:T(128)}, u32[]{:S(2)}) copy-start(f32[2]{0:T(128)} %param.45) | copy-start | bytes 28
  353.8 80.8 %copy-start.12 = (s32[32]{0:T(128)S(1)}, s32[32]{0:T(128)}, u32[]{:S(2)}) copy-start(s32[32]{0:T(128)} %param.49) | copy-start | bytes 388
  420.6 18.8 %copy-start.2 = (f32[2048,256]{1,0:T(8,128)S(1)}, f32[2048,256]{1,0:T(8,128)}, u32[]{:S(2)}) copy-start(f32[2048,256]{1,0:T(8,128)} %get-tuple-element.130) | copy-start | bytes 6291460
  439.4 2.0 copy-start.6
  439.4 2.9 copy-start.5
  441.3 2.0 copy-start.4
  441.3 2.9 copy-start.3
  442.3 3.2 copy-start.1
  445.5 3.7 copy-start

commit v2 on v1

--- a/solution.py
+++ b/solution.py
@@ -252,13 +252,13 @@
     return [
         pltpu.VMEM((size - 1, tall, broad), BF),
         pltpu.VMEM((2, tall, broad), F32),
-        pltpu.SemaphoreType.DMA((2, 3)),
+        pltpu.SemaphoreType.DMA((2,)),
     ] + [step] * 4 + [pltpu.SemaphoreType.REGULAR]
 
 
 class Ring:
-    def __init__(self, cycle, data, outs, way, scratch):
-        self.cycle, self.data, self.outs, self.way = cycle, data, outs, way
+    def __init__(self, cycle, data, target, way, scratch):
+        self.cycle, self.data, self.target, self.way = cycle, data, target, way
         self.size = cycle.size
         self.recv, self.stage, self.stage_sem, self.ss, self.sr, self.gs, self.gr, self.free = scratch
         self.tall, self.broad, self.across = split(data.shape, self.size)
@@ -304,26 +304,17 @@
 
         lax.fori_loop(0, self.tall // RB, part, 0)
 
-    def _puts(self, number, slot):
+    def _out(self, number, slot):
         row, column = self.block(number)
-        puts = []
-        for k, (target, first, count) in enumerate(self.outs):
-            if self.across == 1:
-                source = self.stage.at[slot, :, pl.ds(first, count)]
-                place = target.at[pl.ds(row, self.tall), :]
-            else:
-                source = self.stage.at[slot]
-                place = target.at[pl.ds(row, self.tall), pl.ds(column, self.broad)]
-            puts.append(pltpu.make_async_copy(source, place, self.stage_sem.at[slot, k]))
-        return puts
+        place = self.target.at[pl.ds(row, self.tall), pl.ds(column, self.broad)]
+        return pltpu.make_async_copy(self.stage.at[slot], place, self.stage_sem.at[slot])
 
     def _put(self, number, count):
         slot = lax.rem(count, 2)
 
         @pl.when(count >= 2)
         def _():
-            for put in self._puts(number, slot):
-                put.wait()
+            self._out(number, slot).wait()
 
         row, column = self.block(number)
 
@@ -334,8 +325,7 @@
             return carry
 
         lax.fori_loop(0, self.tall // RB, part, 0)
-        for put in self._puts(number, slot):
-            put.start()
+        self._out(number, slot).start()
 
     def tick(self, t):
         size = self.size
@@ -378,8 +368,7 @@
 
     def drain(self):
         for slot in range(2):
-            for put in self._puts(0, slot):
-                put.wait()
+            self._out(0, slot).wait()
 
         def step(t, carry):
             self._pass(t).wait_send()
@@ -404,7 +393,7 @@
         len_ref, tok_ref, change_ref, par_ref, wq_ref, wk_ref, wv_ref, qb_ref, vb_ref, wo_ref, gate_ref,
         full_o, qkv_o, prob_o, ctx_o, gat_o, nrm_o, pre_o, rstd_o, mid_o, par_o, change_o,
         full, wqkv, wo, qkv, prob, ctx, gat, own, psend, precv, xsend, xrecv,
-        nrm, pre, rstd, mid, par, score, in_sem, out_sem, vec_send, vec_recv, ch_send, ch_recv, *sems,
+        nrm, pre, rstd, mid, par, chg, score, in_sem, out_sem, vec_send, vec_recv, ch_send, ch_recv, *sems,
     ) = refs
     g = Group(n)
     width = heads * HD
@@ -428,14 +417,14 @@
     def change_to(i):
         to = lax.rem(g.me + 1 + i, n)
         return remote(
-            change_ref.at[:, g.slot(to)], change_o.at[:, :, cols(g.me)], ch_send.at[i], ch_recv.at[i], to
+            change_ref.at[:, g.slot(to)], chg.at[:, :, cols(g.me)], ch_send.at[i], ch_recv.at[i], to
         )
 
     def change_from(i):
         to = lax.rem(g.me + 1 + i, n)
         frm = lax.rem(g.me - 1 - i + n, n)
         return remote(
-            change_ref.at[:, g.slot(to)], change_o.at[:, :, cols(frm)], ch_send.at[i], ch_recv.at[i], to
+            change_ref.at[:, g.slot(to)], chg.at[:, :, cols(frm)], ch_send.at[i], ch_recv.at[i], to
         )
 
     loads = [
@@ -445,9 +434,10 @@
         pltpu.make_async_copy(wo_ref, wo, in_sem.at[3]),
         pltpu.make_async_copy(par_ref, par.at[:, cols(g.me)], in_sem.at[4]),
         pltpu.make_async_copy(
-            change_ref.at[:, g.slot(g.me)], change_o.at[:, :, cols(g.me)], in_sem.at[5]
+            change_ref.at[:, g.slot(g.me)], chg.at[:, :, cols(g.me)], in_sem.at[5]
         ),
     ]
+    chg_out = pltpu.make_async_copy(chg, change_o, in_sem.at[6])
 
     def sequence_outs(s):
         return [
@@ -472,9 +462,9 @@
         ga.start(s)
         return carry
 
-    lax.fori_loop(0, seqs, begin, 0)
     for i in range(n - 1):
         vec_to(i).start()
+    lax.fori_loop(0, seqs, begin, 0)
     for load in loads:
         load.start()
     for i in range(n - 1):
@@ -564,10 +554,12 @@
 
     lax.fori_loop(0, seqs, sequence, 0)
     re.cross(seqs - 1)
-    finish(seqs - 1)
     loads[5].wait()
     for i in range(n - 1):
         change_from(i).wait()
+    chg_out.start()
+    finish(seqs - 1)
+    chg_out.wait()
 
     def end(s, carry):
         ga.drain(s)
@@ -694,16 +686,15 @@
         mine = pl.ds(pl.multiple_of(s * SLOT + g.c * half, half), half)
         own[s] = nn(inner[mine, :], w2[...]).reshape(n // 2, rows, D)
 
-        @pl.when(s > 0)
-        def _():
-            finish_forward(s - 1)
+        @pl.when(s > 1)
+        def _():
+            finish_forward(s - 2)
 
         return carry
 
     lax.fori_loop(0, seqs, forward, 0)
     rf.cross(seqs - 1)
     gd.relay(0)
-    finish_forward(seqs - 1)
 
     def row_outs(s):
         return [
@@ -764,6 +755,10 @@
 
         lax.fori_loop(0, units // NB, part, 0)
 
+        @pl.when(s < 2)
+        def _():
+            finish_forward(seqs - 2 + s)
+
         @pl.when(s + 1 < seqs)
         def _():
             gd.relay(s + 1)
@@ -778,9 +773,9 @@
         mine = pl.ds(pl.multiple_of(s * SLOT + g.c * half, half), half)
         own[s] = nt(slope[mine, :], w1[...]).reshape(n // 2, rows, D)
 
-        @pl.when(s > 0)
-        def _():
-            finish_backward(s - 1)
+        @pl.when(s > 1)
+        def _():
+            finish_backward(s - 2)
 
         return carry
 
@@ -799,7 +794,7 @@
         return carry
 
     lax.fori_loop(0, units // NB, down_grad, 0)
-    finish_backward(seqs - 1)
+    finish_backward(seqs - 2)
     for b in range(units // NB):
         grad_out(0, b).wait()
 
@@ -812,6 +807,7 @@
         return carry
 
     lax.fori_loop(0, D // NB, inner_grad, 0)
+    finish_backward(seqs - 1)
     for k in range(7):
         rowsum_o[k : k + 1, :] = jnp.sum(sums[k], axis=0, keepdims=True)
     rowsum_o[7:8, :] = jnp.zeros((1, D), F32)
@@ -839,7 +835,7 @@
         wq_ref, wk_ref, wv_ref, wo_ref, dw1_ref, dw2_ref, out_ref, gate_ref,
         tgrad_o, dwqkv_o, dwo_o, dw1_o, dw2_o, output_o, sums_o,
         dattn, dres, full, qkv, prob, ctx, gat, wqkv, wo, dctx, dqkv, dprob, dscore, acc,
-        block_f, own, psend, precv, xsend, xrecv, tgrad, grad, gwo, sums, dw1, dw2,
+        block_f, own, psend, precv, xsend, xrecv, tgrad, grad, gwo, moved, sums, dw1, dw2,
         in_sem, out_sem, grad_sem, move_send, move_recv, *sems,
     ) = refs
     g = Group(n)
@@ -848,25 +844,24 @@
     for k, (data, target) in enumerate(((dw1, dw1_o), (dw2, dw2_o))):
         for way in (1, -1):
             i = 11 + 8 * len(rings)
-            outs = [(target, 0, data.shape[1])]
-            rings.append(Ring(cycle, data, outs, way, sems[i : i + 8]))
+            rings.append(Ring(cycle, data, target, way, sems[i : i + 8]))
     ticks = rings[0].ticks
 
-    def tick(t):
-        for ring in rings:
+    def tick(t, which):
+        for ring in rings[2 * which : 2 * which + 2]:
             ring.tick(t)
 
     def move_to(i):
         to = lax.rem(g.me + 1 + i, n)
         return remote(
-            out_ref.at[:, :, cols_of(to)], output_o.at[:, g.slot(g.me)], move_send.at[i], move_recv.at[i], to
+            out_ref.at[:, :, cols_of(to)], moved.at[:, g.slot(g.me)], move_send.at[i], move_recv.at[i], to
         )
 
     def move_from(i):
         to = lax.rem(g.me + 1 + i, n)
         frm = lax.rem(g.me - 1 - i + n, n)
         return remote(
-            out_ref.at[:, :, cols_of(to)], output_o.at[:, g.slot(frm)], move_send.at[i], move_recv.at[i], to
+            out_ref.at[:, :, cols_of(to)], moved.at[:, g.slot(frm)], move_send.at[i], move_recv.at[i], to
         )
 
     width = heads * HD
@@ -890,7 +885,7 @@
         pltpu.make_async_copy(full_ref, full, in_sem.at[8]),
         pltpu.make_async_copy(gat_ref, gat, in_sem.at[9]),
         pltpu.make_async_copy(
-            out_ref.at[:, :, cols_of(g.me)], output_o.at[:, g.slot(g.me)], in_sem.at[11]
+            out_ref.at[:, :, cols_of(g.me)], moved.at[:, g.slot(g.me)], in_sem.at[11]
         ),
     ]
     grads_in = [
@@ -911,10 +906,13 @@
     sums[...] = jnp.zeros_like(sums)
     for load in grads_in:
         load.wait()
-    tick(0)
+    tick(0, 0)
+    tick(0, 1)
     ga.relay(0)
     for load in loads[:8]:
         load.wait()
+    tick(1, 0)
+    tick(1, 1)
 
     lanes = lax.broadcasted_iota(jnp.int32, (1, width), 1)
     head_lanes = [
@@ -947,6 +945,8 @@
         d_gated = nt(dattn[here, :], wo[...])
         sums[0] += fold(d_gated * ctx[here, :])
         dctx[...] = (d_gated * gate_ref[...]).astype(BF)
+        first = 2 + s * (heads + 2) // 2
+        tick(first, 0)
 
         @pl.when(s + 1 < seqs)
         def _():
@@ -969,6 +969,7 @@
                 return carry
 
             lax.fori_loop(0, SLOT // 64, softmax, 0)
+            tick(first + (h + 1) // 2, (h + 1) % 2)
             terms = (
                 nn(dscore[...], qkv[here, width : 2 * width] * head_lanes[h]),
                 tn(dscore[...], qkv[here, 0:width] * head_lanes[h]),
@@ -976,7 +977,6 @@
             )
             for k in range(3):
                 acc[k] = terms[k] if h == 0 else acc[k] + terms[k]
-            tick(s * heads + h + 1)
         scales = (HD**-0.5, HD**-0.5, 1.0)
         for k in range(3):
             rounded = (acc[k] * scales[k]).astype(BF)
@@ -986,6 +986,7 @@
             token_block(s, 2 * chip + 1 - g.c)
             psend[s, chip] = block_f[...].astype(BF)
         re.start(s)
+        tick(first + (heads + 1) // 2, 1)
         for chip in range(n // 2):
             token_block(s, 2 * chip + g.c)
             own[s, chip] = block_f[...]
@@ -1018,20 +1019,24 @@
     gwo_out = pltpu.make_async_copy(gwo, dwo_o, in_sem.at[10])
     gwo_out.start()
     finish(seqs - 1)
+    for i in range(n - 1):
+        move_from(i).wait()
+    moved_out = pltpu.make_async_copy(moved, output_o, in_sem.at[14])
+    moved_out.start()
     for k in range(4):
         sums_o[k : k + 1, :] = jnp.sum(sums[k], axis=0, keepdims=True)
     sums_o[4:8, :] = jnp.zeros((4, width), F32)
     gwo_out.wait()
 
     def rest(t, carry):
-        tick(t)
+        tick(t, 0)
+        tick(t, 1)
         return carry
 
-    lax.fori_loop(seqs * heads + 1, ticks, rest, 0)
+    lax.fori_loop(2 + seqs * (heads + 2) // 2, ticks, rest, 0)
+    moved_out.wait()
     for ring in rings:
         ring.drain()
-    for i in range(n - 1):
-        move_from(i).wait()
 
     def end_grad(b, carry):
         grad_out(b).wait()
@@ -1051,19 +1056,18 @@
     (
         len_ref, dwqkv_ref, dwo_ref, output_ref, teacher_ref, row_ref, unit_ref, head_ref,
         dwq_o, dwk_o, dwv_o, dwo_o, small_o, units_o,
-        dwqkv, dwo, output, teacher, parts, small, rbuf, sbuf, ubuf,
+        dwq, dwk, dwv, dwo, output, teacher, parts, small, rbuf, sbuf, ubuf,
         in_sem, r_send, r_recv, s_send, s_recv, u_send, u_recv, *sems,
     ) = refs
     g = Group(n)
     cycle = Cycle(size)
     width = head_ref.shape[1]
     cols = lambda h: pl.ds(pl.multiple_of(h * width, width), width)
-    outs = [(dwq_o, 0, width), (dwk_o, width, width), (dwv_o, 2 * width, width)]
     rings = []
-    for data, targets in ((dwqkv, outs), (dwo, [(dwo_o, 0, D)])):
+    for data, target in ((dwq, dwq_o), (dwk, dwk_o), (dwv, dwv_o), (dwo, dwo_o)):
         for way in (1, -1):
             i = 8 * len(rings)
-            rings.append(Ring(cycle, data, targets, way, sems[i : i + 8]))
+            rings.append(Ring(cycle, data, target, way, sems[i : i + 8]))
 
     def tick(t):
         for ring in rings:
@@ -1082,18 +1086,20 @@
         return remote(unit_ref, ubuf.at[i], u_send.at[i], u_recv.at[i], to)
 
     loads = [
-        pltpu.make_async_copy(dwqkv_ref, dwqkv, in_sem.at[0]),
-        pltpu.make_async_copy(dwo_ref, dwo, in_sem.at[1]),
-        pltpu.make_async_copy(output_ref, output, in_sem.at[2]),
-        pltpu.make_async_copy(teacher_ref, teacher, in_sem.at[3]),
+        pltpu.make_async_copy(dwqkv_ref.at[:, pl.ds(0, width)], dwq, in_sem.at[0]),
+        pltpu.make_async_copy(dwqkv_ref.at[:, pl.ds(width, width)], dwk, in_sem.at[1]),
+        pltpu.make_async_copy(dwqkv_ref.at[:, pl.ds(2 * width, width)], dwv, in_sem.at[2]),
+        pltpu.make_async_copy(dwo_ref, dwo, in_sem.at[3]),
+        pltpu.make_async_copy(output_ref, output, in_sem.at[4]),
+        pltpu.make_async_copy(teacher_ref, teacher, in_sem.at[5]),
     ]
     for load in loads:
         load.start()
     meet(g.all_peers() + [{"dp": lax.rem(cycle.me + 1 + i, size)} for i in range(size - 1)])
-    for load in loads[:2]:
+    for load in loads[:4]:
         load.wait()
     tick(0)
-    for load in loads[2:]:
+    for load in loads[4:]:
         load.wait()
     for i in range(size - 1):
         units_to(i).start()
@@ -1210,8 +1216,9 @@
             v((owned, 128), F32),
             v((owned, D), BF),
             v((8, D), F32),
+            v((seqs, rows, D), BF),
             v((SLOT, SLOT), F32),
-            dma((6,)),
+            dma((7,)),
             dma((seqs, 9)),
             dma((n - 1,)),
             dma((n - 1,)),
@@ -1319,10 +1326,11 @@
             v((tokens, width), F32),
             v((D // NB, NB, 3 * width), BF),
             v((width, D), BF),
+            v((seqs, n, rows, width), BF),
             v((4, 8, width), F32),
             v((D, units), BF),
             v((units, D), BF),
-            dma((14,)),
+            dma((15,)),
             dma((seqs,)),
             dma((D // NB,)),
             dma((n - 1,)),
@@ -1347,7 +1355,9 @@
         [((D, width), F32, hbm())] * 3
         + [((width, D), F32, hbm()), ((8, 2 * width), F32, vmem()), ((2, units), F32, vmem())],
         [
-            v((D, 3 * width), BF),
+            v((D, width), BF),
+            v((D, width), BF),
+            v((D, width), BF),
             v((width, D), BF),
             v((tokens, width), BF),
             v((tokens, width), BF),
@@ -1356,12 +1366,12 @@
             v((n - 1, 8, width), F32),
             v((size - 1, 8, 2 * width), F32),
             v((size - 1, 2, units), F32),
-            dma((4,)),
+            dma((6,)),
             dma((n - 1,)),
             dma((n - 1,)),
         ]
         + [dma((size - 1,))] * 4
-        + ring_scratch((D, 3 * width), size) * 2
+        + ring_scratch((D, width), size) * 6
         + ring_scratch((width, D), size) * 2,
         1_000_000_000,
     )(*args)

time: 453 us -> 384 us (0.85)
  Pallas kernels: 412 us -> 343 us
    pallas_call x1, Pallas kernels: 131 us -> 99.1 us  [feed(): call(functools.partial(feed_kernel, n, seqs, units), 'feed', 1, [smem(),...]
    pallas_call x1, Pallas kernels: 125 us -> 103 us  [attend_back(): call(functools.partial(attend_back_kernel, n, seqs, heads, size), 'attend...]
    pallas_call x1, Pallas kernels: 66.8 us -> 57.2 us  [settle(): call(functools.partial(settle_kernel, n, size, seqs), 'settle', 3, [smem(...]
    pallas_call x1, Pallas kernels: 88.1 us -> 83.1 us  [attend(): call(functools.partial(attend_kernel, n, seqs, heads), 'attend', 0, [smem...]
where the time goes in v2:
time: 384 us
  Pallas kernels  343 us (89%)
  local copies, waits for them, and re-layouts  19.5 us (5%)
  other arithmetic  12.2 us (3%)
  between operations  9.11 us (2%)
    pallas_call x1, Pallas kernels, attend_back(): call(functools.partial(attend_back_kernel, n, seqs, heads, size), 'attend...  103 us
    pallas_call x1, Pallas kernels, feed(): call(functools.partial(feed_kernel, n, seqs, units), 'feed', 1, [smem(),...  99.1 us
    pallas_call x1, Pallas kernels, attend(): call(functools.partial(attend_kernel, n, seqs, heads), 'attend', 0, [smem...  83.1 us
    pallas_call x1, Pallas kernels, settle(): call(functools.partial(settle_kernel, n, size, seqs), 'settle', 3, [smem(...  57.2 us
    unnamed x34, local copies, waits for them, and re-layouts  14.1 us

profile of v2, /device:TPU:0, one launch (start us, length us, event | category | flops | bytes accessed | tf_op | source)
XLA Modules:
  0.0 383.7 jit_solution(7203464375796294042)
XLA Ops:
  0.7 0.8 fusion.19
  1.5 0.7 broadcast_in_dim_reshape.3.refs_10_.refs_14_
  2.1 0.8 fusion.13
  2.9 1.4 stack.31.refs_3_
  4.3 1.2 dynamic_slice.21.refs_0_
  5.5 2.8 subtract_convert_fusion
  8.3 83.1 %attend.1 = (bf16[2048,1024]{1,0:T(8,128)(2,1)}, bf16[2048,768]{1,0:T(8,128)(2,1)}, bf16[4,4,512,512]{3,2,1,0:T(8,128)(2,1)}, f32[2048,256]{1,0:T(8,128)}, bf16[...) custom-call(s32[4]{0:T(128)} %dynamic_slice.21.refs_0_, ...), custom_call_target="tpu_custom_call" | custom-call | flops 10000000000 | bytes 30000000 | tf_op jit(solution)/shard_map/attend/pallas_call | solution.py:1183
  92.1 99.1 %feed.1 = (bf16[512,1024]{1,0:T(8,128)(2,1)}, bf16[512,1024]{1,0:T(8,128)(2,1)}, f32[512,1024]{1,0:T(8,128)}, bf16[1024,1024]{1,0:T(8,128)(2,1)}, bf16[1024,1024...) custom-call(s32[4]{0:T(128)} %dynamic_slice.21.refs_0_, bf16[512,1024]{1,0:T(8,128)(2,1)} %get-tuple-element.53.refs_1_, ...), custom_call_target="tpu_custom_call" | custom-call | flops 30000001024 | bytes 30000000 | tf_op jit(solution)/shard_map/feed/pallas_call | solution.py:1238
  191.2 103.4 %attend_back.1 = (f32[2048,256]{1,0:T(8,128)}, bf16[1024,768]{1,0:T(8,128)(2,1)}, bf16[256,1024]{1,0:T(8,128)(2,1)}, f32[1024,1024]{1,0:T(8,128)}, f32[1024,1024...) custom-call(bf16[512,1024]{1,0:T(8,128)(2,1)} %get-tuple-element.59.refs_0_, ...), custom_call_target="tpu_custom_call" | custom-call | flops 20000000000 | bytes 30000000 | tf_op jit(solution)/shard_map/attend_back/pallas_call | solution.py:1291
  294.7 57.2 %settle.1 = (f32[1024,256]{1,0:T(8,128)}, f32[1024,256]{1,0:T(8,128)}, f32[1024,256]{1,0:T(8,128)}, f32[256,1024]{1,0:T(8,128)}, f32[8,512]{1,0:T(8,128)}, /*index=5*/f32[2,1024]{1,0:T(2,128)}) custom-call(s32[4]{0:T(128)} %dynamic_slice.21.refs_0_, bf16[1024,768]{1,0:T(8,128)(2,1)} %get-tuple-element.71.refs_1_, ...), custom_call_target="tpu_custom_call" | custom-call | flops 1000000000 | bytes 30000000 | tf_op jit(solution)/shard_map/settle/pallas_call | solution.py:1350
  351.9 2.2 slice_reduce_fusion
  361.8 0.6 fusion.9
  362.4 1.4 fusion.22
  364.5 0.6 fusion.2
  368.4 2.3 copy.56
  370.7 1.3 copy.57
  372.0 0.6 copy-done.6
  372.7 1.0 copy.58
  373.6 1.0 copy.59
  374.6 1.0 copy.60
  375.6 1.0 copy.61
  376.8 2.1 copy.62
  379.0 1.6 copy-done
  380.5 2.0 copy.63
  (38 shorter events, 5.5 us)
Async XLA Ops:
  8.3 83.1 %copy-start.7 = (f32[4096]{0:T(1024)S(1)}, f32[4096]{0:T(1024)}, u32[]{:S(2)}) copy-start(f32[4096]{0:T(1024)} %param.43) | copy-start | bytes 49156
  8.3 83.1 %copy-start.9 = (f32[1024]{0:T(1024)S(1)}, f32[1024]{0:T(1024)}, u32[]{:S(2)}) copy-start(f32[1024]{0:T(1024)} %param.47) | copy-start | bytes 12292
  294.6 60.7 %copy-start.11 = (f32[16]{0:T(128)S(1)}, f32[16]{0:T(128)}, u32[]{:S(2)}) copy-start(f32[16]{0:T(128)} %param.42) | copy-start | bytes 196
  294.6 62.0 %copy-start.8 = (f32[1024]{0:T(1024)S(1)}, f32[1024]{0:T(1024)}, u32[]{:S(2)}) copy-start(f32[1024]{0:T(1024)} %param.44) | copy-start | bytes 12292
  294.7 63.3 %copy-start.10 = (f32[2]{0:T(128)S(1)}, f32[2]{0:T(128)}, u32[]{:S(2)}) copy-start(f32[2]{0:T(128)} %param.45) | copy-start | bytes 28
  294.7 71.2 %copy-start.12 = (s32[32]{0:T(128)S(1)}, s32[32]{0:T(128)}, u32[]{:S(2)}) copy-start(s32[32]{0:T(128)} %param.49) | copy-start | bytes 388
  351.9 18.8 %copy-start.2 = (f32[2048,256]{1,0:T(8,128)S(1)}, f32[2048,256]{1,0:T(8,128)}, u32[]{:S(2)}) copy-start(f32[2048,256]{1,0:T(8,128)} %get-tuple-element.130) | copy-start | bytes 6291460
  370.7 2.0 copy-start.6
  370.7 2.9 copy-start.5
  372.7 2.0 copy-start.4
  372.7 2.9 copy-start.3
  373.6 3.2 copy-start.1
  376.8 3.7 copy-start

commit v3 on v2

--- a/solution.py
+++ b/solution.py
@@ -1,4 +1,5 @@
 import functools
+import math
 
 import jax
 import jax.numpy as jnp
@@ -36,18 +37,35 @@
     return jnp.clip(stretched, 0.0, 1.0)
 
 
+def gate_slope(noise, alpha):
+    s = jax.nn.sigmoid((jnp.log(noise) - jnp.log(1.0 - noise) + alpha) / BETA)
+    stretched = s * (ZETA - GAMMA) + GAMMA
+    free = (stretched > 0.0) & (stretched < 1.0)
+    return jnp.where(free, (ZETA - GAMMA) / BETA * s * (1.0 - s), 0.0)
+
+
 def keep_prob(alpha):
-    return jax.nn.sigmoid(alpha - BETA * jnp.log(-GAMMA / ZETA))
-
-
-def lagrangian(head_alpha, unit_alpha, width_alpha, multipliers):
-    heads_kept = jnp.sum(keep_prob(head_alpha))
-    units_kept = jnp.sum(keep_prob(unit_alpha))
-    dims_kept = jnp.sum(keep_prob(width_alpha))
-    full_size = 4.0 * D * D + 2.0 * D * FF
-    expected = (4.0 * HD * heads_kept * dims_kept + 2.0 * units_kept * dims_kept) / full_size
-    gap_value = 1.0 - expected - TARGET
-    return multipliers[0] * gap_value + multipliers[1] * gap_value * gap_value
+    return jax.nn.sigmoid(alpha - BETA * math.log(-GAMMA / ZETA))
+
+
+def lane_of(row, place):
+    lanes = lax.broadcasted_iota(jnp.int32, row.shape, 1)
+    return jnp.sum(jnp.where(lanes == place, row, 0.0), axis=1, keepdims=True)
+
+
+def head_row(noise_ref, alpha_ref, rank, heads):
+    lanes = lax.broadcasted_iota(jnp.int32, (1, heads * HD), 1)
+    noise = jnp.full((1, heads * HD), 0.5, F32)
+    alpha = jnp.zeros((1, heads * HD), F32)
+    for h in range(heads):
+        here = (lanes >= h * HD) & (lanes < (h + 1) * HD)
+        noise = jnp.where(here, lane_of(noise_ref[...], h), noise)
+        alpha = jnp.where(here, lane_of(alpha_ref[...], rank * heads + h), alpha)
+    return noise, alpha
+
+
+def part_of(ref, rank, width):
+    return ref[:, pl.ds(pl.multiple_of(rank * width, width), width)]
 
 
 def nn(a, b):
@@ -251,8 +269,7 @@
     step = pltpu.SemaphoreType.DMA((size - 1,))
     return [
         pltpu.VMEM((size - 1, tall, broad), BF),
-        pltpu.VMEM((2, tall, broad), F32),
-        pltpu.SemaphoreType.DMA((2,)),
+        pltpu.SemaphoreType.DMA((size,)),
     ] + [step] * 4 + [pltpu.SemaphoreType.REGULAR]
 
 
@@ -260,7 +277,7 @@
     def __init__(self, cycle, data, target, way, scratch):
         self.cycle, self.data, self.target, self.way = cycle, data, target, way
         self.size = cycle.size
-        self.recv, self.stage, self.stage_sem, self.ss, self.sr, self.gs, self.gr, self.free = scratch
+        self.recv, self.out_sem, self.ss, self.sr, self.gs, self.gr, self.free = scratch
         self.tall, self.broad, self.across = split(data.shape, self.size)
         self.to, self.frm = {"dp": cycle.beside(way)}, {"dp": cycle.beside(-way)}
         self.ticks = 2 * self.size - 1
@@ -304,28 +321,10 @@
 
         lax.fori_loop(0, self.tall // RB, part, 0)
 
-    def _out(self, number, slot):
+    def _out(self, number, count):
         row, column = self.block(number)
         place = self.target.at[pl.ds(row, self.tall), pl.ds(column, self.broad)]
-        return pltpu.make_async_copy(self.stage.at[slot], place, self.stage_sem.at[slot])
-
-    def _put(self, number, count):
-        slot = lax.rem(count, 2)
-
-        @pl.when(count >= 2)
-        def _():
-            self._out(number, slot).wait()
-
-        row, column = self.block(number)
-
-        def part(i, carry):
-            at = pl.ds(pl.multiple_of(row + i * RB, RB), RB)
-            value = self.data[at, pl.ds(column, self.broad)].astype(F32)
-            self.stage[slot, pl.ds(pl.multiple_of(i * RB, RB), RB), :] = value
-            return carry
-
-        lax.fori_loop(0, self.tall // RB, part, 0)
-        self._out(number, slot).start()
+        return pltpu.make_async_copy(self.view(number), place, self.out_sem.at[count])
 
     def tick(self, t):
         size = self.size
@@ -352,7 +351,7 @@
         def _():
             pl.semaphore_wait(self.free, 1)
             self._pass(0).start()
-            self._put(1, 0)
+            self._out(1, 0).start()
 
         @pl.when((t > size - 1) & (t < 2 * size - 1))
         def _():
@@ -364,14 +363,14 @@
                 pl.semaphore_wait(self.free, 1)
                 self._pass(u + 1).start()
 
-            self._put(-u, u + 1)
+            self._out(-u, u + 1).start()
 
     def drain(self):
-        for slot in range(2):
-            self._out(0, slot).wait()
+        self._out(1, 0).wait()
 
         def step(t, carry):
             self._pass(t).wait_send()
+            self._out(-t, t + 1).wait()
             return carry
 
         lax.fori_loop(0, self.size - 1, step, 0)
@@ -390,10 +389,11 @@
 
 def attend_kernel(n, seqs, heads, *refs):
     (
-        len_ref, tok_ref, change_ref, par_ref, wq_ref, wk_ref, wv_ref, qb_ref, vb_ref, wo_ref, gate_ref,
-        full_o, qkv_o, prob_o, ctx_o, gat_o, nrm_o, pre_o, rstd_o, mid_o, par_o, change_o,
+        len_ref, tok_ref, up_ref, tea_ref, ob_ref, ag_ref, as_ref, db_ref, fg_ref, fs_ref,
+        wn_ref, wa_ref, hn_ref, ha_ref, wq_ref, wk_ref, wv_ref, qb_ref, vb_ref, wo_ref,
+        full_o, qkv_o, prob_o, ctx_o, gat_o, nrm_o, pre_o, rstd_o, mid_o, par_o, change_o, gate_o,
         full, wqkv, wo, qkv, prob, ctx, gat, own, psend, precv, xsend, xrecv,
-        nrm, pre, rstd, mid, par, chg, score, in_sem, out_sem, vec_send, vec_recv, ch_send, ch_recv, *sems,
+        nrm, pre, rstd, mid, par, chg, up, tea, change, vec, score, in_sem, out_sem, vec_send, vec_recv, ch_send, ch_recv, *sems,
     ) = refs
     g = Group(n)
     width = heads * HD
@@ -407,24 +407,24 @@
 
     def vec_to(i):
         to = lax.rem(g.me + 1 + i, n)
-        return remote(par_ref, par.at[:, cols(g.me)], vec_send.at[i], vec_recv.at[i], to)
+        return remote(vec, par.at[:, cols(g.me)], vec_send.at[i], vec_recv.at[i], to)
 
     def vec_from(i):
         to = lax.rem(g.me + 1 + i, n)
         frm = lax.rem(g.me - 1 - i + n, n)
-        return remote(par_ref, par.at[:, cols(frm)], vec_send.at[i], vec_recv.at[i], to)
+        return remote(vec, par.at[:, cols(frm)], vec_send.at[i], vec_recv.at[i], to)
 
     def change_to(i):
         to = lax.rem(g.me + 1 + i, n)
         return remote(
-            change_ref.at[:, g.slot(to)], chg.at[:, :, cols(g.me)], ch_send.at[i], ch_recv.at[i], to
+            change.at[:, g.slot(to)], chg.at[:, :, cols(g.me)], ch_send.at[i], ch_recv.at[i], to
         )
 
     def change_from(i):
         to = lax.rem(g.me + 1 + i, n)
         frm = lax.rem(g.me - 1 - i + n, n)
         return remote(
-            change_ref.at[:, g.slot(to)], chg.at[:, :, cols(frm)], ch_send.at[i], ch_recv.at[i], to
+            change.at[:, g.slot(to)], chg.at[:, :, cols(frm)], ch_send.at[i], ch_recv.at[i], to
         )
 
     loads = [
@@ -432,11 +432,13 @@
         pltpu.make_async_copy(wk_ref, wqkv.at[:, pl.ds(width, width)], in_sem.at[1]),
         pltpu.make_async_copy(wv_ref, wqkv.at[:, pl.ds(2 * width, width)], in_sem.at[2]),
         pltpu.make_async_copy(wo_ref, wo, in_sem.at[3]),
-        pltpu.make_async_copy(par_ref, par.at[:, cols(g.me)], in_sem.at[4]),
-        pltpu.make_async_copy(
-            change_ref.at[:, g.slot(g.me)], chg.at[:, :, cols(g.me)], in_sem.at[5]
-        ),
+        pltpu.make_async_copy(up_ref, up, in_sem.at[4]),
+        pltpu.make_async_copy(tea_ref, tea, in_sem.at[5]),
     ]
+    par_own = pltpu.make_async_copy(vec, par.at[:, cols(g.me)], in_sem.at[7])
+    change_own = pltpu.make_async_copy(
+        change.at[:, g.slot(g.me)], chg.at[:, :, cols(g.me)], in_sem.at[8]
+    )
     chg_out = pltpu.make_async_copy(chg, change_o, in_sem.at[6])
 
     def sequence_outs(s):
@@ -456,6 +458,12 @@
             pltpu.make_async_copy(mid.at[own_rows(s), :], mid_o.at[own_rows(s), :], out_sem.at[s, 8]),
         ]
 
+    for load in loads:
+        load.start()
+    for row, ref in ((0, ob_ref), (2, ag_ref), (3, as_ref), (4, db_ref), (5, fg_ref), (6, fs_ref)):
+        vec[row : row + 1, :] = ref[...]
+    vec[1:2, :] = gate_value(wn_ref[...], part_of(wa_ref, g.me, width))
+    vec[7:8, :] = jnp.zeros((1, width), F32)
     meet(g.all_peers())
 
     def begin(s, carry):
@@ -465,13 +473,26 @@
     for i in range(n - 1):
         vec_to(i).start()
     lax.fori_loop(0, seqs, begin, 0)
+    par_own.start()
+    gate_row = gate_value(*head_row(hn_ref, ha_ref, g.me, heads))
+    gate_o[...] = gate_row
     for load in loads:
-        load.start()
+        load.wait()
+
+    def differ(i, carry):
+        at = pl.ds(pl.multiple_of(i * 32, 32), 32)
+        value = (up[at, :].astype(F32) - tea[at, :].astype(F32)).astype(BF)
+        each = SLOT // n // 32
+        s, q = lax.div(i, SLOT // 32), lax.rem(i, SLOT // 32)
+        change[s, lax.div(q, each), pl.ds(pl.multiple_of(lax.rem(q, each) * 32, 32), 32), :] = value
+        return carry
+
+    lax.fori_loop(0, seqs * SLOT // 32, differ, 0)
+    change_own.start()
     for i in range(n - 1):
         change_to(i).start()
     ga.relay(0)
-    for load in loads[:5]:
-        load.wait()
+    par_own.wait()
     for i in range(n - 1):
         vec_from(i).wait()
     par_o[...] = par[...]
@@ -520,7 +541,7 @@
         def _():
             re.cross(s - 1)
 
-        length = len_ref[s]
+        length = len_ref[lax.axis_index("dp") * seqs + s]
         for h in range(heads):
             score[...] = nt(qkv[here, 0:width] * head_lanes[h], qkv[here, width : 2 * width])
 
@@ -536,7 +557,7 @@
             lax.fori_loop(0, SLOT // 64, softmax, 0)
             term = nn(prob[s, h], qkv[here, 2 * width : 3 * width] * head_lanes[h])
             ctx[here, :] = term if h == 0 else ctx[here, :] + term
-        gat[here, :] = (ctx[here, :] * gate_ref[...]).astype(BF)
+        gat[here, :] = (ctx[here, :] * gate_row).astype(BF)
         for copy in sequence_outs(s):
             copy.start()
         half = SLOT // 2
@@ -554,7 +575,7 @@
 
     lax.fori_loop(0, seqs, sequence, 0)
     re.cross(seqs - 1)
-    loads[5].wait()
+    change_own.wait()
     for i in range(n - 1):
         change_from(i).wait()
     chg_out.start()
@@ -572,10 +593,10 @@
 
 def feed_kernel(n, seqs, units, *refs):
     (
-        len_ref, mid_ref, nrm_ref, pre_ref, rstd_ref, par, change_ref, w1_ref, b1_ref, w2_ref, ugate_ref,
+        len_ref, mid_ref, nrm_ref, pre_ref, rstd_ref, par, change_ref, w1_ref, b1_ref, w2_ref, un_ref, ua_ref,
         out_o, dlow_o, dres_o, dw1_o, dw2_o, rowsum_o, unitsum_o,
         midf, dffn, w1, w2, act, inner, slope, own, psend, precv, xsend, xrecv,
-        nrm, pre, rstd, change, dtwo, dsend, fout, dlow, dres, wide, grad, sums, unit_sums,
+        nrm, pre, rstd, change, dtwo, dsend, fout, dlow, dres, wide, grad, sums, unit_sums, ugate_ref,
         in_sem, out_sem, grad_sem, *sems,
     ) = refs
     g = Group(n)
@@ -609,13 +630,14 @@
         load.start()
     sums[...] = jnp.zeros_like(sums)
     unit_sums[...] = jnp.zeros_like(unit_sums)
+    ugate_ref[...] = gate_value(un_ref[...], part_of(ua_ref, g.me, units))
     gm.relay(0)
     for load in loads:
         load.wait()
 
     def finish_forward(s):
         rf.arrive(s)
-        length = len_ref[s]
+        length = len_ref[lax.axis_index("dp") * seqs + s]
 
         def block(i, carry):
             at = pl.ds(pl.multiple_of(i * RB, RB), RB)
@@ -843,8 +865,8 @@
     rings = []
     for k, (data, target) in enumerate(((dw1, dw1_o), (dw2, dw2_o))):
         for way in (1, -1):
-            i = 11 + 8 * len(rings)
-            rings.append(Ring(cycle, data, target, way, sems[i : i + 8]))
+            i = 11 + 7 * len(rings)
+            rings.append(Ring(cycle, data, target, way, sems[i : i + 7]))
     ticks = rings[0].ticks
 
     def tick(t, which):
@@ -1066,8 +1088,8 @@
     rings = []
     for data, target in ((dwq, dwq_o), (dwk, dwk_o), (dwv, dwv_o), (dwo, dwo_o)):
         for way in (1, -1):
-            i = 8 * len(rings)
-            rings.append(Ring(cycle, data, target, way, sems[i : i + 8]))
+            i = 7 * len(rings)
+            rings.append(Ring(cycle, data, target, way, sems[i : i + 7]))
 
     def tick(t):
         for ring in rings:
@@ -1105,7 +1127,7 @@
         units_to(i).start()
 
     def sequence(s, total):
-        length = len_ref[s]
+        length = len_ref[cycle.me * seqs + s]
 
         def block(i, total):
             at = pl.ds(pl.multiple_of(s * SLOT + i * 32, 32), 32)
@@ -1149,6 +1171,91 @@
         ring.drain()
 
 
+def complete_kernel(n, heads, units, *refs):
+    (
+        dw1_ref, dw2_ref, dwq_ref, dwk_ref, dwv_ref, dwo_ref, tgrad_ref, output_ref,
+        small_ref, unit_ref, ha_ref, ua_ref, wa_ref, mult_ref, hn_ref, un_ref, wn_ref, len_ref,
+        dw1_o, dw2_o, dwq_o, dwk_o, dwv_o, dwo_o, tgrad_o, output_o,
+        qb_o, vb_o, ob_o, ag_o, as_o, db_o, fg_o, fs_o, b1_o, ha_o, ua_o, wa_o, mse_o, mult_o,
+        dw1, dw2, dwq, dwk, dwv, dwo, tgrad, output, fw1, fw2, fwq, fwk, fwv, fwo, in_sem, out_sem,
+    ) = refs
+    width = heads * HD
+    rank = lax.axis_index("hid")
+    wide = (
+        (dw1_ref, dw1, fw1, dw1_o), (dw2_ref, dw2, fw2, dw2_o), (dwq_ref, dwq, fwq, dwq_o),
+        (dwk_ref, dwk, fwk, dwk_o), (dwv_ref, dwv, fwv, dwv_o), (dwo_ref, dwo, fwo, dwo_o),
+        (tgrad_ref, tgrad, tgrad, tgrad_o), (output_ref, output, output, output_o),
+    )
+    parts = 4
+
+    def piece(ref, p):
+        rows = ref.shape[0] // parts
+        return ref.at[pl.ds(pl.multiple_of(p * rows, rows), rows), :]
+
+    def load(k, p):
+        return pltpu.make_async_copy(piece(wide[k][0], p), piece(wide[k][1], p), in_sem.at[k, p])
+
+    def store(k, p):
+        return pltpu.make_async_copy(piece(wide[k][2], p), piece(wide[k][3], p), out_sem.at[k, p])
+
+    for k in range(len(wide)):
+        for p in range(parts):
+            load(k, p).start()
+
+    head_all = small_ref[:, width : 2 * width]
+    for ref, row in ((ob_o, 6), (ag_o, 4), (as_o, 5), (db_o, 3), (fg_o, 0), (fs_o, 1)):
+        ref[...] = small_ref[row : row + 1, 0:width]
+    qb_o[...] = head_all[1:2, :]
+    vb_o[...] = head_all[3:4, :]
+    b1_o[...] = unit_ref[1:2, :]
+    keeps = [keep_prob(ref[...]) for ref in (ha_ref, ua_ref, wa_ref)]
+    heads_kept, units_kept, dims_kept = [jnp.sum(k, axis=1, keepdims=True) for k in keeps]
+    full_size = 4.0 * D * D + 2.0 * D * FF
+    gap = 1.0 - (4.0 * HD * heads_kept * dims_kept + 2.0 * units_kept * dims_kept) / full_size - TARGET
+    pull = -(lane_of(mult_ref[...], 0) + 2.0 * lane_of(mult_ref[...], 1) * gap) / full_size
+    slot = lax.broadcasted_iota(jnp.int32, (1, 2), 1)
+    mult_o[...] = mult_ref[...] + ASCENT * jnp.where(slot == 0, gap, gap * gap)
+
+    def pulled(alpha, factor):
+        k = keep_prob(alpha)
+        return pull * factor * k * (1.0 - k)
+
+    unit_alpha = part_of(ua_ref, rank, units)
+    ua_o[...] = unit_ref[0:1, :] * gate_slope(un_ref[...], unit_alpha) + pulled(unit_alpha, 2.0 * dims_kept)
+    width_alpha = part_of(wa_ref, rank, width)
+    wa_o[...] = small_ref[2:3, 0:width] * gate_slope(wn_ref[...], width_alpha) + pulled(
+        width_alpha, 4.0 * HD * heads_kept + 2.0 * units_kept
+    )
+    noise_row, alpha_row = head_row(hn_ref, ha_ref, rank, heads)
+    lanes = lax.broadcasted_iota(jnp.int32, (1, width), 1)
+    per_lane = head_all[0:1, :] * gate_slope(noise_row, alpha_row)
+    head_pulled = pulled(alpha_row, 4.0 * HD * dims_kept) * (1.0 / HD)
+    for h in range(heads):
+        here = (lanes >= h * HD) & (lanes < (h + 1) * HD)
+        ha_o[:, h : h + 1] = jnp.sum(jnp.where(here, per_lane + head_pulled, 0.0), axis=1, keepdims=True)
+    live = jnp.sum(len_ref[...].astype(F32), axis=1, keepdims=True)
+    mse_o[...] = jnp.sum(small_ref[7:8, 0:width], axis=1, keepdims=True) / (live * D)
+
+    for k, (_, low, high, _) in enumerate(wide):
+        rows = low.shape[0] // parts
+        for p in range(parts):
+            load(k, p).wait()
+            if low is not high:
+
+                step = min(64, rows)
+
+                def widen(i, carry, low=low, high=high, first=p * rows, step=step):
+                    at = pl.ds(pl.multiple_of(first + i * step, step), step)
+                    high[at, :] = low[at, :].astype(F32)
+                    return carry
+
+                lax.fori_loop(0, rows // step, widen, 0)
+            store(k, p).start()
+    for k in range(len(wide)):
+        for p in range(parts):
+            store(k, p).wait()
+
+
 def hbm():
     return pl.BlockSpec(memory_space=pl.ANY)
 
@@ -1184,7 +1291,7 @@
         functools.partial(attend_kernel, n, seqs, heads),
         "attend",
         0,
-        [smem(), hbm(), hbm(), vmem(), hbm(), hbm(), hbm(), vmem(), vmem(), hbm(), vmem()],
+        [smem()] + [hbm()] * 3 + [vmem()] * 10 + [hbm()] * 3 + [vmem()] * 2 + [hbm()],
         [
             ((tokens, D), BF, hbm()),
             ((tokens, 3 * width), BF, hbm()),
@@ -1197,6 +1304,7 @@
             ((owned, D), BF, hbm()),
             ((8, D), F32, vmem()),
             ((seqs, rows, D), BF, hbm()),
+            ((1, width), F32, vmem()),
         ],
         [
             v((tokens, D), BF),
@@ -1217,8 +1325,12 @@
             v((owned, D), BF),
             v((8, D), F32),
             v((seqs, rows, D), BF),
+            v((tokens, width), BF),
+            v((tokens, width), BF),
+            v((seqs, n, rows, width), BF),
+            v((8, width), F32),
             v((SLOT, SLOT), F32),
-            dma((7,)),
+            dma((9,)),
             dma((seqs, 9)),
             dma((n - 1,)),
             dma((n - 1,)),
@@ -1239,7 +1351,7 @@
         functools.partial(feed_kernel, n, seqs, units),
         "feed",
         1,
-        [smem(), hbm(), hbm(), hbm(), hbm(), vmem(), hbm(), hbm(), vmem(), hbm(), vmem()],
+        [smem(), hbm(), hbm(), hbm(), hbm(), vmem(), hbm(), hbm(), vmem(), hbm(), vmem(), vmem()],
         [
             ((owned, D), BF, hbm()),
             ((owned, D), BF, hbm()),
@@ -1275,6 +1387,7 @@
             v((D // NB, NB, D), BF),
             v((7, 8, D), F32),
             v((2, 8, units), F32),
+            v((1, units), F32),
             dma((6,)),
             dma((seqs, 3)),
             dma((2, D // NB)),
@@ -1297,8 +1410,8 @@
             ((tokens, width), F32, hbm()),
             ((D, 3 * width), BF, hbm()),
             ((width, D), BF, hbm()),
-            ((D, units), F32, hbm()),
-            ((units, D), F32, hbm()),
+            ((D, units), BF, hbm()),
+            ((units, D), BF, hbm()),
             ((seqs, n, rows, width), BF, hbm()),
             ((8, width), F32, vmem()),
         ],
@@ -1352,8 +1465,8 @@
         "settle",
         3,
         [smem()] + [hbm()] * 4 + [vmem()] * 3,
-        [((D, width), F32, hbm())] * 3
-        + [((width, D), F32, hbm()), ((8, 2 * width), F32, vmem()), ((2, units), F32, vmem())],
+        [((D, width), BF, hbm())] * 3
+        + [((width, D), BF, hbm()), ((8, 2 * width), F32, vmem()), ((2, units), F32, vmem())],
         [
             v((D, width), BF),
             v((D, width), BF),
@@ -1374,6 +1487,27 @@
         + ring_scratch((D, width), size) * 6
         + ring_scratch((width, D), size) * 2,
         1_000_000_000,
+    )(*args)
+
+
+def complete(n, heads, units, tokens, args):
+    v, dma, width = pltpu.VMEM, pltpu.SemaphoreType.DMA, heads * HD
+    shapes = [(D, units), (units, D), (D, width), (D, width), (D, width), (width, D)]
+    rows = [(width,)] * 8 + [(units,), (heads,), (units,), (width,), (1,), (2,)]
+    return pl.pallas_call(
+        functools.partial(complete_kernel, n, heads, units),
+        name="complete",
+        out_shape=[jax.ShapeDtypeStruct(shape, F32) for shape in shapes]
+        + [jax.ShapeDtypeStruct((tokens, width), F32), jax.ShapeDtypeStruct((tokens, width), BF)]
+        + [jax.ShapeDtypeStruct((1, count), F32) for (count,) in rows],
+        in_specs=[hbm()] * 8 + [vmem()] * 10,
+        out_specs=[hbm()] * 8 + [vmem()] * len(rows),
+        scratch_shapes=[v(shape, BF) for shape in shapes]
+        + [v((tokens, width), F32), v((tokens, width), BF)]
+        + [v(shape, F32) for shape in shapes]
+        + [dma((8, 4))] * 2,
+        compiler_params=pltpu.CompilerParams(vmem_limit_bytes=VMEM_LIMIT),
+        cost_estimate=pl.CostEstimate(flops=10_000_000, bytes_accessed=24_000_000, transcendentals=0),
     )(*args)
 
 
@@ -1412,44 +1546,34 @@
     units = inner_weight.shape[1]
     seqs = row_count // SLOT
     rows = SLOT // n
-    rank = lax.axis_index("hid")
-    local_lengths = lax.dynamic_slice_in_dim(lengths, lax.axis_index("dp") * seqs, seqs)
-    head_local = lax.dynamic_slice_in_dim(head_alpha, rank * heads, heads)
-    unit_local = lax.dynamic_slice_in_dim(unit_alpha, rank * units, units)
-    width_local = lax.dynamic_slice_in_dim(width_alpha, rank * width, width)
-    head_gate, head_pull = jax.vjp(lambda part: gate_value(head_noise, part), head_local)
-    unit_gate, unit_pull = jax.vjp(lambda part: gate_value(unit_noise, part), unit_local)
-    width_gate, width_pull = jax.vjp(lambda part: gate_value(width_noise, part), width_local)
-    gate_row = jnp.repeat(head_gate, HD)[None, :]
-    vectors = jnp.stack(
-        [
-            output_bias,
-            width_gate,
-            attention_gain,
-            attention_shift,
-            down_bias,
-            final_gain,
-            final_shift,
-            jnp.zeros_like(down_bias),
-        ]
-    )
-    change = (upstream.astype(F32) - teacher.astype(F32)).astype(BF).reshape(seqs, n, rows, width)
-    full, qkv, prob, ctx, gat, nrm, pre, rstd, mid, par, change_rows = attend(
+    flat = lambda vector: vector.reshape(1, vector.shape[0])
+    head_alpha, unit_alpha, width_alpha = flat(head_alpha), flat(unit_alpha), flat(width_alpha)
+    head_noise, unit_noise, width_noise = flat(head_noise), flat(unit_noise), flat(width_noise)
+    full, qkv, prob, ctx, gat, nrm, pre, rstd, mid, par, change_rows, gate_row = attend(
         n,
         seqs,
         heads,
         (
-            local_lengths,
+            lengths,
             tokens,
-            change,
-            vectors,
+            upstream,
+            teacher,
+            flat(output_bias),
+            flat(attention_gain),
+            flat(attention_shift),
+            flat(down_bias),
+            flat(final_gain),
+            flat(final_shift),
+            width_noise,
+            width_alpha,
+            head_noise,
+            head_alpha,
             query_weight,
             key_weight,
             value_weight,
-            query_bias[None, :],
-            value_bias[None, :],
+            flat(query_bias),
+            flat(value_bias),
             output_weight,
-            gate_row,
         ),
     )
     out_rows, d_low, d_res, dw_inner, dw_down, row_sums, unit_sums = feed(
@@ -1457,7 +1581,7 @@
         seqs,
         units,
         (
-            local_lengths,
+            lengths,
             mid,
             nrm,
             pre,
@@ -1465,9 +1589,10 @@
             par,
             change_rows.reshape(seqs * rows, D),
             inner_weight,
-            inner_bias[None, :],
+            flat(inner_bias),
             down_weight,
-            unit_gate[None, :],
+            unit_noise,
+            unit_alpha,
         ),
     )
     tokens_grad, dw_qkv, dw_o, dw_inner, dw_down, output, head_sums = attend_back(
@@ -1501,40 +1626,58 @@
         seqs,
         width,
         units,
-        (local_lengths, dw_qkv, dw_o, output, teacher, row_sums, unit_sums, head_sums),
+        (lengths, dw_qkv, dw_o, output, teacher, row_sums, unit_sums, head_sums),
     )
-    rows_all, head_all = small[:, :width], small[:, width:]
-    distill_mse = jnp.sum(rows_all[7]) / (jnp.sum(lengths).astype(F32) * D)
-    lag = jax.grad(lagrangian, argnums=(0, 1, 2, 3))(head_alpha, unit_alpha, width_alpha, multipliers)
-    head_alpha_grad = head_pull(jnp.sum(head_all[0].reshape(heads, HD), axis=1))[0]
-    head_alpha_grad += lax.dynamic_slice_in_dim(lag[0], rank * heads, heads)
-    unit_alpha_grad = unit_pull(unit_all[0])[0]
-    unit_alpha_grad += lax.dynamic_slice_in_dim(lag[1], rank * units, units)
-    width_alpha_grad = width_pull(rows_all[2])[0]
-    width_alpha_grad += lax.dynamic_slice_in_dim(lag[2], rank * width, width)
+    dw_inner, dw_down, dw_q, dw_k, dw_v, dw_o, tokens_grad, output, *vectors = complete(
+        n,
+        heads,
+        units,
+        row_count,
+        (
+            dw_inner,
+            dw_down,
+            dw_q,
+            dw_k,
+            dw_v,
+            dw_o,
+            tokens_grad,
+            output,
+            small,
+            unit_all,
+            head_alpha,
+            unit_alpha,
+            width_alpha,
+            flat(multipliers),
+            head_noise,
+            unit_noise,
+            width_noise,
+            flat(lengths),
+        ),
+    )
+    qb, vb, ob, ag, shift, db, fg, fs, b1, ha, ua, wa, mse, mult = [v.reshape(v.shape[1]) for v in vectors]
     return (
         output,
         tokens_grad,
         dw_q,
-        head_all[1],
+        qb,
         dw_k,
         dw_v,
-        head_all[3],
+        vb,
         dw_o,
-        rows_all[6],
-        rows_all[4],
-        rows_all[5],
+        ob,
+        ag,
+        shift,
         dw_inner,
-        unit_all[1],
+        b1,
         dw_down,
-        rows_all[3],
-        rows_all[0],
-        rows_all[1],
-        head_alpha_grad,
-        unit_alpha_grad,
-        width_alpha_grad,
-        distill_mse,
-        multipliers + ASCENT * lag[3],
+        db,
+        fg,
+        fs,
+        ha,
+        ua,
+        wa,
+        mse.reshape(()),
+        mult,
     )
 
 

time: 384 us -> 355 us (0.924)
  local copies, waits for them, and re-layouts: 19.5 us -> 0 us
  other arithmetic: 12.2 us -> 0 us
  Pallas kernels: 343 us -> 354 us
  between operations: 9.11 us -> 0.85 us
    unnamed x34 -> x0, local copies, waits for them, and re-layouts: 14.1 us -> none
    pallas_call x0 -> x1, Pallas kernels: none -> 10.4 us  [complete(): pl.pallas_call(functools.partial(complete_kernel, n, heads, units), name=...]
    reduce_sum x6 -> x0, other arithmetic: 4.78 us -> none  [the longest x2 2.82 us: on_device(): distill_mse = jnp.sum(rows_all[7]) / (jnp.sum(lengths).astype(F32) * D)]
where the time goes in v3:
time: 355 us; the launch traced here: 354 us
  Pallas kernels  354 us (100%)
    pallas_call x1, Pallas kernels, attend_back(): call(functools.partial(attend_back_kernel, n, seqs, heads, size), 'attend...  104 us
    pallas_call x1, Pallas kernels, feed(): call(functools.partial(feed_kernel, n, seqs, units), 'feed', 1, [smem(),...  99.1 us
    pallas_call x1, Pallas kernels, attend(): call(functools.partial(attend_kernel, n, seqs, heads), 'attend', 0, [smem...  83.2 us
    pallas_call x1, Pallas kernels, settle(): call(functools.partial(settle_kernel, n, size, seqs), 'settle', 3, [smem(...  57.5 us
    pallas_call x1, Pallas kernels, complete(): pl.pallas_call(functools.partial(complete_kernel, n, heads, units), name=...  10.4 us

profile of v3, /device:TPU:0, one launch (start us, length us, event | category | flops | bytes accessed | tf_op | source)
XLA Modules:
  0.0 354.5 jit_solution(13062704274117155269)
XLA Ops:
  0.7 83.2 %attend.1 = (bf16[2048,1024]{1,0:T(8,128)(2,1)}, bf16[2048,768]{1,0:T(8,128)(2,1)}, bf16[4,4,512,512]{3,2,1,0:T(8,128)(2,1)}, f32[2048,256]{1,0:T(8,128)}, bf16[...) custom-call(s32[32]{0:T(128)} %refs_0_.5, ...), custom_call_target="tpu_custom_call" | custom-call | flops 10000000000 | bytes 30000000 | tf_op jit(solution)/shard_map/attend/pallas_call | solution.py:1290
  83.9 99.1 %feed.1 = (bf16[512,1024]{1,0:T(8,128)(2,1)}, bf16[512,1024]{1,0:T(8,128)(2,1)}, f32[512,1024]{1,0:T(8,128)}, bf16[1024,1024]{1,0:T(8,128)(2,1)}, bf16[1024,1024...) custom-call(s32[32]{0:T(128)} %refs_0_.5, bf16[512,1024]{1,0:T(8,128)(2,1)} %get-tuple-element.76.refs_1_, ...), custom_call_target="tpu_custom_call" | custom-call | flops 30000001024 | bytes 30000000 | tf_op jit(solution)/shard_map/feed/pallas_call | solution.py:1350
  183.0 103.5 %attend_back.1 = (f32[2048,256]{1,0:T(8,128)}, bf16[1024,768]{1,0:T(8,128)(2,1)}, bf16[256,1024]{1,0:T(8,128)(2,1)}, bf16[1024,1024]{1,0:T(8,128)(2,1)}, bf16[10...) custom-call(bf16[512,1024]{1,0:T(8,128)(2,1)} %get-tuple-element.82.refs_0_, ...), custom_call_target="tpu_custom_call" | custom-call | flops 20000000000 | bytes 30000000 | tf_op jit(solution)/shard_map/attend_back/pallas_call | solution.py:1404
  286.5 57.5 %settle.1 = (bf16[1024,256]{1,0:T(8,128)(2,1)}, bf16[1024,256]{1,0:T(8,128)(2,1)}, bf16[1024,256]{1,0:T(8,128)(2,1)}, bf16[256,1024]{1,0:T(8,128)(2,1)}, f32[8,512]{1,0:T(8,128)}, /*index=5*/f32[2,1024]{1,0:T(2,128)}) custom-call(s32[32]{0:T(128)} %refs_0_.5, bf16[1024,768]{1,0:T(8,128)(2,1)} %get-tuple-element.95.refs_1_, ...), custom_call_target="tpu_custom_call" | custom-call | flops 1000000000 | bytes 30000000 | tf_op jit(solution)/shard_map/settle/pallas_call | solution.py:1463
  344.0 10.4 %complete.1 = (f32[1024,1024]{1,0:T(8,128)}, f32[1024,1024]{1,0:T(8,128)}, f32[1024,256]{1,0:T(8,128)}, f32[1024,256]{1,0:T(8,128)}, f32[1024,256]{1,0:T(8,128)}...) custom-call(bf16[1024,1024]{1,0:T(8,128)(2,1)} %get-tuple-element.93, ...), custom_call_target="tpu_custom_call" | custom-call | flops 10000000 | bytes 24000000 | tf_op jit(solution)/shard_map/complete/pallas_call | solution.py:1497

commit v4 on v3

--- a/solution.py
+++ b/solution.py
@@ -489,8 +489,6 @@
 
     lax.fori_loop(0, seqs * SLOT // 32, differ, 0)
     change_own.start()
-    for i in range(n - 1):
-        change_to(i).start()
     ga.relay(0)
     par_own.wait()
     for i in range(n - 1):
@@ -501,6 +499,8 @@
     head_lanes = [
         jnp.where((lanes >= h * HD) & (lanes < (h + 1) * HD), 1.0, 0.0).astype(BF) for h in range(heads)
     ]
+
+    scaled_lanes = [lane * HD**-0.5 for lane in head_lanes]
 
     def finish(s):
         re.arrive(s)
@@ -541,20 +541,25 @@
         def _():
             re.cross(s - 1)
 
+        @pl.when(s == seqs - 2)
+        def _():
+            for i in range(n - 1):
+                change_to(i).start()
+
         length = len_ref[lax.axis_index("dp") * seqs + s]
+        bias = jnp.where(lax.broadcasted_iota(jnp.int32, (1, SLOT), 1) < length, 0.0, MASKED)
         for h in range(heads):
-            score[...] = nt(qkv[here, 0:width] * head_lanes[h], qkv[here, width : 2 * width])
+            score[...] = nt(qkv[here, 0:width] * scaled_lanes[h], qkv[here, width : 2 * width])
 
             def softmax(i, carry, h=h):
                 at = pl.ds(pl.multiple_of(i * 64, 64), 64)
-                places = lax.broadcasted_iota(jnp.int32, (64, SLOT), 1)
-                scores = jnp.where(places < length, score[at, :] * (HD**-0.5), MASKED)
+                scores = score[at, :] + bias
                 exponent = jnp.exp(scores - jnp.max(scores, axis=1, keepdims=True))
                 total = jnp.sum(exponent, axis=1, keepdims=True)
                 prob[s, h, at, :] = (exponent * (1.0 / total)).astype(BF)
                 return carry
 
-            lax.fori_loop(0, SLOT // 64, softmax, 0)
+            lax.fori_loop(0, SLOT // 64, softmax, 0, unroll=True)
             term = nn(prob[s, h], qkv[here, 2 * width : 3 * width] * head_lanes[h])
             ctx[here, :] = term if h == 0 else ctx[here, :] + term
         gat[here, :] = (ctx[here, :] * gate_row).astype(BF)
@@ -990,7 +995,7 @@
                 dscore[at, :] = (weighted - p * total).astype(BF)
                 return carry
 
-            lax.fori_loop(0, SLOT // 64, softmax, 0)
+            lax.fori_loop(0, SLOT // 64, softmax, 0, unroll=True)
             tick(first + (h + 1) // 2, (h + 1) % 2)
             terms = (
                 nn(dscore[...], qkv[here, width : 2 * width] * head_lanes[h]),

time: 355 us -> 345 us (0.972)
  Pallas kernels: 354 us -> 344 us
    pallas_call x1, Pallas kernels: 83.2 us -> 73.8 us  [attend(): call(functools.partial(attend_kernel, n, seqs, heads), 'attend', 0, [smem...]
where the time goes in v4:
time: 345 us
  Pallas kernels  344 us (100%)
    pallas_call x1, Pallas kernels, attend_back(): call(functools.partial(attend_back_kernel, n, seqs, heads, size), 'attend...  103 us
    pallas_call x1, Pallas kernels, feed(): call(functools.partial(feed_kernel, n, seqs, units), 'feed', 1, [smem(),...  99.3 us
    pallas_call x1, Pallas kernels, attend(): call(functools.partial(attend_kernel, n, seqs, heads), 'attend', 0, [smem...  73.8 us
    pallas_call x1, Pallas kernels, settle(): call(functools.partial(settle_kernel, n, size, seqs), 'settle', 3, [smem(...  57.3 us
    pallas_call x1, Pallas kernels, complete(): pl.pallas_call(functools.partial(complete_kernel, n, heads, units), name=...  10.4 us

profile of v4, /device:TPU:0, one launch (start us, length us, event | category | flops | bytes accessed | tf_op | source)
XLA Modules:
  0.0 344.8 jit_solution(4766710424385940417)
XLA Ops:
  0.7 73.8 %attend.1 = (bf16[2048,1024]{1,0:T(8,128)(2,1)}, bf16[2048,768]{1,0:T(8,128)(2,1)}, bf16[4,4,512,512]{3,2,1,0:T(8,128)(2,1)}, f32[2048,256]{1,0:T(8,128)}, bf16[...) custom-call(s32[32]{0:T(128)} %refs_0_.5, ...), custom_call_target="tpu_custom_call" | custom-call | flops 10000000000 | bytes 30000000 | tf_op jit(solution)/shard_map/attend/pallas_call | solution.py:1295
  74.5 99.3 %feed.1 = (bf16[512,1024]{1,0:T(8,128)(2,1)}, bf16[512,1024]{1,0:T(8,128)(2,1)}, f32[512,1024]{1,0:T(8,128)}, bf16[1024,1024]{1,0:T(8,128)(2,1)}, bf16[1024,1024...) custom-call(s32[32]{0:T(128)} %refs_0_.5, bf16[512,1024]{1,0:T(8,128)(2,1)} %get-tuple-element.76.refs_1_, ...), custom_call_target="tpu_custom_call" | custom-call | flops 30000001024 | bytes 30000000 | tf_op jit(solution)/shard_map/feed/pallas_call | solution.py:1355
  173.8 103.2 %attend_back.1 = (f32[2048,256]{1,0:T(8,128)}, bf16[1024,768]{1,0:T(8,128)(2,1)}, bf16[256,1024]{1,0:T(8,128)(2,1)}, bf16[1024,1024]{1,0:T(8,128)(2,1)}, bf16[10...) custom-call(bf16[512,1024]{1,0:T(8,128)(2,1)} %get-tuple-element.82.refs_0_, ...), custom_call_target="tpu_custom_call" | custom-call | flops 20000000000 | bytes 30000000 | tf_op jit(solution)/shard_map/attend_back/pallas_call | solution.py:1409
  277.0 57.3 %settle.1 = (bf16[1024,256]{1,0:T(8,128)(2,1)}, bf16[1024,256]{1,0:T(8,128)(2,1)}, bf16[1024,256]{1,0:T(8,128)(2,1)}, bf16[256,1024]{1,0:T(8,128)(2,1)}, f32[8,512]{1,0:T(8,128)}, /*index=5*/f32[2,1024]{1,0:T(2,128)}) custom-call(s32[32]{0:T(128)} %refs_0_.5, bf16[1024,768]{1,0:T(8,128)(2,1)} %get-tuple-element.95.refs_1_, ...), custom_call_target="tpu_custom_call" | custom-call | flops 1000000000 | bytes 30000000 | tf_op jit(solution)/shard_map/settle/pallas_call | solution.py:1468
  334.3 10.4 %complete.1 = (f32[1024,1024]{1,0:T(8,128)}, f32[1024,1024]{1,0:T(8,128)}, f32[1024,256]{1,0:T(8,128)}, f32[1024,256]{1,0:T(8,128)}, f32[1024,256]{1,0:T(8,128)}...) custom-call(bf16[1024,1024]{1,0:T(8,128)(2,1)} %get-tuple-element.93, ...), custom_call_target="tpu_custom_call" | custom-call | flops 10000000 | bytes 24000000 | tf_op jit(solution)/shard_map/complete/pallas_call | solution.py:1502

commit v5 on v4

--- a/solution.py
+++ b/solution.py
@@ -858,17 +858,19 @@
 
 def attend_back_kernel(n, seqs, heads, size, *refs):
     (
-        dlow_ref, dres_ref, full_ref, qkv_ref, prob_ref, ctx_ref, gat_ref,
-        wq_ref, wk_ref, wv_ref, wo_ref, dw1_ref, dw2_ref, out_ref, gate_ref,
-        tgrad_o, dwqkv_o, dwo_o, dw1_o, dw2_o, output_o, sums_o,
+        len_ref, dlow_ref, dres_ref, full_ref, qkv_ref, prob_ref, ctx_ref, gat_ref,
+        wq_ref, wk_ref, wv_ref, wo_ref, dw1_ref, dw2_ref, out_ref, teacher_ref, gate_ref, row_ref, unit_ref,
+        tgrad_o, dwq_o, dwk_o, dwv_o, dwo_o, dw1_o, dw2_o, output_o, small_o, units_o,
         dattn, dres, full, qkv, prob, ctx, gat, wqkv, wo, dctx, dqkv, dprob, dscore, acc,
-        block_f, own, psend, precv, xsend, xrecv, tgrad, grad, gwo, moved, sums, dw1, dw2,
-        in_sem, out_sem, grad_sem, move_send, move_recv, *sems,
+        block_f, own, psend, precv, xsend, xrecv, tgrad, moved, sums, dw1, dw2,
+        dwq, dwk, dwv, dwo, teacher, parts, small, rbuf, sbuf, ubuf,
+        in_sem, out_sem, move_send, move_recv, r_send, r_recv, s_send, s_recv, u_send, u_recv, *sems,
     ) = refs
     g = Group(n)
     cycle = Cycle(size)
     rings = []
-    for k, (data, target) in enumerate(((dw1, dw1_o), (dw2, dw2_o))):
+    grads = ((dw1, dw1_o), (dw2, dw2_o), (dwq, dwq_o), (dwk, dwk_o), (dwv, dwv_o), (dwo, dwo_o))
+    for data, target in grads:
         for way in (1, -1):
             i = 11 + 7 * len(rings)
             rings.append(Ring(cycle, data, target, way, sems[i : i + 7]))
@@ -877,6 +879,18 @@
     def tick(t, which):
         for ring in rings[2 * which : 2 * which + 2]:
             ring.tick(t)
+
+    def row_to(i):
+        to = lax.rem(g.me + 1 + i, n)
+        return remote(parts.at[:, cols_of(to)], rbuf.at[i], r_send.at[i], r_recv.at[i], to)
+
+    def small_to(i):
+        to = {"dp": lax.rem(cycle.me + 1 + i, size)}
+        return remote(small, sbuf.at[i], s_send.at[i], s_recv.at[i], to)
+
+    def units_to(i):
+        to = {"dp": lax.rem(cycle.me + 1 + i, size)}
+        return remote(unit_ref, ubuf.at[i], u_send.at[i], u_recv.at[i], to)
 
     def move_to(i):
         to = lax.rem(g.me + 1 + i, n)
@@ -914,14 +928,15 @@
         pltpu.make_async_copy(
             out_ref.at[:, :, cols_of(g.me)], moved.at[:, g.slot(g.me)], in_sem.at[11]
         ),
+        pltpu.make_async_copy(teacher_ref, teacher, in_sem.at[10]),
     ]
     grads_in = [
         pltpu.make_async_copy(dw1_ref, dw1, in_sem.at[12]),
         pltpu.make_async_copy(dw2_ref, dw2, in_sem.at[13]),
     ]
-    meet(g.all_peers() + [{"dp": cycle.beside(1)}, {"dp": cycle.beside(-1)}])
     for load in grads_in:
         load.start()
+    meet(g.all_peers() + [{"dp": lax.rem(cycle.me + 1 + i, size)} for i in range(size - 1)])
 
     def begin(s, carry):
         ga.start(s)
@@ -982,6 +997,13 @@
         @pl.when(s > 0)
         def _():
             re.cross(s - 1)
+
+        @pl.when(s == 1)
+        def _():
+            for i in range(n - 1):
+                move_to(i).start()
+            for i in range(size - 1):
+                units_to(i).start()
 
         for h in range(heads):
             d_context = dctx[...] * head_lanes[h]
@@ -1026,143 +1048,72 @@
 
     lax.fori_loop(0, seqs, sequence, 0)
     re.cross(seqs - 1)
-    for i in range(n - 1):
-        move_to(i).start()
     for load in loads[8:]:
         load.wait()
 
-    def grad_out(b):
-        at = pl.ds(pl.multiple_of(b * NB, NB), NB)
-        return pltpu.make_async_copy(grad.at[b], dwqkv_o.at[at, :], grad_sem.at[b])
+    def rest(t, carry):
+        tick(t, 0)
+        tick(t, 1)
+        return carry
+
+    lax.fori_loop(2 + seqs * (heads + 2) // 2, ticks, rest, 0)
 
     def token_grad(b, carry):
         cols = pl.ds(pl.multiple_of(b * NB, NB), NB)
-        grad[b] = tn(full[:, cols], dqkv[...]).astype(BF)
-        grad_out(b).start()
+        term = tn(full[:, cols], dqkv[...])
+        for k, grad in enumerate((dwq, dwk, dwv)):
+            grad[cols, :] = term[:, k * width : (k + 1) * width].astype(BF)
         return carry
 
     lax.fori_loop(0, D // NB, token_grad, 0)
-    gwo[...] = tn(gat[...], dattn[...]).astype(BF)
-    gwo_out = pltpu.make_async_copy(gwo, dwo_o, in_sem.at[10])
-    gwo_out.start()
-    finish(seqs - 1)
+    for which in range(2, 5):
+        tick(0, which)
+    dwo[...] = tn(gat[...], dattn[...]).astype(BF)
+    tick(0, 5)
     for i in range(n - 1):
         move_from(i).wait()
     moved_out = pltpu.make_async_copy(moved, output_o, in_sem.at[14])
     moved_out.start()
-    for k in range(4):
-        sums_o[k : k + 1, :] = jnp.sum(sums[k], axis=0, keepdims=True)
-    sums_o[4:8, :] = jnp.zeros((4, width), F32)
-    gwo_out.wait()
-
-    def rest(t, carry):
-        tick(t, 0)
-        tick(t, 1)
-        return carry
-
-    lax.fori_loop(2 + seqs * (heads + 2) // 2, ticks, rest, 0)
-    moved_out.wait()
-    for ring in rings:
-        ring.drain()
-
-    def end_grad(b, carry):
-        grad_out(b).wait()
-        return carry
-
-    lax.fori_loop(0, D // NB, end_grad, 0)
-
-    def end(s, carry):
-        ga.drain(s)
-        out(s).wait()
-        return carry
-
-    lax.fori_loop(0, seqs, end, 0)
-
-
-def settle_kernel(n, size, seqs, *refs):
-    (
-        len_ref, dwqkv_ref, dwo_ref, output_ref, teacher_ref, row_ref, unit_ref, head_ref,
-        dwq_o, dwk_o, dwv_o, dwo_o, small_o, units_o,
-        dwq, dwk, dwv, dwo, output, teacher, parts, small, rbuf, sbuf, ubuf,
-        in_sem, r_send, r_recv, s_send, s_recv, u_send, u_recv, *sems,
-    ) = refs
-    g = Group(n)
-    cycle = Cycle(size)
-    width = head_ref.shape[1]
-    cols = lambda h: pl.ds(pl.multiple_of(h * width, width), width)
-    rings = []
-    for data, target in ((dwq, dwq_o), (dwk, dwk_o), (dwv, dwv_o), (dwo, dwo_o)):
-        for way in (1, -1):
-            i = 7 * len(rings)
-            rings.append(Ring(cycle, data, target, way, sems[i : i + 7]))
-
-    def tick(t):
-        for ring in rings:
-            ring.tick(t)
-
-    def row_to(i):
-        to = lax.rem(g.me + 1 + i, n)
-        return remote(parts.at[:, cols(to)], rbuf.at[i], r_send.at[i], r_recv.at[i], to)
-
-    def small_to(i):
-        to = {"dp": lax.rem(cycle.me + 1 + i, size)}
-        return remote(small, sbuf.at[i], s_send.at[i], s_recv.at[i], to)
-
-    def units_to(i):
-        to = {"dp": lax.rem(cycle.me + 1 + i, size)}
-        return remote(unit_ref, ubuf.at[i], u_send.at[i], u_recv.at[i], to)
-
-    loads = [
-        pltpu.make_async_copy(dwqkv_ref.at[:, pl.ds(0, width)], dwq, in_sem.at[0]),
-        pltpu.make_async_copy(dwqkv_ref.at[:, pl.ds(width, width)], dwk, in_sem.at[1]),
-        pltpu.make_async_copy(dwqkv_ref.at[:, pl.ds(2 * width, width)], dwv, in_sem.at[2]),
-        pltpu.make_async_copy(dwo_ref, dwo, in_sem.at[3]),
-        pltpu.make_async_copy(output_ref, output, in_sem.at[4]),
-        pltpu.make_async_copy(teacher_ref, teacher, in_sem.at[5]),
-    ]
-    for load in loads:
-        load.start()
-    meet(g.all_peers() + [{"dp": lax.rem(cycle.me + 1 + i, size)} for i in range(size - 1)])
-    for load in loads[:4]:
-        load.wait()
-    tick(0)
-    for load in loads[4:]:
-        load.wait()
-    for i in range(size - 1):
-        units_to(i).start()
-
-    def sequence(s, total):
+
+    def squares(s, total):
         length = len_ref[cycle.me * seqs + s]
 
         def block(i, total):
-            at = pl.ds(pl.multiple_of(s * SLOT + i * 32, 32), 32)
+            each = rows // 32
+            at = pl.ds(pl.multiple_of(lax.rem(i, each) * 32, 32), 32)
+            value = moved[s, lax.div(i, each), at, :].astype(F32)
             place = i * 32 + lax.broadcasted_iota(jnp.int32, (32, 1), 0)
-            differ = output[at, :].astype(F32) - teacher[at, :].astype(F32)
+            differ = value - teacher[pl.ds(pl.multiple_of(s * SLOT + i * 32, 32), 32), :].astype(F32)
             return total + fold(jnp.where(place < length, differ * differ, 0.0))
 
         return lax.fori_loop(0, SLOT // 32, block, total)
 
-    squares = lax.fori_loop(0, seqs, sequence, jnp.zeros((8, width), F32))
+    square_sum = lax.fori_loop(0, seqs, squares, jnp.zeros((8, width), F32))
     parts[...] = row_ref[...]
     for h in range(n):
-        parts[7:8, h * width : (h + 1) * width] = jnp.sum(squares, axis=0, keepdims=True)
+        parts[7:8, h * width : (h + 1) * width] = jnp.sum(square_sum, axis=0, keepdims=True)
     for i in range(n - 1):
         row_to(i).start()
-    tick(1)
-    total = parts[:, cols(g.me)]
+    for which in range(2, 6):
+        tick(1, which)
+    finish(seqs - 1)
+    total = parts[:, cols_of(g.me)]
     for i in range(n - 1):
         row_to(i).wait()
         total = total + rbuf[i]
     small[:, 0:width] = total
-    small[:, width : 2 * width] = head_ref[...]
+    for k in range(4):
+        small[k : k + 1, width : 2 * width] = jnp.sum(sums[k], axis=0, keepdims=True)
+    small[4:8, width : 2 * width] = jnp.zeros((4, width), F32)
     for i in range(size - 1):
         small_to(i).start()
 
-    def rest(t, carry):
-        tick(t)
+    def last(t, carry):
+        for which in range(2, 6):
+            tick(t, which)
         return carry
 
-    lax.fori_loop(2, rings[0].ticks, rest, 0)
+    lax.fori_loop(2, ticks, last, 0)
     small_sum = small[...]
     unit_sum = unit_ref[...]
     for i in range(size - 1):
@@ -1172,8 +1123,16 @@
         unit_sum = unit_sum + ubuf[i]
     small_o[...] = small_sum
     units_o[...] = unit_sum
+    moved_out.wait()
     for ring in rings:
         ring.drain()
+
+    def end(s, carry):
+        ga.drain(s)
+        out(s).wait()
+        return carry
+
+    lax.fori_loop(0, seqs, end, 0)
 
 
 def complete_kernel(n, heads, units, *refs):
@@ -1410,15 +1369,18 @@
         functools.partial(attend_back_kernel, n, seqs, heads, size),
         "attend_back",
         2,
-        [hbm()] * 14 + [vmem()],
+        [smem()] + [hbm()] * 15 + [vmem()] * 3,
         [
             ((tokens, width), F32, hbm()),
-            ((D, 3 * width), BF, hbm()),
+            ((D, width), BF, hbm()),
+            ((D, width), BF, hbm()),
+            ((D, width), BF, hbm()),
             ((width, D), BF, hbm()),
             ((D, units), BF, hbm()),
             ((units, D), BF, hbm()),
             ((seqs, n, rows, width), BF, hbm()),
-            ((8, width), F32, vmem()),
+            ((8, 2 * width), F32, vmem()),
+            ((2, units), F32, vmem()),
         ],
         [
             v((tokens, D), BF),
@@ -1442,56 +1404,35 @@
             v((seqs, nx - 1, SLOT, width), BF),
             v((seqs, nx - 1, SLOT, width), BF),
             v((tokens, width), F32),
-            v((D // NB, NB, 3 * width), BF),
-            v((width, D), BF),
             v((seqs, n, rows, width), BF),
             v((4, 8, width), F32),
             v((D, units), BF),
             v((units, D), BF),
-            dma((15,)),
-            dma((seqs,)),
-            dma((D // NB,)),
-            dma((n - 1,)),
-            dma((n - 1,)),
-        ]
-        + gather_sems(seqs, nx)
-        + reduce_sems(seqs, nx)
-        + ring_scratch((D, units), size) * 2
-        + ring_scratch((units, D), size) * 2,
-        20_000_000_000,
-    )(*args)
-
-
-def settle(n, size, seqs, width, units, args):
-    v, dma = pltpu.VMEM, pltpu.SemaphoreType.DMA
-    tokens = seqs * SLOT
-    return call(
-        functools.partial(settle_kernel, n, size, seqs),
-        "settle",
-        3,
-        [smem()] + [hbm()] * 4 + [vmem()] * 3,
-        [((D, width), BF, hbm())] * 3
-        + [((width, D), BF, hbm()), ((8, 2 * width), F32, vmem()), ((2, units), F32, vmem())],
-        [
             v((D, width), BF),
             v((D, width), BF),
             v((D, width), BF),
             v((width, D), BF),
-            v((tokens, width), BF),
             v((tokens, width), BF),
             v((8, D), F32),
             v((8, 2 * width), F32),
             v((n - 1, 8, width), F32),
             v((size - 1, 8, 2 * width), F32),
             v((size - 1, 2, units), F32),
-            dma((6,)),
+            dma((15,)),
+            dma((seqs,)),
+            dma((n - 1,)),
+            dma((n - 1,)),
             dma((n - 1,)),
             dma((n - 1,)),
         ]
         + [dma((size - 1,))] * 4
+        + gather_sems(seqs, nx)
+        + reduce_sems(seqs, nx)
+        + ring_scratch((D, units), size) * 2
+        + ring_scratch((units, D), size) * 2
         + ring_scratch((D, width), size) * 6
         + ring_scratch((width, D), size) * 2,
-        1_000_000_000,
+        20_000_000_000,
     )(*args)
 
 
@@ -1600,13 +1541,14 @@
             unit_alpha,
         ),
     )
-    tokens_grad, dw_qkv, dw_o, dw_inner, dw_down, output, head_sums = attend_back(
+    tokens_grad, dw_q, dw_k, dw_v, dw_o, dw_inner, dw_down, output, small, unit_all = attend_back(
         n,
         seqs,
         heads,
         units,
         size,
         (
+            lengths,
             d_low,
             d_res,
             full,
@@ -1621,18 +1563,13 @@
             dw_inner,
             dw_down,
             out_rows.reshape(seqs, rows, D),
+            teacher,
             gate_row,
+            row_sums,
+            unit_sums,
         ),
     )
     output = output.reshape(row_count, width)
-    dw_q, dw_k, dw_v, dw_o, small, unit_all = settle(
-        n,
-        size,
-        seqs,
-        width,
-        units,
-        (lengths, dw_qkv, dw_o, output, teacher, row_sums, unit_sums, head_sums),
-    )
     dw_inner, dw_down, dw_q, dw_k, dw_v, dw_o, tokens_grad, output, *vectors = complete(
         n,
         heads,

time: 345 us -> 331 us (0.959)
  Pallas kernels: 344 us -> 330 us
    pallas_call x1 -> x0, Pallas kernels: 57.3 us -> none  [settle(): call(functools.partial(settle_kernel, n, size, seqs), 'settle', 3, [smem(...]
    pallas_call x1, Pallas kernels: 103 us -> 147 us  [attend_back(): call(functools.partial(attend_back_kernel, n, seqs, heads, size), 'attend...]
where the time goes in v5:
time: 331 us
  Pallas kernels  330 us (100%)
    pallas_call x1, Pallas kernels, attend_back(): call(functools.partial(attend_back_kernel, n, seqs, heads, size), 'attend...  147 us
    pallas_call x1, Pallas kernels, feed(): call(functools.partial(feed_kernel, n, seqs, units), 'feed', 1, [smem(),...  99.3 us
    pallas_call x1, Pallas kernels, attend(): call(functools.partial(attend_kernel, n, seqs, heads), 'attend', 0, [smem...  73.9 us
    pallas_call x1, Pallas kernels, complete(): pl.pallas_call(functools.partial(complete_kernel, n, heads, units), name=...  10.4 us

profile of v5, /device:TPU:0, one launch (start us, length us, event | category | flops | bytes accessed | tf_op | source)
XLA Modules:
  0.0 331.0 jit_solution(1100441971608293714)
XLA Ops:
  0.7 73.9 %attend.1 = (bf16[2048,1024]{1,0:T(8,128)(2,1)}, bf16[2048,768]{1,0:T(8,128)(2,1)}, bf16[4,4,512,512]{3,2,1,0:T(8,128)(2,1)}, f32[2048,256]{1,0:T(8,128)}, bf16[...) custom-call(s32[32]{0:T(128)} %refs_0_.5, ...), custom_call_target="tpu_custom_call" | custom-call | flops 10000000000 | bytes 30000000 | tf_op jit(solution)/shard_map/attend/pallas_call | solution.py:1254
  74.5 99.3 %feed.1 = (bf16[512,1024]{1,0:T(8,128)(2,1)}, bf16[512,1024]{1,0:T(8,128)(2,1)}, f32[512,1024]{1,0:T(8,128)}, bf16[1024,1024]{1,0:T(8,128)(2,1)}, bf16[1024,1024...) custom-call(s32[32]{0:T(128)} %refs_0_.5, bf16[512,1024]{1,0:T(8,128)(2,1)} %get-tuple-element.73.refs_1_, ...), custom_call_target="tpu_custom_call" | custom-call | flops 30000001024 | bytes 30000000 | tf_op jit(solution)/shard_map/feed/pallas_call | solution.py:1314
  173.8 146.7 %attend_back.1 = (f32[2048,256]{1,0:T(8,128)}, bf16[1024,256]{1,0:T(8,128)(2,1)}, bf16[1024,256]{1,0:T(8,128)(2,1)}, bf16[1024,256]{1,0:T(8,128)(2,1)}, bf16[256...) custom-call(s32[32]{0:T(128)} %refs_0_.5, ...), custom_call_target="tpu_custom_call" | custom-call | flops 20000000000 | bytes 30000000 | tf_op jit(solution)/shard_map/attend_back/pallas_call | solution.py:1368
  320.5 10.4 %complete.1 = (f32[1024,1024]{1,0:T(8,128)}, f32[1024,1024]{1,0:T(8,128)}, f32[1024,256]{1,0:T(8,128)}, f32[1024,256]{1,0:T(8,128)}, f32[1024,256]{1,0:T(8,128)}...) custom-call(bf16[1024,1024]{1,0:T(8,128)(2,1)} %get-tuple-element.92, ...), custom_call_target="tpu_custom_call" | custom-call | flops 10000000 | bytes 24000000 | tf_op jit(solution)/shard_map/complete/pallas_call | solution.py:1443

commit v6 on v5

--- a/solution.py
+++ b/solution.py
@@ -879,6 +879,12 @@
     def tick(t, which):
         for ring in rings[2 * which : 2 * which + 2]:
             ring.tick(t)
+
+    def slot_tick(s, place):
+        served = [0, heads // 2, heads // 2 + 1, heads + 1]
+        if place in served:
+            k = served.index(place)
+            tick(2 + s * 2 + k // 2, k % 2)
 
     def row_to(i):
         to = lax.rem(g.me + 1 + i, n)
@@ -948,13 +954,12 @@
     sums[...] = jnp.zeros_like(sums)
     for load in grads_in:
         load.wait()
-    tick(0, 0)
-    tick(0, 1)
+    for t in range(2):
+        tick(t, 0)
+        tick(t, 1)
     ga.relay(0)
     for load in loads[:8]:
         load.wait()
-    tick(1, 0)
-    tick(1, 1)
 
     lanes = lax.broadcasted_iota(jnp.int32, (1, width), 1)
     head_lanes = [
@@ -987,8 +992,7 @@
         d_gated = nt(dattn[here, :], wo[...])
         sums[0] += fold(d_gated * ctx[here, :])
         dctx[...] = (d_gated * gate_ref[...]).astype(BF)
-        first = 2 + s * (heads + 2) // 2
-        tick(first, 0)
+        slot_tick(s, 0)
 
         @pl.when(s + 1 < seqs)
         def _():
@@ -1018,7 +1022,7 @@
                 return carry
 
             lax.fori_loop(0, SLOT // 64, softmax, 0, unroll=True)
-            tick(first + (h + 1) // 2, (h + 1) % 2)
+            slot_tick(s, h + 1)
             terms = (
                 nn(dscore[...], qkv[here, width : 2 * width] * head_lanes[h]),
                 tn(dscore[...], qkv[here, 0:width] * head_lanes[h]),
@@ -1035,7 +1039,7 @@
             token_block(s, 2 * chip + 1 - g.c)
             psend[s, chip] = block_f[...].astype(BF)
         re.start(s)
-        tick(first + (heads + 1) // 2, 1)
+        slot_tick(s, heads + 1)
         for chip in range(n // 2):
             token_block(s, 2 * chip + g.c)
             own[s, chip] = block_f[...]
@@ -1055,14 +1059,14 @@
         tick(t, 0)
         tick(t, 1)
         return carry
-
-    lax.fori_loop(2 + seqs * (heads + 2) // 2, ticks, rest, 0)
 
     def token_grad(b, carry):
         cols = pl.ds(pl.multiple_of(b * NB, NB), NB)
         term = tn(full[:, cols], dqkv[...])
         for k, grad in enumerate((dwq, dwk, dwv)):
             grad[cols, :] = term[:, k * width : (k + 1) * width].astype(BF)
+        tick(2 + 2 * seqs + b, 0)
+        tick(2 + 2 * seqs + b, 1)
         return carry
 
     lax.fori_loop(0, D // NB, token_grad, 0)
@@ -1070,6 +1074,7 @@
         tick(0, which)
     dwo[...] = tn(gat[...], dattn[...]).astype(BF)
     tick(0, 5)
+    lax.fori_loop(2 + 2 * seqs + D // NB, ticks, rest, 0)
     for i in range(n - 1):
         move_from(i).wait()
     moved_out = pltpu.make_async_copy(moved, output_o, in_sem.at[14])

time: 331 us -> 325 us (0.982)
  Pallas kernels: 330 us -> 324 us
    pallas_call x1, Pallas kernels: 147 us -> 141 us  [attend_back(): call(functools.partial(attend_back_kernel, n, seqs, heads, size), 'attend...]
where the time goes in v6:
time: 325 us
  Pallas kernels  324 us (100%)
    pallas_call x1, Pallas kernels, attend_back(): call(functools.partial(attend_back_kernel, n, seqs, heads, size), 'attend...  141 us
    pallas_call x1, Pallas kernels, feed(): call(functools.partial(feed_kernel, n, seqs, units), 'feed', 1, [smem(),...  99.3 us
    pallas_call x1, Pallas kernels, attend(): call(functools.partial(attend_kernel, n, seqs, heads), 'attend', 0, [smem...  73.9 us
    pallas_call x1, Pallas kernels, complete(): pl.pallas_call(functools.partial(complete_kernel, n, heads, units), name=...  10.4 us

profile of v6, /device:TPU:0, one launch (start us, length us, event | category | flops | bytes accessed | tf_op | source)
XLA Modules:
  0.0 325.1 jit_solution(2349952799669508724)
XLA Ops:
  0.7 73.9 %attend.1 = (bf16[2048,1024]{1,0:T(8,128)(2,1)}, bf16[2048,768]{1,0:T(8,128)(2,1)}, bf16[4,4,512,512]{3,2,1,0:T(8,128)(2,1)}, f32[2048,256]{1,0:T(8,128)}, bf16[...) custom-call(s32[32]{0:T(128)} %refs_0_.5, ...), custom_call_target="tpu_custom_call" | custom-call | flops 10000000000 | bytes 30000000 | tf_op jit(solution)/shard_map/attend/pallas_call | solution.py:1259
  74.5 99.3 %feed.1 = (bf16[512,1024]{1,0:T(8,128)(2,1)}, bf16[512,1024]{1,0:T(8,128)(2,1)}, f32[512,1024]{1,0:T(8,128)}, bf16[1024,1024]{1,0:T(8,128)(2,1)}, bf16[1024,1024...) custom-call(s32[32]{0:T(128)} %refs_0_.5, bf16[512,1024]{1,0:T(8,128)(2,1)} %get-tuple-element.73.refs_1_, ...), custom_call_target="tpu_custom_call" | custom-call | flops 30000001024 | bytes 30000000 | tf_op jit(solution)/shard_map/feed/pallas_call | solution.py:1319
  173.8 140.7 %attend_back.1 = (f32[2048,256]{1,0:T(8,128)}, bf16[1024,256]{1,0:T(8,128)(2,1)}, bf16[1024,256]{1,0:T(8,128)(2,1)}, bf16[1024,256]{1,0:T(8,128)(2,1)}, bf16[256...) custom-call(s32[32]{0:T(128)} %refs_0_.5, ...), custom_call_target="tpu_custom_call" | custom-call | flops 20000000000 | bytes 30000000 | tf_op jit(solution)/shard_map/attend_back/pallas_call | solution.py:1373
  314.6 10.4 %complete.1 = (f32[1024,1024]{1,0:T(8,128)}, f32[1024,1024]{1,0:T(8,128)}, f32[1024,256]{1,0:T(8,128)}, f32[1024,256]{1,0:T(8,128)}, f32[1024,256]{1,0:T(8,128)}...) custom-call(bf16[1024,1024]{1,0:T(8,128)(2,1)} %get-tuple-element.92, ...), custom_call_target="tpu_custom_call" | custom-call | flops 10000000 | bytes 24000000 | tf_op jit(solution)/shard_map/complete/pallas_call | solution.py:1448

commit v7 on v6

--- a/solution.py
+++ b/solution.py
@@ -227,7 +227,7 @@
                 self.xsend[s, j, at, :] = total.astype(BF)
                 return carry
 
-            lax.fori_loop(0, rows // RB, add, 0)
+            lax.fori_loop(0, rows // RB, add, 0, unroll=4)
             self._cross(s, j).start()
 
     def arrive(self, s):
@@ -319,7 +319,7 @@
             self.data[at, cols] = (self.data[at, cols].astype(F32) + arrived).astype(BF)
             return carry
 
-        lax.fori_loop(0, self.tall // RB, part, 0)
+        lax.fori_loop(0, self.tall // RB, part, 0, unroll=True)
 
     def _out(self, number, count):
         row, column = self.block(number)
@@ -521,7 +521,7 @@
             mid[here, :] = middle.astype(BF)
             return carry
 
-        lax.fori_loop(0, rows // RB, block, 0)
+        lax.fori_loop(0, rows // RB, block, 0, unroll=4)
         for copy in row_outs(s):
             copy.start()
 
@@ -669,7 +669,7 @@
             dsend[here, :] = d_ffn.astype(BF)
             return carry
 
-        lax.fori_loop(0, rows // RB, block, 0)
+        lax.fori_loop(0, rows // RB, block, 0, unroll=4)
         gd.start(s)
 
     def forward(s, carry):
@@ -694,7 +694,7 @@
                 slope[row, cols] = (gate * steep).astype(BF)
                 return carry
 
-            lax.fori_loop(0, SLOT // 32, block, 0)
+            lax.fori_loop(0, SLOT // 32, block, 0, unroll=8)
             return carry
 
         lax.fori_loop(0, units // NB, part, 0)
@@ -751,7 +751,7 @@
             dlow[here, :] = d_attn.astype(BF)
             return carry
 
-        lax.fori_loop(0, rows // RB, block, 0)
+        lax.fori_loop(0, rows // RB, block, 0, unroll=4)
         for copy in row_outs(s):
             copy.start()
 
@@ -775,7 +775,7 @@
                 return (unit_part, bias_part)
 
             zero = jnp.zeros((8, NB), F32)
-            unit_part, bias_part = lax.fori_loop(0, SLOT // 32, block, (zero, zero))
+            unit_part, bias_part = lax.fori_loop(0, SLOT // 32, block, (zero, zero), unroll=8)
             unit_sums[0, :, cols] += unit_part
             unit_sums[1, :, cols] += bias_part
             return carry
@@ -977,7 +977,7 @@
             tgrad[pl.ds(pl.multiple_of(s * SLOT + i * 32, 32), 32), :] = re.total(s, at)
             return carry
 
-        lax.fori_loop(0, SLOT // 32, block, 0)
+        lax.fori_loop(0, SLOT // 32, block, 0, unroll=4)
         out(s).start()
 
     def token_block(s, h):

time: 325 us -> 320 us (0.985)
  Pallas kernels: 324 us -> 319 us
    pallas_call x1, Pallas kernels: 73.9 us -> 70.5 us  [attend(): call(functools.partial(attend_kernel, n, seqs, heads), 'attend', 0, [smem...]
where the time goes in v7:
time: 320 us
  Pallas kernels  319 us (100%)
    pallas_call x1, Pallas kernels, attend_back(): call(functools.partial(attend_back_kernel, n, seqs, heads, size), 'attend...  140 us
    pallas_call x1, Pallas kernels, feed(): call(functools.partial(feed_kernel, n, seqs, units), 'feed', 1, [smem(),...  98 us
    pallas_call x1, Pallas kernels, attend(): call(functools.partial(attend_kernel, n, seqs, heads), 'attend', 0, [smem...  70.5 us
    pallas_call x1, Pallas kernels, complete(): pl.pallas_call(functools.partial(complete_kernel, n, heads, units), name=...  10.4 us

profile of v7, /device:TPU:0, one launch (start us, length us, event | category | flops | bytes accessed | tf_op | source)
XLA Modules:
  0.0 319.8 jit_solution(10760770906654500422)
XLA Ops:
  0.7 70.5 %attend.1 = (bf16[2048,1024]{1,0:T(8,128)(2,1)}, bf16[2048,768]{1,0:T(8,128)(2,1)}, bf16[4,4,512,512]{3,2,1,0:T(8,128)(2,1)}, f32[2048,256]{1,0:T(8,128)}, bf16[...) custom-call(s32[32]{0:T(128)} %refs_0_.5, ...), custom_call_target="tpu_custom_call" | custom-call | flops 10000000000 | bytes 30000000 | tf_op jit(solution)/shard_map/attend/pallas_call | solution.py:1259
  71.1 98.0 %feed.1 = (bf16[512,1024]{1,0:T(8,128)(2,1)}, bf16[512,1024]{1,0:T(8,128)(2,1)}, f32[512,1024]{1,0:T(8,128)}, bf16[1024,1024]{1,0:T(8,128)(2,1)}, bf16[1024,1024...) custom-call(s32[32]{0:T(128)} %refs_0_.5, bf16[512,1024]{1,0:T(8,128)(2,1)} %get-tuple-element.73.refs_1_, ...), custom_call_target="tpu_custom_call" | custom-call | flops 30000001024 | bytes 30000000 | tf_op jit(solution)/shard_map/feed/pallas_call | solution.py:1319
  169.1 140.1 %attend_back.1 = (f32[2048,256]{1,0:T(8,128)}, bf16[1024,256]{1,0:T(8,128)(2,1)}, bf16[1024,256]{1,0:T(8,128)(2,1)}, bf16[1024,256]{1,0:T(8,128)(2,1)}, bf16[256...) custom-call(s32[32]{0:T(128)} %refs_0_.5, ...), custom_call_target="tpu_custom_call" | custom-call | flops 20000000000 | bytes 30000000 | tf_op jit(solution)/shard_map/attend_back/pallas_call | solution.py:1373
  309.3 10.4 %complete.1 = (f32[1024,1024]{1,0:T(8,128)}, f32[1024,1024]{1,0:T(8,128)}, f32[1024,256]{1,0:T(8,128)}, f32[1024,256]{1,0:T(8,128)}, f32[1024,256]{1,0:T(8,128)}...) custom-call(bf16[1024,1024]{1,0:T(8,128)(2,1)} %get-tuple-element.92, ...), custom_call_target="tpu_custom_call" | custom-call | flops 10000000 | bytes 24000000 | tf_op jit(solution)/shard_map/complete/pallas_call | solution.py:1448

commit v8 on v7

--- a/solution.py
+++ b/solution.py
@@ -537,15 +537,6 @@
         def _():
             ga.relay(s + 1)
 
-        @pl.when(s > 0)
-        def _():
-            re.cross(s - 1)
-
-        @pl.when(s == seqs - 2)
-        def _():
-            for i in range(n - 1):
-                change_to(i).start()
-
         length = len_ref[lax.axis_index("dp") * seqs + s]
         bias = jnp.where(lax.broadcasted_iota(jnp.int32, (1, SLOT), 1) < length, 0.0, MASKED)
         for h in range(heads):
@@ -571,6 +562,12 @@
         re.start(s)
         mine = pl.ds(pl.multiple_of(s * SLOT + g.c * half, half), half)
         own[s] = nn(gat[mine, :], wo[...]).reshape(n // 2, rows, D)
+        re.cross(s)
+
+        @pl.when(s == seqs - 3)
+        def _():
+            for i in range(n - 1):
+                change_to(i).start()
 
         @pl.when(s > 0)
         def _():
@@ -579,7 +576,6 @@
         return carry
 
     lax.fori_loop(0, seqs, sequence, 0)
-    re.cross(seqs - 1)
     change_own.wait()
     for i in range(n - 1):
         change_from(i).wait()

time: 320 us -> 316 us (0.988)
  Pallas kernels: 319 us -> 314 us
    pallas_call x1, Pallas kernels: 70.5 us -> 65 us  [attend(): call(functools.partial(attend_kernel, n, seqs, heads), 'attend', 0, [smem...]
where the time goes in v8:
time: 316 us; the launch traced here: 315 us
  Pallas kernels  314 us (99%)
    pallas_call x1, Pallas kernels, attend_back(): call(functools.partial(attend_back_kernel, n, seqs, heads, size), 'attend...  141 us
    pallas_call x1, Pallas kernels, feed(): call(functools.partial(feed_kernel, n, seqs, units), 'feed', 1, [smem(),...  98.2 us
    pallas_call x1, Pallas kernels, attend(): call(functools.partial(attend_kernel, n, seqs, heads), 'attend', 0, [smem...  65 us
    pallas_call x1, Pallas kernels, complete(): pl.pallas_call(functools.partial(complete_kernel, n, heads, units), name=...  10.4 us

profile of v8, /device:TPU:0, one launch (start us, length us, event | category | flops | bytes accessed | tf_op | source)
XLA Modules:
  0.0 315.2 jit_solution(3354769253574048001)
XLA Ops:
  0.7 65.0 %attend.1 = (bf16[2048,1024]{1,0:T(8,128)(2,1)}, bf16[2048,768]{1,0:T(8,128)(2,1)}, bf16[4,4,512,512]{3,2,1,0:T(8,128)(2,1)}, f32[2048,256]{1,0:T(8,128)}, bf16[...) custom-call(s32[32]{0:T(128)} %refs_0_.5, ...), custom_call_target="tpu_custom_call" | custom-call | flops 10000000000 | bytes 30000000 | tf_op jit(solution)/shard_map/attend/pallas_call | solution.py:1255
  65.6 98.2 %feed.1 = (bf16[512,1024]{1,0:T(8,128)(2,1)}, bf16[512,1024]{1,0:T(8,128)(2,1)}, f32[512,1024]{1,0:T(8,128)}, bf16[1024,1024]{1,0:T(8,128)(2,1)}, bf16[1024,1024...) custom-call(s32[32]{0:T(128)} %refs_0_.5, bf16[512,1024]{1,0:T(8,128)(2,1)} %get-tuple-element.73.refs_1_, ...), custom_call_target="tpu_custom_call" | custom-call | flops 30000001024 | bytes 30000000 | tf_op jit(solution)/shard_map/feed/pallas_call | solution.py:1315
  163.8 140.8 %attend_back.1 = (f32[2048,256]{1,0:T(8,128)}, bf16[1024,256]{1,0:T(8,128)(2,1)}, bf16[1024,256]{1,0:T(8,128)(2,1)}, bf16[1024,256]{1,0:T(8,128)(2,1)}, bf16[256...) custom-call(s32[32]{0:T(128)} %refs_0_.5, ...), custom_call_target="tpu_custom_call" | custom-call | flops 20000000000 | bytes 30000000 | tf_op jit(solution)/shard_map/attend_back/pallas_call | solution.py:1369
  304.7 10.4 %complete.1 = (f32[1024,1024]{1,0:T(8,128)}, f32[1024,1024]{1,0:T(8,128)}, f32[1024,256]{1,0:T(8,128)}, f32[1024,256]{1,0:T(8,128)}, f32[1024,256]{1,0:T(8,128)}...) custom-call(bf16[1024,1024]{1,0:T(8,128)(2,1)} %get-tuple-element.92, ...), custom_call_target="tpu_custom_call" | custom-call | flops 10000000 | bytes 24000000 | tf_op jit(solution)/shard_map/complete/pallas_call | solution.py:1444
